TPU v7x, 32 devices: a whole 2x2x4 slice. The times are simulated.
32 devices in a mesh: tiles: 16 (over z, y, x), chan: 2 (over core).
Axes of the slice: x: 2, y: 2, z: 4, core: 2. Of those that a mesh axis runs over, the one named last changes fastest.
Arguments:
- features: bfloat16 [64, 2048, 256], P('chan', 'tiles'), may hold values from -6 to 6
- tile_valid: int32 [256, 32], P('tiles'), may hold values 0 or 1
- parent_owner: int32 [2048], P('tiles'), may hold values from 0 to 15, as said below
- w_first: bfloat16 [9, 64, 64], P(None, 'chan'), may hold values from -0.25 to 0.25
- w_second: bfloat16 [9, 64, 64], P(None, 'chan'), may hold values from -0.25 to 0.25
- w_merge: bfloat16 [4, 64, 64], P(None, None, 'chan'), may hold values from -0.375 to 0.375
Outputs:
- enhanced: bfloat16 [64, 2048, 256], P('chan', 'tiles')
- parents: bfloat16 [64, 3072, 64], P('chan', 'tiles')
Inputs may be any that keep to these rules, and one draw needn't show every extreme that they name: `parent_owner`: within the 128 parents whose children lie on one index of tiles, no owner appears more than 16 times, and some owner appears exactly 16 times for some index. Half of the owners own 3 * 64 parents in all, the other half 128 / 2.
All inputs are finite; a program needn't handle non-finite values. No bound on the sum of `tile_valid` on one device may be relied on, other than what follows from the above.
Results may differ from a plain program's by a relative error of at most 0.0052.
Values may be sent and summed in bfloat16 or wider, within the bound.
No kernel may reach another device: no remote copies, remote signals or barrier semaphores. Data moves between devices by JAX's collectives and lax.ppermute only.
A program may use at most 128 MiB of HBM per device.

v0:
```python
import jax
import jax.numpy as jnp
from jax import lax
from jax.sharding import PartitionSpec as P


def extended(cells, sides, width):
    for axis, dim in sides:
        count = lax.axis_size(axis)
        ends = count - 1
        head = lax.slice_in_dim(cells, 0, width, axis=dim)
        tail = lax.slice_in_dim(cells, cells.shape[dim] - width, cells.shape[dim], axis=dim)
        cells = jnp.concatenate(
            [
                lax.ppermute(tail, axis, [(i, (i + 1) % count) for i in range(ends)]),
                cells,
                lax.ppermute(head, axis, [((i + 1) % count, i) for i in range(ends)]),
            ],
            axis=dim,
        )
    return cells


def tap_sum(running, shard_piece, weights, dilation, rows_out):
    col_count = shard_piece.shape[2]
    padded = jnp.pad(shard_piece, ((0, 0), (0, 0), (dilation, dilation)))
    for row_tap in range(3):
        for col_tap in range(3):
            window = padded[
                :,
                row_tap * dilation : row_tap * dilation + rows_out,
                col_tap * dilation : col_tap * dilation + col_count,
            ]
            running = running + jnp.einsum(
                "oi,irc->orc",
                weights[3 * row_tap + col_tap],
                window,
                preferred_element_type=jnp.float32,
            )
    return running


def merge_taps(source, weights):
    in_count, rows, cols = source.shape
    taps_view = source.reshape(in_count, rows // 2, 2, cols // 2, 2)
    running = jnp.zeros((weights.shape[1], rows // 2, cols // 2), jnp.float32)
    for row_tap in range(2):
        for col_tap in range(2):
            running = running + jnp.einsum(
                "oi,irc->orc",
                weights[2 * row_tap + col_tap],
                taps_view[:, :, row_tap, :, col_tap],
                preferred_element_type=jnp.float32,
            )
    return running


def to_tiles(merged, tile_side):
    count, rows, cols = merged.shape
    grid = merged.reshape(count, rows // tile_side, tile_side, cols // tile_side, tile_side)
    return grid.transpose(0, 1, 3, 2, 4).reshape(
        count, rows // tile_side * (cols // tile_side), tile_side * tile_side
    )


def routing(parent_owner, devices, capacity):
    parents_dev = parent_owner.shape[0]
    matches = (parent_owner[:, None] == jnp.arange(devices, dtype=jnp.int32)[None, :]).astype(
        jnp.int32
    )
    earlier = jnp.cumsum(matches, axis=0) - matches
    within = jnp.sum(earlier * matches, axis=1)
    slot_index = parent_owner * capacity + within
    chosen = (
        slot_index[None, :] == jnp.arange(devices * capacity, dtype=jnp.int32)[:, None]
    ).astype(jnp.int32)
    filled = jnp.sum(chosen, axis=1)
    source_row = jnp.sum(chosen * jnp.arange(parents_dev, dtype=jnp.int32)[None, :], axis=1)
    return (source_row, filled)


def pack(payload, source_row, filled):
    picked = jnp.take(payload, source_row, axis=1)
    packed = jnp.where(filled[None, :, None] > 0, picked, jnp.zeros_like(picked))
    slot_flags = filled.astype(jnp.bfloat16)[None, :]
    return (packed, slot_flags)


def compact(received, got_flags, own_cap):
    live_slots = got_flags[0].astype(jnp.int32)
    position = jnp.cumsum(live_slots) - live_slots
    chosen = (
        (position[None, :] == jnp.arange(own_cap, dtype=jnp.int32)[:, None])
        & (live_slots[None, :] > 0)
    ).astype(jnp.int32)
    source_slot = jnp.sum(
        chosen * jnp.arange(live_slots.shape[0], dtype=jnp.int32)[None, :], axis=1
    )
    present = jnp.sum(chosen, axis=1)
    picked = jnp.take(received, source_slot, axis=1)
    return jnp.where(present[None, :, None] > 0, picked, jnp.zeros_like(picked))


def deliver(parent_tiles, source_row, filled, own_cap):
    packed, slot_flags = pack(parent_tiles, source_row, filled)
    received, got_flags = (
        lax.all_to_all(packed, "tiles", split_axis=1, concat_axis=1, tiled=True),
        lax.all_to_all(slot_flags, "tiles", split_axis=1, concat_axis=1, tiled=True),
    )
    return compact(received, got_flags, own_cap)


def on_device(features, tile_valid, parent_owner, w_first, w_second, w_merge):
    channels, row_count, col_count = features.shape
    tile_rows, tile_cols = tile_valid.shape
    tile_side = row_count // tile_rows
    parents_dev = parent_owner.shape[0]
    devices = lax.axis_size("tiles")
    capacity = 2 * max(1, parents_dev // devices)
    own_cap = 3 * parents_dev // 2
    cell_mask = jnp.broadcast_to(
        tile_valid.astype(jnp.bfloat16)[:, None, :, None],
        (tile_rows, tile_side, tile_cols, tile_side),
    ).reshape(1, row_count, col_count)
    source_row, filled = routing(parent_owner, devices, capacity)
    half_rows = row_count // 2
    swapped = lax.all_to_all(features, "chan", split_axis=1, concat_axis=0, tiled=True)
    full_first, full_second, full_merge = (
        lax.all_gather(w_first, "chan", axis=1, tiled=True),
        lax.all_gather(w_second, "chan", axis=1, tiled=True),
        lax.all_gather(w_merge, "chan", axis=2, tiled=True),
    )
    half_mask = lax.dynamic_slice_in_dim(
        cell_mask, lax.axis_index("chan") * half_rows, half_rows, 1
    )
    stacked = jnp.concatenate([swapped, half_mask], axis=0)
    widened = extended(stacked, ((("tiles", "chan"), 1),), 3)
    all_channels = swapped.shape[0]
    start_first = jnp.zeros((all_channels, half_rows + 4, col_count), jnp.float32)
    first_out = tap_sum(start_first, widened[:all_channels], full_first, 1, half_rows + 4)
    hidden = jnp.maximum(first_out * widened[all_channels:, 1:-1].astype(jnp.float32), 0.0).astype(
        jnp.bfloat16
    )
    start_second = jnp.zeros((all_channels, half_rows, col_count), jnp.float32)
    second_out = tap_sum(start_second, hidden, full_second, 2, half_rows)
    half_enhanced = (
        half_mask.astype(jnp.float32) * (swapped.astype(jnp.float32) + second_out)
    ).astype(jnp.bfloat16)
    half_parents = to_tiles(merge_taps(half_enhanced, full_merge).astype(jnp.bfloat16), tile_side)
    enhanced, parent_tiles = (
        lax.all_to_all(half_enhanced, "chan", split_axis=0, concat_axis=1, tiled=True),
        lax.all_to_all(half_parents, "chan", split_axis=0, concat_axis=1, tiled=True),
    )
    parents = deliver(parent_tiles, source_row, filled, own_cap)
    return (enhanced, parents)


def solution(mesh):
    return jax.shard_map(
        on_device,
        mesh=mesh,
        in_specs=(
            P("chan", "tiles", None),
            P("tiles", None),
            P("tiles"),
            P(None, "chan", None),
            P(None, "chan", None),
            P(None, None, "chan"),
        ),
        out_specs=(P("chan", "tiles", None), P("chan", "tiles", None)),
        check_vma=False,
    )
```

profile of v0, /device:TPU:8, one launch (start us, length us, event | category | flops | bytes accessed | tf_op | source)
XLA Modules:
  0.0 209.7 jit_solution(3948986278628641102)
XLA Ops:
  0.6 4.1 %copy.88 = bf16[32,128,256]{2,0,1:T(8,128)(2,1)} copy(bf16[32,128,256]{2,1,0:T(8,128)(2,1)} %param.6) | data formatting | bytes 4194304 | tf_op args[0]
  4.7 3.9 %all-to-all-start = ((bf16[32,128,256]{2,0,1:T(8,128)(2,1)}), bf16[32,128,256]{2,0,1:T(8,128)(2,1)S(1)}, u32[]{:S(2)}, u32[]{:S(2)}) async-start(bf16[32,128,256]{2,0,1:T(8,128)(2,1)} %copy.88), calls=%async_computation | async-start | bytes 4194304 | tf_op jit(solution)/shard_map/all_to_all | solution.py:127
  14.8 4.0 %collective-permute-start.1 = (bf16[65,3,256]{2,0,1:T(8,128)(2,1)S(1)}, bf16[65,3,256]{2,0,1:T(8,128)(2,1)S(1)}, u32[]{:S(2)}, u32[]{:S(2)}) collective-permute-start(bf16[65,3,256]{2,0,1:T(8,128)(2,1)S(1)} %get-tuple-element.23), channel_id=1, source_target_pairs={{1,0},{2,1},{3,2},{4,3},{5,4},{6,5},{7,6},{8,7},{9,8},{10,9},{11,1... | collective-permute-start | bytes 299528 | tf_op jit(solution)/shard_map/ppermute | solution.py:17
  29.4 2.8 %fusion.8 = f32[68,256,64]{1,2,0:T(8,128)} fusion(bf16[65,70,256]{2,0,1:T(8,128)(2,1)S(1)} %pad_maximum_fusion, bf16[9,64,64]{2,1,0:T(8,128)(2,1)S(1)} %all_gather.9), kind=kOutput, calls=%fused_computation.25 | convolution fusion | flops 142606336 | bytes 6701056 | tf_op jit(solution)/shard_map/oi,irc->orc/dot_general | solution.py:34
  32.2 2.9 %fusion.6 = f32[68,256,64]{1,2,0:T(8,128)} fusion(bf16[64,70,256]{2,0,1:T(8,128)(2,1)S(1)} %slice.216, bf16[9,64,64]{2,1,0:T(8,128)(2,1)S(1)} %all_gather.9), kind=kOutput, calls=%fused_computation.23 | convolution fusion | flops 142606336 | bytes 6766592 | tf_op jit(solution)/shard_map/oi,irc->orc/dot_general | solution.py:34
  35.1 2.9 %fusion.5 = f32[68,256,64]{1,2,0:T(8,128)} fusion(bf16[64,70,256]{2,0,1:T(8,128)(2,1)S(1)} %slice.216, bf16[9,64,64]{2,1,0:T(8,128)(2,1)S(1)} %all_gather.9), kind=kOutput, calls=%fused_computation.22 | convolution fusion | flops 142606336 | bytes 6766592 | tf_op jit(solution)/shard_map/oi,irc->orc/dot_general | solution.py:34
  40.7 2.9 %fusion.4 = f32[68,256,64]{1,2,0:T(8,128)} fusion(bf16[64,70,256]{2,0,1:T(8,128)(2,1)S(1)} %slice.216, bf16[9,64,64]{2,1,0:T(8,128)(2,1)S(1)} %all_gather.9), kind=kOutput, calls=%fused_computation.21 | convolution fusion | flops 142606336 | bytes 6766592 | tf_op jit(solution)/shard_map/oi,irc->orc/dot_general | solution.py:34
  43.6 2.9 %fusion.3 = f32[68,256,64]{1,2,0:T(8,128)} fusion(bf16[64,70,256]{2,0,1:T(8,128)(2,1)S(1)} %slice.216, bf16[9,64,64]{2,1,0:T(8,128)(2,1)S(1)} %all_gather.9), kind=kOutput, calls=%fused_computation.20 | convolution fusion | flops 142606336 | bytes 6766592 | tf_op jit(solution)/shard_map/oi,irc->orc/dot_general | solution.py:34
  46.5 3.0 %fusion.2 = f32[68,256,64]{1,2,0:T(8,128)} fusion(bf16[64,70,256]{2,0,1:T(8,128)(2,1)S(1)} %slice.216, bf16[9,64,64]{2,1,0:T(8,128)(2,1)S(1)} %all_gather.9), kind=kOutput, calls=%fused_computation.19 | convolution fusion | flops 142606336 | bytes 6766592 | tf_op jit(solution)/shard_map/oi,irc->orc/dot_general | solution.py:34
  49.5 2.8 %fusion.12 = f32[68,256,64]{1,2,0:T(8,128)} fusion(bf16[65,70,256]{2,0,1:T(8,128)(2,1)S(1)} %pad_maximum_fusion, bf16[9,64,64]{2,1,0:T(8,128)(2,1)S(1)} %all_gather.9), kind=kOutput, calls=%fused_computation.29 | convolution fusion | flops 142606336 | bytes 6701056 | tf_op jit(solution)/shard_map/oi,irc->orc/dot_general | solution.py:34
  52.4 12.8 %fusion.25 = bf16[64,68,256]{2,0,1:T(8,128)(2,1)S(1)} fusion(f32[68,256]{1,0:T(8,128)S(1)} %bitcast.164, bf16[64,70,256]{2,0,1:T(8,128)(2,1)S(1)} %slice.216, f32[68,256,64]{1,2,0:T(8,128)} %fusion.8, f32[68,256,64]{1,2,0:T(8,128)} %fusion.6, f32[68,256,64]{1,2,0:T(8,128)} %fusion.5, f32[68,256,64]{1,2,0:T(8,128)} %fusion.10, f32[68,256,64]{1,2,0:T(8,128)} %fusion.4, ...), kind=kOutput, calls=%fused_computation.43 | convolution fusion | flops 154861568 | bytes 40263680 | tf_op jit(solution)/shard_map/oi,irc->orc/dot_general | solution.py:34
  81.4 2.8 %fusion.14 = f32[64,256,64]{1,2,0:T(8,128)} fusion(bf16[64,68,256]{2,0,1:T(8,128)(2,1)S(1)} %fusion.25, bf16[9,64,64]{2,1,0:T(8,128)(2,1)S(1)} %all_gather.10), kind=kOutput, calls=%fused_computation.31 | convolution fusion | flops 134217728 | bytes 6438912 | tf_op jit(solution)/shard_map/oi,irc->orc/dot_general | solution.py:34
  86.8 13.3 %fusion.1 = bf16[64,64,256]{2,0,1:T(8,128)(2,1)} fusion(f32[64,256,64]{1,2,0:T(8,128)} %fusion.19, f32[64,256,64]{1,2,0:T(8,128)} %fusion.18, f32[64,256,64]{1,2,0:T(8,128)} %fusion.17, f32[64,256,64]{1,2,0:T(8,128)} %fusion.21, f32[64,256,64]{1,2,0:T(8,128)} %fusion.16, f32[64,256,64]{1,2,0:T(8,128)} %fusion.15, f32[64,256,64]{1,2,0:T(8,128)} %fusion.14, ...), kind=kOutput, calls=%fused_computation.11 | convolution fusion | flops 146800640 | bytes 40058880 | tf_op jit(solution)/shard_map/oi,irc->orc/dot_general | solution.py:34
  100.1 4.8 %copy.93 = bf16[64,64,256]{0,2,1:T(8,128)(2,1)} copy(bf16[64,64,256]{2,0,1:T(8,128)(2,1)} %fusion.1) | data formatting | bytes 4194304 | tf_op jit(solution)/shard_map/convert_element_type | solution.py:148
  104.9 12.2 %fusion.52 = (bf16[64,32,1,128,1]{0,4,3,2,1:T(2,128)(2,1)S(1)}, bf16[64,32,1,128,1]{0,4,3,2,1:T(2,128)(2,1)}, bf16[64,32,1,128,1]{0,4,3,2,1:T(2,128)(2,1)}, bf16[64,32,1,128,1]{0,4,3,2,1:T(2,128)(2,1)}) fusion(bf16[64,32,2,128,2]{0,4,3,2,1:T(2,128)(2,1)} %bitcast.155), kind=kLoop, calls=%fused_computation.121 | loop fusion | bytes 4194304 | tf_op jit(solution)/shard_map/slice | solution.py:52
  117.1 5.2 %copy.114 = bf16[64,32,1,128,1]{3,0,1,4,2:T(8,128)(2,1)} copy(bf16[64,32,1,128,1]{0,4,3,2,1:T(2,128)(2,1)} %get-tuple-element.21) | data formatting | bytes 1048576
  122.3 4.6 %copy.116 = bf16[64,32,1,128,1]{3,0,1,4,2:T(8,128)(2,1)S(1)} copy(bf16[64,32,1,128,1]{0,4,3,2,1:T(2,128)(2,1)} %get-tuple-element.20) | data formatting | bytes 1048576
  126.9 4.6 %copy.118 = bf16[64,32,1,128,1]{3,0,1,4,2:T(8,128)(2,1)S(1)} copy(bf16[64,32,1,128,1]{0,4,3,2,1:T(2,128)(2,1)} %get-tuple-element.19) | data formatting | bytes 1048576
  131.6 3.6 %copy.120 = bf16[64,32,1,128,1]{3,0,1,4,2:T(8,128)(2,1)} copy(bf16[64,32,1,128,1]{0,4,3,2,1:T(2,128)(2,1)S(1)} %get-tuple-element.18) | data formatting | bytes 1048576
  141.4 4.2 %all_to_all.65 = bf16[2,2,65536]{2,1,0:T(2,128)(2,1)S(1)} all-to-all(bf16[2,2,65536]{2,1,0:T(2,128)(2,1)S(1)} %reshape.172), channel_id=1, replica_groups=mesh['tiles'=16,'chan'=2] {'chan'}, dimensions={0} | all-to-all | bytes 1048576 | tf_op jit(solution)/shard_map/all_to_all | solution.py:152
  145.5 7.5 %all-to-all-start.2 = ((bf16[1,16,16]{2,0,1:T(2,128)(2,1)}), bf16[1,16,16]{2,0,1:T(2,128)(2,1)S(1)}, u32[]{:S(2)}, u32[]{:S(2)}) async-start(bf16[1,16,16]{2,0,1:T(2,128)(2,1)} %convert_element_type.84), calls=%async_computation.2 | async-start | bytes 16384 | tf_op jit(solution)/shard_map/all_to_all | solution.py:108
  162.8 6.6 %all_to_all.66 = bf16[64,64,256]{2,1,0:T(8,128)(2,1)S(1)} all-to-all(bf16[64,64,256]{2,1,0:T(8,128)(2,1)} %copy.90), channel_id=1, replica_groups=mesh['tiles'=16,'chan'=2] {'chan'}, dimensions={0} | all-to-all | bytes 4194304 | tf_op jit(solution)/shard_map/all_to_all | solution.py:151
  169.4 6.9 %all-to-all-start.4 = ((bf16[16,2,16384]{2,1,0:T(2,128)(2,1)}), bf16[16,2,16384]{2,1,0:T(2,128)(2,1)S(1)}, u32[]{:S(2)}, u32[]{:S(2)}) async-start(bf16[16,2,16384]{2,1,0:T(2,128)(2,1)} %reshape.174), calls=%async_computation.4 | async-start | bytes 2097152 | tf_op jit(solution)/shard_map/all_to_all | solution.py:107
  178.8 23.3 %all-to-all-done.4 = bf16[16,2,16384]{2,1,0:T(2,128)(2,1)S(1)} async-done(((bf16[16,2,16384]{2,1,0:T(2,128)(2,1)}), bf16[16,2,16384]{2,1,0:T(2,128)(2,1)S(1)}, u32[]{:S(2)}, u32[]{:S(2)}) %all-to-all-start.4) | async-done | bytes 1048608 | tf_op jit(solution)/shard_map/all_to_all | solution.py:107
  (94 shorter events, 64.2 us)
Async XLA Ops:
  4.7 3.9 %copy-start.7 = (s32[16,32]{1,0:T(8,128)S(1)}, s32[16,32]{1,0:T(8,128)}, u32[]{:S(2)}) copy-start(s32[16,32]{1,0:T(8,128)} %param.7) | copy-start | bytes 6148
  4.7 6.8 %all-to-all-start = ((bf16[32,128,256]{2,0,1:T(8,128)(2,1)}), bf16[32,128,256]{2,0,1:T(8,128)(2,1)S(1)}, u32[]{:S(2)}, u32[]{:S(2)}) async-start(bf16[32,128,256]{2,0,1:T(8,128)(2,1)} %copy.88), calls=%async_computation | async-start | bytes 4194304 | tf_op jit(solution)/shard_map/all_to_all | solution.py:127
  11.5 1.3 copy-start.2
  14.6 6.1 %copy-start.4 = (bf16[9,32,64]{2,1,0:T(8,128)(2,1)S(1)}, bf16[9,32,64]{2,1,0:T(8,128)(2,1)}, u32[]{:S(2)}) copy-start(bf16[9,32,64]{2,1,0:T(8,128)(2,1)} %param.9) | copy-start | bytes 110596
  14.6 8.0 %copy-start.5 = (bf16[9,32,64]{2,1,0:T(8,128)(2,1)S(1)}, bf16[9,32,64]{2,1,0:T(8,128)(2,1)}, u32[]{:S(2)}) copy-start(bf16[9,32,64]{2,1,0:T(8,128)(2,1)} %param.10) | copy-start | bytes 110596
  14.6 9.9 %copy-start.6 = (bf16[4,64,32]{1,2,0:T(8,128)(2,1)S(1)}, bf16[4,64,32]{1,2,0:T(8,128)(2,1)}, u32[]{:S(2)}) copy-start(bf16[4,64,32]{1,2,0:T(8,128)(2,1)} %param.11) | copy-start | bytes 49156
  14.7 12.5 %copy-start.8 = (s32[128]{0:T(128)S(1)}, s32[128]{0:T(128)}, u32[]{:S(2)}) copy-start(s32[128]{0:T(128)} %param.8) | copy-start | bytes 1540
  14.8 13.7 %collective-permute-start.1 = (bf16[65,3,256]{2,0,1:T(8,128)(2,1)S(1)}, bf16[65,3,256]{2,0,1:T(8,128)(2,1)S(1)}, u32[]{:S(2)}, u32[]{:S(2)}) collective-permute-start(bf16[65,3,256]{2,0,1:T(8,128)(2,1)S(1)} %get-tuple-element.23), channel_id=1, source_target_pairs={{1,0},{2,1},{3,2},{4,3},{5,4},{6,5},{7,6},{8,7},{9,8},{10,9},{11,1... | collective-permute-start | bytes 299528 | tf_op jit(solution)/shard_map/ppermute | solution.py:17
  18.8 9.7 %collective-permute-start = (bf16[65,3,256]{2,0,1:T(8,128)(2,1)S(1)}, bf16[65,3,256]{2,0,1:T(8,128)(2,1)S(1)}, u32[]{:S(2)}, u32[]{:S(2)}) collective-permute-start(bf16[65,3,256]{2,0,1:T(8,128)(2,1)S(1)} %get-tuple-element.22), channel_id=1, source_target_pairs={{0,1},{1,2},{2,3},{3,4},{4,5},{5,6},{6,7},{7,8},{8,9},{9,10},{10,1... | collective-permute-start | bytes 299528 | tf_op jit(solution)/shard_map/ppermute | solution.py:15
  136.5 1.0 copy-start.3
  145.5 17.3 %all-to-all-start.2 = ((bf16[1,16,16]{2,0,1:T(2,128)(2,1)}), bf16[1,16,16]{2,0,1:T(2,128)(2,1)S(1)}, u32[]{:S(2)}, u32[]{:S(2)}) async-start(bf16[1,16,16]{2,0,1:T(2,128)(2,1)} %convert_element_type.84), calls=%async_computation.2 | async-start | bytes 16384 | tf_op jit(solution)/shard_map/all_to_all | solution.py:108
  155.4 2.7 %copy-start = (bf16[64,64,256]{2,0,1:T(8,128)(2,1)S(1)}, bf16[64,64,256]{2,0,1:T(8,128)(2,1)}, u32[]{:S(2)}) copy-start(bf16[64,64,256]{2,0,1:T(8,128)(2,1)} %fusion.1) | copy-start | bytes 6291460
  158.1 2.5 %copy-start.1 = (bf16[256,32,64]{2,1,0:T(8,128)(2,1)S(1)}, bf16[256,32,64]{2,1,0:T(8,128)(2,1)}, u32[]{:S(2)}) copy-start(bf16[256,32,64]{2,1,0:T(8,128)(2,1)} %fusion.54) | copy-start | bytes 3145732
  169.4 32.7 %all-to-all-start.4 = ((bf16[16,2,16384]{2,1,0:T(2,128)(2,1)}), bf16[16,2,16384]{2,1,0:T(2,128)(2,1)S(1)}, u32[]{:S(2)}, u32[]{:S(2)}) async-start(bf16[16,2,16384]{2,1,0:T(2,128)(2,1)} %reshape.174), calls=%async_computation.4 | async-start | bytes 2097152 | tf_op jit(solution)/shard_map/all_to_all | solution.py:107
where the time goes:
time: 211 us; the launch traced here: 210 us
  matrix products  72.8 us (35%)
  local copies, waits for them, and re-layouts  63.5 us (30%)
  waiting for transfers between devices  24.8 us (12%)
  starting transfers between devices  24.2 us (11%)
  blocking collectives  16.6 us (8%)
  other arithmetic  6.83 us (3%)
    dot_general x18, matrix products, tap_sum(): jnp.einsum('oi,irc->orc', weights[3 * row_tap + col_tap], window, preferr...  70.6 us
    unnamed x35, local copies, waits for them, and re-layouts  31.6 us
    all_to_all x1, waiting for transfers between devices, deliver(): lax.all_to_all(packed, 'tiles', split_axis=1, concat_axis=1, tiled=True)  23.3 us
    slice x1, local copies, waits for them, and re-layouts, merge_taps(): taps_view[:, :, row_tap, :, col_tap]  12.2 us
    all_to_all x1, starting transfers between devices, deliver(): lax.all_to_all(slot_flags, 'tiles', split_axis=1, concat_axis=1, tiled=True)  7.46 us
    convert_element_type x2, local copies, waits for them, and re-layouts, on_device(): half_enhanced = (half_mask.astype(jnp.float32) * (swapped.astype(jnp.floa...  7.29 us
    all_to_all x1, starting transfers between devices, deliver(): lax.all_to_all(packed, 'tiles', split_axis=1, concat_axis=1, tiled=True)  6.92 us
    all_to_all x1, blocking collectives, on_device(): lax.all_to_all(half_enhanced, 'chan', split_axis=0, concat_axis=1, tiled=...  6.62 us
  transfers between devices with their start and end apart: 5, of which 2 were waited for; matrix products, arithmetic and copies ran while one was open for 7% of the time, Pallas kernels for 0%

commit v1 on v0

v1 whole, which is shorter than its diff:
```python
import functools

import jax
import jax.numpy as jnp
from jax import lax
from jax.experimental import pallas as pl
from jax.experimental.pallas import tpu as pltpu
from jax.sharding import PartitionSpec as P

BF = jnp.bfloat16
F32 = jnp.float32
HALO = 4
BLK = 16


def iota(shape, dim):
    return lax.broadcasted_iota(jnp.int32, shape, dim)


def ones_where(cond):
    return jnp.where(cond, 1.0, 0.0).astype(BF)


def mm(a, b):
    return jnp.dot(a, b, preferred_element_type=F32)


def mm_nt(a, b):
    return lax.dot_general(a, b, (((1,), (1,)), ((), ())), preferred_element_type=F32)


def swap_matrix(outer, inner):
    n = outer * inner
    row, col = iota((n, n), 0), iota((n, n), 1)
    return ones_where((row % inner == col // outer) & (row // inner == col % outer))


def shifted(x, amount):
    cols = x.shape[1]
    lane = iota(x.shape, 1)
    rolled = pltpu.roll(x, amount % cols, 1)
    inside = lane >= amount if amount > 0 else lane < cols + amount
    return jnp.where(inside, rolled, 0.0)


def conv_kernel(
    side,
    core_ref,
    feat_hbm,
    recv_ref,
    mid_own_ref,
    mid_oth_ref,
    out_own_ref,
    out_oth_ref,
    valid_ref,
    wown_ref,
    woth_ref,
    eown_ref,
    eoth_ref,
    mown_ref,
    moth_ref,
    feat,
    xs,
    hs,
    es,
    mask,
    w1,
    w2,
    wm,
    pa_ref,
    pb_ref,
    sem,
):
    core = core_ref[0]
    chans, rows, cols = recv_ref.shape
    allc = 2 * chans
    copy = pltpu.make_async_copy(
        feat_hbm.at[:, pl.ds(pl.multiple_of(core * rows, rows), rows), :], feat, sem
    )
    copy.start()

    for dst, base in ((w1, 0), (w2, 9)):
        total = None
        for b in range(3):
            tall = jnp.concatenate(
                [ref[base + 3 * a + b] for a in range(3) for ref in (wown_ref, woth_ref)], axis=0
            )
            src, pos = iota((allc, 3 * allc), 0), iota((allc, 3 * allc), 1)
            place = ones_where(pos == b * allc + (src + chans * core) % allc)
            part = mm(tall, place)
            total = part if total is None else total + part
        dst[...] = total.astype(BF)
    tall = jnp.concatenate(
        [ref[18 + 2 * a + b] for b in range(2) for a in range(2) for ref in (wown_ref, woth_ref)],
        axis=0,
    )
    order = ones_where(iota((allc, allc), 1) == (iota((allc, allc), 0) + chans * core) % allc)
    wm[...] = mm_nt(order, tall).astype(BF)

    tiles_r, tiles_c = valid_ref.shape
    widen = ones_where(iota((tiles_c, cols), 1) // side == iota((tiles_c, cols), 0))
    mask[pl.ds(side, tiles_r), :] = mm(valid_ref[...].astype(F32).astype(BF), widen)

    def put(dst, index, x, amount):
        dst[index, 0:allc, :] = shifted(x, amount).astype(BF)
        dst[index, allc : 2 * allc, :] = x.astype(BF)
        dst[index, 2 * allc : 3 * allc, :] = shifted(x, -amount).astype(BF)

    turn4 = swap_matrix(HALO, chans)
    first_row = 5
    for own_ref, oth_ref, outer in ((mid_own_ref, mid_oth_ref, False), (out_own_ref, out_oth_ref, True)):
        own, oth = mm(turn4, own_ref[...]), mm(turn4, oth_ref[...])
        low = core == 0 if outer else core == 1
        start = jnp.where(low, first_row - HALO, first_row + rows)
        for r in range(HALO):
            x = jnp.concatenate(
                [own[r * chans : (r + 1) * chans], oth[r * chans : (r + 1) * chans]], axis=0
            )
            put(xs, start + r, x, 1)
        if outer:
            top = own[0:1, :]
            bottom = own[(HALO - 1) * chans : (HALO - 1) * chans + 1, :]

            @pl.when(core == 0)
            def _():
                mask[pl.ds(side - 1, 1), :] = top

            @pl.when(core == 1)
            def _():
                mask[pl.ds(side + tiles_r, 1), :] = bottom

    xs[0] = jnp.zeros(xs.shape[1:], BF)
    turn = swap_matrix(BLK, BLK)
    copy.wait()

    def lay(step, carry):
        at = pl.multiple_of(step * BLK, BLK)
        parts = []
        for ref in (feat, recv_ref):
            for ch in range(0, chans, BLK):
                block = ref[ch : ch + BLK, pl.ds(at, BLK), :].reshape(BLK * BLK, cols)
                parts.append(mm(turn, block))
        for r in range(BLK):
            x = jnp.concatenate([p[r * BLK : (r + 1) * BLK] for p in parts], axis=0)
            put(xs, first_row + at + r, x, 1)
        return carry

    lax.fori_loop(0, rows // BLK, lay, 0)

    base = side + core * (rows // side)
    steps = rows // side + 1
    for i in range(2):
        pa_ref[i] = jnp.zeros((allc, cols), F32)
        pb_ref[i] = jnp.zeros((allc, cols), F32)

    def first(step, carry):
        pa, pb = pa_ref[0], pb_ref[0]
        m0 = mask[pl.ds(base + step - 1, 1), :]
        m1 = mask[pl.ds(base + step, 1), :]
        for j in range(side):
            q = step * side + j
            y = mm(w1[...], xs[q])
            total = pa + y[2 * allc :]
            pa = pb + y[allc : 2 * allc]
            pb = y[:allc]
            h = jnp.maximum(total * (m0 if j < 6 else m1), 0.0)
            put(hs, q, h, 2)
        pa_ref[0] = pa
        pb_ref[0] = pb
        return carry

    lax.fori_loop(0, steps, first, 0)

    pa_ref[0] = jnp.zeros((allc, cols), F32)
    pb_ref[0] = jnp.zeros((allc, cols), F32)
    half = cols // 2
    pick = ones_where(iota((cols, cols), 0) == 2 * (iota((cols, cols), 1) % half) + iota((cols, cols), 1) // half)

    def second(step, carry):
        pa, pb = [pa_ref[0], pa_ref[1]], [pb_ref[0], pb_ref[1]]
        m0 = mask[pl.ds(base + step - 1, 1), :]
        rows_e = []
        for j in range(side):
            q = step * side + j
            i = j % 2
            z = mm(w2[...], hs[q])
            total = pa[i] + z[2 * allc :]
            pa[i] = pb[i] + z[allc : 2 * allc]
            pb[i] = z[:allc]
            x = xs[jnp.maximum(q - 3, 0), allc : 2 * allc, :].astype(F32)
            e = (m0 * (x + total)).astype(BF)
            es[q] = e
            rows_e.append(e)
        for i in range(2):
            pa_ref[i] = pa[i]
            pb_ref[i] = pb[i]

        @pl.when(step > 0)
        def _():
            tile = step - 1
            s = mm(jnp.concatenate(rows_e, axis=0), pick).astype(BF)
            pairs = []
            for k in range(side // 2):
                sp = s[k * 2 * allc : (k + 1) * 2 * allc]
                pairs.append(jnp.concatenate([sp[:, :half], sp[:, half:]], axis=0))
            for k in range(0, side // 2, 2):
                both = mm(wm[...], jnp.concatenate(pairs[k : k + 2], axis=1)).astype(BF)
                for n in range(2):
                    u = (side // 2) * (tile % 2) + k + n
                    at_u = pl.ds(pl.multiple_of(u * chans, chans), chans)
                    at_g = pl.ds(pl.multiple_of((tile // 2) * half, half), half)
                    piece = both[:, n * half : (n + 1) * half]
                    mown_ref[at_u, at_g] = piece[:chans]
                    moth_ref[at_u, at_g] = piece[chans:]

        return carry

    lax.fori_loop(0, steps, second, 0)

    def unlay(step, carry):
        at = pl.multiple_of(step * BLK, BLK)
        for n, ref in ((0, eown_ref), (1, eoth_ref)):
            for ch in range(0, chans, BLK):
                c0 = n * chans + ch
                block = es[pl.ds(side + at, BLK), c0 : c0 + BLK, :].reshape(BLK * BLK, cols)
                ref[ch : ch + BLK, pl.ds(at, BLK), :] = (
                    mm(turn, block).astype(BF).reshape(BLK, BLK, cols)
                )
        return carry

    lax.fori_loop(0, rows // BLK, unlay, 0)


def pack_kernel(side, slots, core_ref, owner_ref, mown_ref, mrecv_ref, out_ref, code_ref):
    core = core_ref[0]
    count = owner_ref.shape[0]
    rows, width = mown_ref.shape
    blocks, all_rows, lanes = out_ref.shape
    per = side * slots
    owner = jnp.broadcast_to(owner_ref[...], (count, lanes))
    is_owner = owner == iota((count, lanes), 1)
    lower = ones_where(iota((count, count), 0) > iota((count, count), 1))
    earlier = mm(lower, ones_where(is_owner))
    within = jnp.sum(jnp.where(is_owner, earlier, 0.0), axis=1, keepdims=True)
    code = (owner * per).astype(F32) + within
    wide = jnp.broadcast_to(code[:, None, :], (count, side, lanes))
    step_v = (iota((count, side, lanes), 1) * slots).astype(F32)
    code_ref[...] = (wide + step_v).reshape(count * side, lanes).astype(jnp.int32)
    mine = pl.multiple_of(core * width, width)
    other = pl.multiple_of((1 - core) * width, width)

    def block(step, carry):
        outs = []
        for ref, at in ((mown_ref, mine), (mrecv_ref, other)):
            code = code_ref[pl.ds(at, width), :]
            cols = []
            for n in range(2):
                lane = iota((width, lanes), 1) + (2 * step + n) * lanes
                cols.append(ones_where(code == lane))
            outs.append(mm(ref[...], jnp.concatenate(cols, axis=1)))
        total = (outs[0] + outs[1]).astype(BF)
        for n in range(2):
            at = 2 * step + n
            out_ref[at, 0:rows, :] = total[:, n * lanes : (n + 1) * lanes]
            goal = (iota((count, lanes), 1) + at * lanes) // per
            tally = mm(jnp.ones((all_rows - rows, count), BF), ones_where(owner == goal))
            out_ref[at, rows:all_rows, :] = tally.astype(BF)
        return carry

    lax.fori_loop(0, blocks // 2, block, 0)


def unpack_kernel(side, slots, got_ref, out_ref, where_ref, *wide_refs):
    blocks, all_rows, lanes = got_ref.shape
    chans, cells, cap = out_ref.shape
    rows = side * chans
    per = side * slots
    lane0, lane1 = iota((lanes, lanes), 0), iota((lanes, lanes), 1)
    heads = lane0 % per == 0
    before = ones_where(heads & (lane0 // per < lane1 // per))
    every = ones_where(heads)
    room = where_ref.shape[0]
    slot = (iota((room, lanes), 1) % slots).astype(F32)
    goal = iota((room, lanes), 0).astype(F32)
    running = jnp.zeros((1, lanes), F32)
    for b in range(blocks):
        tally = got_ref[b, rows:all_rows, :]
        inside = mm(tally, before)[0:1]
        whole = mm(tally, every)[0:1]
        first = running + inside
        live = slot < jnp.broadcast_to(tally.astype(F32)[0:1], (room, lanes))
        where_ref[:, b * lanes : (b + 1) * lanes] = ones_where(live & (goal == first + slot))
        running = running + whole

    def column(v, carry):
        keep = iota((rows, lanes), 1) % per // slots == v
        total = None
        for b in range(0, blocks, 2):
            pair = [
                jnp.where(keep, got_ref[b + n, 0:rows, :], jnp.zeros((rows, lanes), BF))
                for n in range(2)
            ]
            part = mm_nt(
                jnp.concatenate(pair, axis=1), where_ref[:, b * lanes : (b + 2) * lanes]
            )
            total = part if total is None else total + part
        for u in range(side):
            piece = total[u * chans : (u + 1) * chans]
            for n, ref in enumerate(wide_refs):
                ref[pl.ds(u * side + v, chans, stride=cells), :] = piece[:, n * lanes : (n + 1) * lanes]
        return carry

    lax.fori_loop(0, side, column, 0)
    for n, ref in enumerate(wide_refs):
        keep = min(lanes, cap - n * lanes)
        full = ref[...].astype(BF).reshape(chans, cells, lanes)
        out_ref[:, :, n * lanes : n * lanes + keep] = full[:, :, :keep]


def on_device(features, tile_valid, parent_owner, w_first, w_second, w_merge):
    chans, row_count, col_count = features.shape
    tile_rows, tile_cols = tile_valid.shape
    side = row_count // tile_rows
    parents_dev = parent_owner.shape[0]
    devices = lax.axis_size("tiles")
    slots = 2 * max(1, parents_dev // devices)
    own_cap = 3 * parents_dev // 2
    rows = row_count // 2
    core = lax.axis_index("chan")
    core1 = jnp.reshape(core, (1,)).astype(jnp.int32)
    swap = [(0, 1), (1, 0)]

    flat = chans * HALO
    send_main = lax.dynamic_slice_in_dim(features, (1 - core) * rows, rows, 1)
    mid_send = lax.dynamic_slice_in_dim(features, rows - HALO + HALO * core, HALO, 1)
    mid_own = lax.dynamic_slice_in_dim(features, rows - HALO * core, HALO, 1)
    flags = jnp.repeat(tile_valid[jnp.array([0, tile_rows - 1])].astype(BF), side, axis=1)
    flags = jnp.broadcast_to(flags[:, None, :], (2, chans, col_count))
    head = jnp.concatenate([features[:, : HALO - 1], flags[0][:, None]], axis=1)
    tail = jnp.concatenate([flags[1][:, None], features[:, row_count - HALO + 1 :]], axis=1)
    head, tail = head.reshape(flat, col_count), tail.reshape(flat, col_count)
    down_up = [(2 * t, 2 * t + 2) for t in range(devices - 1)]
    down_up += [(2 * t + 1, 2 * t - 1) for t in range(1, devices)]
    cross = [(2 * t + 1, 2 * t + 2) for t in range(devices - 1)]
    cross += [(2 * t, 2 * t - 1) for t in range(1, devices)]
    both = ("tiles", "chan")
    outer_own = lax.ppermute(jnp.where(core == 0, tail, head), both, down_up)
    outer_oth = lax.ppermute(jnp.where(core == 0, head, tail), both, cross)
    w_own = jnp.concatenate([w_first, w_second, jnp.swapaxes(w_merge, 1, 2)], axis=0)
    w_oth = lax.ppermute(w_own, "chan", swap)
    mid_oth = lax.ppermute(mid_send.reshape(flat, col_count), "chan", swap)
    recv = lax.ppermute(send_main, "chan", swap)

    vmem = pl.BlockSpec(memory_space=pltpu.VMEM)
    smem = pl.BlockSpec(memory_space=pltpu.SMEM)
    allc = 2 * chans
    width = parents_dev * side // 2
    e_own, e_oth, m_own, m_oth = pl.pallas_call(
        functools.partial(conv_kernel, side),
        out_shape=(
            jax.ShapeDtypeStruct((chans, rows, col_count), BF),
            jax.ShapeDtypeStruct((chans, rows, col_count), BF),
            jax.ShapeDtypeStruct((side * chans, width), BF),
            jax.ShapeDtypeStruct((side * chans, width), BF),
        ),
        in_specs=[smem, pl.BlockSpec(memory_space=pl.ANY)] + [vmem] * 8,
        out_specs=(vmem,) * 4,
        scratch_shapes=[
            pltpu.VMEM((chans, rows, col_count), BF),
            pltpu.VMEM((rows + 16, 3 * allc, col_count), BF),
            pltpu.VMEM((rows + side, 3 * allc, col_count), BF),
            pltpu.VMEM((rows + side, allc, col_count), BF),
            pltpu.VMEM((tile_rows + 2 * side, col_count), F32),
            pltpu.VMEM((3 * allc, 3 * allc), BF),
            pltpu.VMEM((3 * allc, 3 * allc), BF),
            pltpu.VMEM((allc, 4 * allc), BF),
            pltpu.VMEM((2, allc, col_count), F32),
            pltpu.VMEM((2, allc, col_count), F32),
            pltpu.SemaphoreType.DMA,
        ],
        name="conv",
    )(core1, features, recv, mid_own.reshape(flat, col_count), mid_oth, outer_own, outer_oth, tile_valid, w_own, w_oth)

    m_recv = lax.ppermute(m_oth, "chan", swap)
    e_recv = lax.ppermute(e_oth, "chan", swap)
    lanes = 128
    blocks = devices * slots * side // lanes
    all_rows = side * chans + 8
    packed = pl.pallas_call(
        functools.partial(pack_kernel, side, slots),
        out_shape=jax.ShapeDtypeStruct((blocks, all_rows, lanes), BF),
        in_specs=[smem, vmem, vmem, vmem],
        out_specs=vmem,
        scratch_shapes=[pltpu.VMEM((parents_dev * side, lanes), jnp.int32)],
        name="pack",
    )(core1, parent_owner[:, None], m_own, m_recv)

    def to_peers(x):
        fold = devices // blocks
        if fold > 1:
            x = x.reshape(blocks, all_rows, fold, lanes // fold)
            x = x.transpose(0, 2, 1, 3).reshape(devices, all_rows, lanes // fold)
        x = lax.all_to_all(x, "tiles", split_axis=0, concat_axis=0, tiled=True)
        if fold > 1:
            x = x.reshape(blocks, fold, all_rows, lanes // fold)
            x = x.transpose(0, 2, 1, 3).reshape(blocks, all_rows, lanes)
        return x

    got = to_peers(packed)
    cells = side * side
    room = pl.cdiv(own_cap, lanes) * lanes
    parents = pl.pallas_call(
        functools.partial(unpack_kernel, side, slots),
        out_shape=jax.ShapeDtypeStruct((chans, cells, own_cap), BF),
        in_specs=[vmem],
        out_specs=vmem,
        scratch_shapes=[
            pltpu.VMEM((room, blocks * lanes), BF),
        ]
        + [pltpu.VMEM((chans * cells, lanes), F32)] * (room // lanes),
        name="unpack",
    )(got)
    enhanced = jnp.where(
        core == 0,
        jnp.concatenate([e_own, e_recv], axis=1),
        jnp.concatenate([e_recv, e_own], axis=1),
    )
    return enhanced, jnp.swapaxes(parents, 1, 2)


def solution(mesh):
    return jax.shard_map(
        on_device,
        mesh=mesh,
        in_specs=(
            P("chan", "tiles", None),
            P("tiles", None),
            P("tiles"),
            P(None, "chan", None),
            P(None, "chan", None),
            P(None, None, "chan"),
        ),
        out_specs=(P("chan", "tiles", None), P("chan", "tiles", None)),
        check_vma=False,
    )
```

time: 211 us -> 86.2 us (0.41)
  matrix products: 72.8 us -> 0 us
  local copies, waits for them, and re-layouts: 63.5 us -> 8.57 us
  Pallas kernels: 0 us -> 31.9 us
  blocking collectives: 16.6 us -> 0 us
  starting transfers between devices: 24.2 us -> 13.1 us
  other arithmetic: 6.83 us -> 2.3 us
  waiting for transfers between devices: 24.8 us -> 29 us
    dot_general x22 -> x0, matrix products: 72.8 us -> none  [the longest x18 70.6 us: tap_sum(): jnp.einsum('oi,irc->orc', weights[3 * row_tap + col_tap], window, preferr...]
    pallas_call x0 -> x3, Pallas kernels: none -> 31.9 us  [the longest x1 18.3 us: on_device(): pl.pallas_call(functools.partial(conv_kernel, side), out_shape=(jax.Shape...]
    unnamed x35 -> x30, local copies, waits for them, and re-layouts: 31.6 us -> 2.76 us
    all_to_all x3 -> x1, starting transfers between devices: 18.3 us -> 5.74 us  [to_peers(): x = lax.all_to_all(x, 'tiles', split_axis=0, concat_axis=0, tiled=True)]
    slice x4 -> x2, local copies, waits for them, and re-layouts: 12.6 us -> 1.04 us  [the longest x1 1.03 us: on_device(): features[:, row_count - HALO + 1:]]
    all_to_all x2 -> x0, blocking collectives: 10.8 us -> none  [the longest x1 6.62 us: on_device(): lax.all_to_all(half_enhanced, 'chan', split_axis=0, concat_axis=1, tiled=...]
    convert_element_type x6 -> x0, local copies, waits for them, and re-layouts: 8.62 us -> none  [the longest x2 7.29 us: on_device(): half_enhanced = (half_mask.astype(jnp.float32) * (swapped.astype(jnp.floa...]
    ppermute x2 -> x7, waiting for transfers between devices: 0.01 us -> 7.39 us  [the longest x1 2.96 us: on_device(): outer_oth = lax.ppermute(jnp.where(core == 0, head, tail), both, cross)]
  transfers between devices with their start and end apart: 5 -> 8, of which waited for: 2 -> 5; matrix products, arithmetic and copies ran while one was open for 7% -> 8% of each run, Pallas kernels for 0% -> 0%
where the time goes in v1:
time: 86.2 us; the launch traced here: 85.8 us
  Pallas kernels  31.9 us (37%)
  waiting for transfers between devices  29 us (34%)
  starting transfers between devices  13.1 us (15%)
  local copies, waits for them, and re-layouts  8.57 us (10%)
  other arithmetic  2.3 us (3%)
  between operations  0.87 us (1%)
    all_to_all x1, waiting for transfers between devices, to_peers(): x = lax.all_to_all(x, 'tiles', split_axis=0, concat_axis=0, tiled=True)  21.7 us
    pallas_call x1, Pallas kernels, on_device(): pl.pallas_call(functools.partial(conv_kernel, side), out_shape=(jax.Shape...  18.3 us
    pallas_call x1, Pallas kernels, on_device(): pl.pallas_call(functools.partial(unpack_kernel, side, slots), out_shape=j...  8.52 us
    all_to_all x1, starting transfers between devices, to_peers(): x = lax.all_to_all(x, 'tiles', split_axis=0, concat_axis=0, tiled=True)  5.74 us
    pallas_call x1, Pallas kernels, on_device(): pl.pallas_call(functools.partial(pack_kernel, side, slots), out_shape=jax...  5.08 us
    ppermute x1, starting transfers between devices, on_device(): outer_own = lax.ppermute(jnp.where(core == 0, tail, head), both, down_up)  3.4 us
    ppermute x1, starting transfers between devices, on_device(): outer_oth = lax.ppermute(jnp.where(core == 0, head, tail), both, cross)  3.08 us
    ppermute x1, waiting for transfers between devices, on_device(): outer_oth = lax.ppermute(jnp.where(core == 0, head, tail), both, cross)  2.96 us
  transfers between devices with their start and end apart: 8, of which 5 were waited for; matrix products, arithmetic and copies ran while one was open for 8% of the time, Pallas kernels for 0%

profile of v1, /device:TPU:8, one launch (start us, length us, event | category | flops | bytes accessed | tf_op | source)
XLA Modules:
  0.0 85.8 jit_solution(7589158235645810139)
XLA Ops:
  0.7 1.4 %constant_dynamic-slice_fusion.2 = bf16[32,64,256]{2,1,0:T(8,128)(2,1)S(1)} fusion(bf16[32,128,256]{2,1,0:T(8,128)(2,1)} %feat_hbm.1, s32[]{:T(128)S(6)} %select_n.39), kind=kLoop, calls=%fused_computation.11 | loop fusion | bytes 2097156 | tf_op jit(solution)/shard_map/dynamic_slice | solution.py:334
  2.1 1.0 %constant_dynamic-slice_fusion = (bf16[32,4,256]{2,1,0:T(4,128)(2,1)S(1)}, bf16[32,4,256]{2,1,0:T(4,128)(2,1)S(1)}) fusion(bf16[32,128,256]{2,1,0:T(8,128)(2,1)} %feat_hbm.1, s32[]{:T(128)S(6)} %select_n.41, s32[]{:T(128)S(6)} %select_n.40), kind=kLoop, calls=%fused_computation.9 | loop fusion | bytes 262152 | tf_op jit(solution)/shard_map/dynamic_slice | solution.py:335
  3.2 0.6 collective-permute-start.1
  3.9 0.6 gather_fusion
  4.9 1.0 %fusion = (bf16[32,3,256]{2,1,0:T(4,128)(2,1)S(1)}, bf16[32,3,256]{2,1,0:T(4,128)(2,1)S(1)}) fusion(bf16[32,128,256]{2,1,0:T(8,128)(2,1)} %feat_hbm.1), kind=kLoop, calls=%fused_computation.14 | loop fusion | bytes 196608 | tf_op jit(solution)/shard_map/slice | solution.py:340
  6.0 0.2 broadcast_select_fusion
  6.2 3.4 %collective-permute-start.2 = (bf16[128,256]{1,0:T(8,128)(2,1)S(1)}, bf16[128,256]{1,0:T(8,128)(2,1)S(1)}, u32[]{:S(2)}, u32[]{:S(2)}) collective-permute-start(bf16[128,256]{1,0:T(8,128)(2,1)S(1)} %select_n.45), channel_id=1, source_target_pairs={{0,2},{2,4},{4,6},{6,8},{8,10},{10,12},{12,14},{14,16},{16,18},{18... | collective-permute-start | bytes 196616 | tf_op jit(solution)/shard_map/ppermute | solution.py:347
  9.6 3.1 %collective-permute-start.3 = (bf16[128,256]{1,0:T(8,128)(2,1)S(1)}, bf16[128,256]{1,0:T(8,128)(2,1)S(1)}, u32[]{:S(2)}, u32[]{:S(2)}) collective-permute-start(bf16[128,256]{1,0:T(8,128)(2,1)S(1)} %select_n.47), channel_id=1, source_target_pairs={{1,2},{3,4},{5,6},{7,8},{9,10},{11,12},{13,14},{15,16},{17,18},{19... | collective-permute-start | bytes 196616 | tf_op jit(solution)/shard_map/ppermute | solution.py:348
  12.7 0.6 reshape.31.mid_own_ref
  13.3 0.8 collective-permute-done.2.out_own_ref
  14.1 3.0 %collective-permute-done.3.out_oth_ref = bf16[128,256]{1,0:T(8,128)(2,1)S(1)} collective-permute-done((bf16[128,256]{1,0:T(8,128)(2,1)S(1)}, bf16[128,256]{1,0:T(8,128)(2,1)S(1)}, u32[]{:S(2)}, u32[]{:S(2)}) %collective-permute-start.3) | collective-permute-done | bytes 65568 | tf_op jit(solution)/shard_map/ppermute | solution.py:348
  17.1 0.6 copy-done.10
  17.8 0.4 copy-done.2
  18.1 18.3 %conv.1 = (bf16[32,64,256]{2,1,0:T(8,128)(2,1)}, bf16[32,64,256]{2,1,0:T(8,128)(2,1)}, bf16[256,512]{1,0:T(8,128)(2,1)}, bf16[256,512]{1,0:T(8,128)(2,1)}) custom-call(s32[1]{0:T(128)} %bitcast.core_ref, bf16[32,128,256]{2,1,0:T(8,128)(2,1)} %feat_hbm.1, bf16[32,64,256]{2,1,0:T(8,128)(2,1)} %copy-done.2, bf16[128,256]{1,0:T(8,128)(2,1)} %reshape.31.mid_own_ref, ...), custom_call_target="tpu_custom_call" | custom-call | tf_op jit(solution)/shard_map/conv/pallas_call | solution.py:358
  36.5 0.7 copy.10.owner_ref
  37.3 1.0 %collective-permute-done.6.mrecv_ref = bf16[256,512]{1,0:T(8,128)(2,1)S(1)} collective-permute-done((bf16[256,512]{1,0:T(8,128)(2,1)}, bf16[256,512]{1,0:T(8,128)(2,1)S(1)}, u32[]{:S(2)}, u32[]{:S(2)}) %collective-permute-start.6) | collective-permute-done | bytes 262176 | tf_op jit(solution)/shard_map/ppermute | solution.py:384
  38.3 0.7 copy-done.4
  39.0 5.1 %pack.1 = bf16[16,264,128]{2,1,0:T(8,128)(2,1)} custom-call(s32[1]{0:T(128)} %bitcast.core_ref, s32[128,1]{1,0:T(8,128)} %copy.10.owner_ref, bf16[256,512]{1,0:T(8,128)(2,1)} %get-tuple-element.8.mown_ref, bf16[256,512]{1,0:T(8,128)(2,1)} %copy-done.4), custom_call_target="tpu_custom_call" | custom-call | tf_op jit(solution)/shard_map/pack/pallas_call | solution.py:389
  44.0 5.7 %all-to-all-start = ((bf16[16,264,128]{2,1,0:T(8,128)(2,1)}), bf16[16,264,128]{2,1,0:T(8,128)(2,1)S(1)}, u32[]{:S(2)}, u32[]{:S(2)}) async-start(bf16[16,264,128]{2,1,0:T(8,128)(2,1)} %pack.1), calls=%async_computation | async-start | bytes 2162688 | tf_op jit(solution)/shard_map/all_to_all | solution.py:403
  49.9 2.6 %collective-permute-done.5 = bf16[32,64,256]{2,1,0:T(8,128)(2,1)S(1)} collective-permute-done((bf16[32,64,256]{2,1,0:T(8,128)(2,1)S(1)}, bf16[32,64,256]{2,1,0:T(8,128)(2,1)S(1)}, u32[]{:S(2)}, u32[]{:S(2)}) %collective-permute-start.5) | collective-permute-done | bytes 1048608 | tf_op jit(solution)/shard_map/ppermute | solution.py:385
  52.5 2.1 %maximum_select_fusion = bf16[32,128,256]{2,1,0:T(8,128)(2,1)} fusion(bf16[32,64,256]{2,1,0:T(8,128)(2,1)S(1)} %collective-permute-done.5, bf16[32,64,256]{2,1,0:T(8,128)(2,1)S(1)} %copy-done.1, pred[]{:T(512)S(6)} %eq.2), kind=kLoop, calls=%fused_computation.1 | loop fusion | flops 9437184 | bytes 4194305 | tf_op jit(solution)/shard_map/jit(_where)/select_n | solution.py:423
  54.6 21.7 %all-to-all-done.got_ref = bf16[16,264,128]{2,1,0:T(8,128)(2,1)S(1)} async-done(((bf16[16,264,128]{2,1,0:T(8,128)(2,1)}), bf16[16,264,128]{2,1,0:T(8,128)(2,1)S(1)}, u32[]{:S(2)}, u32[]{:S(2)}) %all-to-all-start) | async-done | bytes 1081376 | tf_op jit(solution)/shard_map/all_to_all | solution.py:403
  76.3 1.0 %copy-done = bf16[16,264,128]{2,1,0:T(8,128)(2,1)} copy-done((bf16[16,264,128]{2,1,0:T(8,128)(2,1)}, bf16[16,264,128]{2,1,0:T(8,128)(2,1)S(1)}, u32[]{:S(2)}) %copy-start) | copy-done | bytes 1081368
  77.3 8.5 %unpack.1 = bf16[32,64,192]{2,1,0:T(8,128)(2,1)} custom-call(bf16[16,264,128]{2,1,0:T(8,128)(2,1)} %copy-done), custom_call_target="tpu_custom_call" | custom-call | tf_op jit(solution)/shard_map/unpack/pallas_call | solution.py:412
  (47 shorter events, 1.0 us)
Async XLA Ops:
  0.6 3.1 %copy-start.12 = (bf16[4,64,32]{1,2,0:T(8,128)(2,1)S(1)}, bf16[4,64,32]{1,2,0:T(8,128)(2,1)}, u32[]{:S(2)}) copy-start(bf16[4,64,32]{1,2,0:T(8,128)(2,1)} %param.12) | copy-start | bytes 49156
  0.6 3.1 %copy-start.6 = (bf16[9,32,64]{2,1,0:T(8,128)(2,1)S(1)}, bf16[9,32,64]{2,1,0:T(8,128)(2,1)}, u32[]{:S(2)}) copy-start(bf16[9,32,64]{2,1,0:T(8,128)(2,1)} %param.11) | copy-start | bytes 110596
  0.7 3.1 %copy-start.7 = (bf16[9,32,64]{2,1,0:T(8,128)(2,1)S(1)}, bf16[9,32,64]{2,1,0:T(8,128)(2,1)}, u32[]{:S(2)}) copy-start(bf16[9,32,64]{2,1,0:T(8,128)(2,1)} %param.10) | copy-start | bytes 110596
  0.7 3.3 %copy-start.11 = (s32[16,32]{1,0:T(8,128)S(1)}, s32[16,32]{1,0:T(8,128)}, u32[]{:S(2)}) copy-start(s32[16,32]{1,0:T(8,128)} %valid_ref.1) | copy-start | bytes 6148
  2.0 15.0 %collective-permute-start = (bf16[32,64,256]{2,1,0:T(8,128)(2,1)S(1)}, bf16[32,64,256]{2,1,0:T(8,128)(2,1)S(1)}, u32[]{:S(2)}, u32[]{:S(2)}) collective-permute-start(bf16[32,64,256]{2,1,0:T(8,128)(2,1)S(1)} %constant_dynamic-slice_fusion.2), channel_id=1, source_target_pairs={{0,1},{1,0},{2,3},{3,2},{4,5},{5,4},{6,7},{7,6},{8,9},{9,8},{10,11... | collective-permute-start | bytes 3145736 | tf_op jit(solution)/shard_map/ppermute | solution.py:352
  3.2 10.1 %collective-permute-start.1 = (bf16[128,256]{1,0:T(8,128)(2,1)S(1)}, bf16[128,256]{1,0:T(8,128)(2,1)S(1)}, u32[]{:S(2)}, u32[]{:S(2)}) collective-permute-start(bf16[128,256]{1,0:T(8,128)(2,1)S(1)} %reshape.32), channel_id=1, source_target_pairs={{0,1},{1,0},{2,3},{3,2},{4,5},{5,4},{6,7},{7,6},{8,9},{9,8},{10,11... | collective-permute-start | bytes 196616 | tf_op jit(solution)/shard_map/ppermute | solution.py:351
  3.8 13.3 %copy-start.3 = (bf16[22,32,64]{2,1,0:T(8,128)(2,1)}, bf16[22,32,64]{2,1,0:T(8,128)(2,1)S(1)}, u32[]{:S(2)}) copy-start(bf16[22,32,64]{2,1,0:T(8,128)(2,1)S(1)} %pad_maximum_fusion.wown_ref) | copy-start | bytes 270340
  3.8 13.3 %collective-permute-start.4 = (bf16[22,32,64]{2,1,0:T(8,128)(2,1)S(1)}, bf16[22,32,64]{2,1,0:T(8,128)(2,1)S(1)}, u32[]{:S(2)}, u32[]{:S(2)}) collective-permute-start(bf16[22,32,64]{2,1,0:T(8,128)(2,1)S(1)} %pad_maximum_fusion.wown_ref), channel_id=1, source_target_pairs={{0,1},{1,0},{2,3},{3,2},{4,5},{5,4},{6,7},{7,6},{8,9},{9,8},{10,11... | collective-permute-start | bytes 270344 | tf_op jit(solution)/shard_map/ppermute | solution.py:350
  6.1 30.4 %copy-start.13 = (s32[128]{0:T(128)S(1)}, s32[128]{0:T(128)}, u32[]{:S(2)}) copy-start(s32[128]{0:T(128)} %param.9) | copy-start | bytes 1540
  6.2 8.0 %collective-permute-start.2 = (bf16[128,256]{1,0:T(8,128)(2,1)S(1)}, bf16[128,256]{1,0:T(8,128)(2,1)S(1)}, u32[]{:S(2)}, u32[]{:S(2)}) collective-permute-start(bf16[128,256]{1,0:T(8,128)(2,1)S(1)} %select_n.45), channel_id=1, source_target_pairs={{0,2},{2,4},{4,6},{6,8},{8,10},{10,12},{12,14},{14,16},{16,18},{18... | collective-permute-start | bytes 196616 | tf_op jit(solution)/shard_map/ppermute | solution.py:347
  9.6 7.5 %collective-permute-start.3 = (bf16[128,256]{1,0:T(8,128)(2,1)S(1)}, bf16[128,256]{1,0:T(8,128)(2,1)S(1)}, u32[]{:S(2)}, u32[]{:S(2)}) collective-permute-start(bf16[128,256]{1,0:T(8,128)(2,1)S(1)} %select_n.47), channel_id=1, source_target_pairs={{1,2},{3,4},{5,6},{7,8},{9,10},{11,12},{13,14},{15,16},{17,18},{19... | collective-permute-start | bytes 196616 | tf_op jit(solution)/shard_map/ppermute | solution.py:348
  13.3 3.8 %copy-start.8 = (bf16[128,256]{1,0:T(8,128)(2,1)}, bf16[128,256]{1,0:T(8,128)(2,1)S(1)}, u32[]{:S(2)}) copy-start(bf16[128,256]{1,0:T(8,128)(2,1)S(1)} %collective-permute-done.1.mid_oth_ref) | copy-start | bytes 196612
  14.1 3.0 %copy-start.9 = (bf16[128,256]{1,0:T(8,128)(2,1)}, bf16[128,256]{1,0:T(8,128)(2,1)S(1)}, u32[]{:S(2)}) copy-start(bf16[128,256]{1,0:T(8,128)(2,1)S(1)} %collective-permute-done.2.out_own_ref) | copy-start | bytes 196612
  17.1 0.6 copy-start.10
  17.1 0.7 copy-start.5
  17.1 1.0 %copy-start.2 = (bf16[32,64,256]{2,1,0:T(8,128)(2,1)}, bf16[32,64,256]{2,1,0:T(8,128)(2,1)S(1)}, u32[]{:S(2)}) copy-start(bf16[32,64,256]{2,1,0:T(8,128)(2,1)S(1)} %collective-permute-done.recv_ref) | copy-start | bytes 3145732
  36.4 16.1 %copy-start.1 = (bf16[32,64,256]{2,1,0:T(8,128)(2,1)S(1)}, bf16[32,64,256]{2,1,0:T(8,128)(2,1)}, u32[]{:S(2)}) copy-start(bf16[32,64,256]{2,1,0:T(8,128)(2,1)} %get-tuple-element.6) | copy-start | bytes 3145732
  36.4 1.8 %collective-permute-start.6 = (bf16[256,512]{1,0:T(8,128)(2,1)}, bf16[256,512]{1,0:T(8,128)(2,1)S(1)}, u32[]{:S(2)}, u32[]{:S(2)}) collective-permute-start(bf16[256,512]{1,0:T(8,128)(2,1)} %get-tuple-element.9), channel_id=1, source_target_pairs={{0,1},{1,0},{2,3},{3,2},{4,5},{5,4},{6,7},{7,6},{8,9},{9,8},{10,11... | collective-permute-start | bytes 786440 | tf_op jit(solution)/shard_map/ppermute | solution.py:384
  37.3 12.5 %copy-start.14 = (bf16[32,64,256]{2,1,0:T(8,128)(2,1)S(1)}, bf16[32,64,256]{2,1,0:T(8,128)(2,1)}, u32[]{:S(2)}) copy-start(bf16[32,64,256]{2,1,0:T(8,128)(2,1)} %get-tuple-element.7) | copy-start | bytes 3145732
  38.3 0.7 copy-start.4
  44.0 32.2 %all-to-all-start = ((bf16[16,264,128]{2,1,0:T(8,128)(2,1)}), bf16[16,264,128]{2,1,0:T(8,128)(2,1)S(1)}, u32[]{:S(2)}, u32[]{:S(2)}) async-start(bf16[16,264,128]{2,1,0:T(8,128)(2,1)} %pack.1), calls=%async_computation | async-start | bytes 2162688 | tf_op jit(solution)/shard_map/all_to_all | solution.py:403
  49.8 2.7 %collective-permute-start.5 = (bf16[32,64,256]{2,1,0:T(8,128)(2,1)S(1)}, bf16[32,64,256]{2,1,0:T(8,128)(2,1)S(1)}, u32[]{:S(2)}, u32[]{:S(2)}) collective-permute-start(bf16[32,64,256]{2,1,0:T(8,128)(2,1)S(1)} %copy-done.14), channel_id=1, source_target_pairs={{0,1},{1,0},{2,3},{3,2},{4,5},{5,4},{6,7},{7,6},{8,9},{9,8},{10,11... | collective-permute-start | bytes 3145736 | tf_op jit(solution)/shard_map/ppermute | solution.py:385
  76.3 1.0 %copy-start = (bf16[16,264,128]{2,1,0:T(8,128)(2,1)}, bf16[16,264,128]{2,1,0:T(8,128)(2,1)S(1)}, u32[]{:S(2)}) copy-start(bf16[16,264,128]{2,1,0:T(8,128)(2,1)S(1)} %all-to-all-done.got_ref) | copy-start | bytes 3244036

commit v2 on v1

v2 whole, which is shorter than its diff:
```python
import functools

import jax
import jax.numpy as jnp
from jax import lax
from jax.experimental import pallas as pl
from jax.experimental.pallas import tpu as pltpu
from jax.sharding import PartitionSpec as P

BF = jnp.bfloat16
F32 = jnp.float32
HALO = 4
BLK = 16


def iota(shape, dim):
    return lax.broadcasted_iota(jnp.int32, shape, dim)


def ones_where(cond):
    return jnp.where(cond, 1.0, 0.0).astype(BF)


def mm(a, b):
    return jnp.dot(a, b, preferred_element_type=F32)


def mm_nt(a, b):
    return lax.dot_general(a, b, (((1,), (1,)), ((), ())), preferred_element_type=F32)


def swap_matrix(outer, inner):
    n = outer * inner
    row, col = iota((n, n), 0), iota((n, n), 1)
    return ones_where((row % inner == col // outer) & (row // inner == col % outer))


def shifted(x, amount):
    lanes = 128
    parts = [x[:, at : at + lanes] for at in range(0, x.shape[1], lanes)]
    turned = [pltpu.roll(p, amount % lanes, 1) for p in parts]
    lane = iota(parts[0].shape, 1)
    zero = jnp.zeros_like(parts[0])
    outs = []
    for n in range(len(parts)):
        if amount > 0:
            edge = turned[n - 1] if n else zero
            outs.append(jnp.where(lane < amount, edge, turned[n]))
        else:
            edge = turned[n + 1] if n + 1 < len(parts) else zero
            outs.append(jnp.where(lane >= lanes + amount, edge, turned[n]))
    return jnp.concatenate(outs, axis=1)


def widen_matrix(tiles_c, cols, side):
    return ones_where(iota((tiles_c, cols), 1) // side == iota((tiles_c, cols), 0))


def as_bf(x):
    return x.astype(F32).astype(BF)


def edges_kernel(side, place_ref, feat_hbm, valid_ref, one_ref, two_ref, edge, sems):
    core = place_ref[0]
    chans, rows, cols = feat_hbm.shape
    copies = []
    for n, at in enumerate((0, rows - BLK)):
        copies.append(pltpu.make_async_copy(feat_hbm.at[:, at : at + BLK, :], edge.at[n], sems.at[n]))
        copies[-1].start()
    tiles_r, tiles_c = valid_ref.shape
    masks = mm(as_bf(valid_ref[...]), widen_matrix(tiles_c, cols, side))
    flat = chans * HALO
    row, col = iota((flat, chans * BLK), 0), iota((flat, chans * BLK), 1)
    same = row // HALO == col // BLK
    spot = iota((flat, cols), 0) % HALO
    made = []
    for n in range(2):
        if n == 0:
            hit = same & (row % HALO == col % BLK) & (row % HALO < HALO - 1)
            flag, line = spot == HALO - 1, masks[0:1]
        else:
            hit = same & (row % HALO + BLK - HALO == col % BLK) & (row % HALO > 0)
            flag, line = spot == 0, masks[tiles_r - 1 : tiles_r]
        take = ones_where(hit)
        copies[n].wait()
        body = mm(take, edge[n].reshape(chans * BLK, cols))
        made.append(jnp.where(flag, jnp.broadcast_to(line, (flat, cols)), body).astype(BF))
    low = core == 0
    one_ref[...] = jnp.where(low, made[1], made[0])
    two_ref[...] = jnp.where(low, made[0], made[1])


def weights_kernel(place_ref, wown_ref, woth_ref, w1_ref, w2_ref, wm_ref):
    core = place_ref[0]
    chans, allc = wown_ref.shape[1:]
    for dst, base in ((w1_ref, 0), (w2_ref, 9)):
        total = None
        for b in range(3):
            tall = jnp.concatenate(
                [ref[base + 3 * a + b] for a in range(3) for ref in (wown_ref, woth_ref)], axis=0
            )
            src, pos = iota((allc, 3 * allc), 0), iota((allc, 3 * allc), 1)
            place = ones_where(pos == b * allc + (src + chans * core) % allc)
            part = mm(tall, place)
            total = part if total is None else total + part
        dst[...] = total.astype(BF)
    tall = jnp.concatenate(
        [ref[18 + 2 * a + b] for b in range(2) for a in range(2) for ref in (wown_ref, woth_ref)],
        axis=0,
    )
    order = ones_where(iota((allc, allc), 1) == (iota((allc, allc), 0) + chans * core) % allc)
    wm_ref[...] = mm_nt(order, tall).astype(BF)


def conv_kernel(
    side,
    place_ref,
    own_hbm,
    oth_hbm,
    out_own_ref,
    out_oth_ref,
    valid_ref,
    w1,
    w2,
    wm,
    es_hbm,
    mown_ref,
    moth_ref,
    feat,
    xs,
    hs,
    es,
    mask,
    pa_ref,
    pb_ref,
    in_sems,
    out_sem,
):
    core = place_ref[0]
    rows, allc, cols = es_hbm.shape
    chans = allc // 2
    main = rows // BLK
    copies = []
    for m in range(main + 1):
        at = rows - BLK * core if m == main else rows * core + BLK * m
        for n, ref in enumerate((own_hbm, oth_hbm)):
            copy = pltpu.make_async_copy(
                ref.at[:, pl.ds(pl.multiple_of(at, BLK), BLK), :], feat.at[n, m], in_sems.at[n, m]
            )
            copy.start()
            copies.append(copy)

    tiles_r, tiles_c = valid_ref.shape
    mask[pl.ds(side, tiles_r), :] = mm(as_bf(valid_ref[...]), widen_matrix(tiles_c, cols, side))

    def put(dst, index, x, amount):
        dst[index, 0:allc, :] = shifted(x, amount)
        dst[index, allc : 2 * allc, :] = x
        dst[index, 2 * allc : 3 * allc, :] = shifted(x, -amount)

    first_row = 5
    turn4 = swap_matrix(HALO, chans)
    own, oth = mm(turn4, out_own_ref[...]), mm(turn4, out_oth_ref[...])
    start = jnp.where(core == 0, first_row - HALO, first_row + rows)
    for r in range(HALO):
        at = slice(r * chans, (r + 1) * chans)
        put(xs, start + r, jnp.concatenate([own[at], oth[at]], axis=0).astype(BF), 1)
    top = own[0:1, :]
    bottom = own[(HALO - 1) * chans : (HALO - 1) * chans + 1, :]

    @pl.when(core == 0)
    def _():
        mask[pl.ds(side - 1, 1), :] = top

    @pl.when(core == 1)
    def _():
        mask[pl.ds(side + tiles_r, 1), :] = bottom

    xs[0] = jnp.zeros(xs.shape[1:], BF)
    turn = swap_matrix(BLK, BLK)
    few = HALO * BLK
    row, col = iota((few, BLK * BLK), 0), iota((few, BLK * BLK), 1)
    turn_mid = ones_where(
        (row % BLK == col // BLK) & (row // BLK + (BLK - HALO) * core == col % BLK)
    )
    mid_start = jnp.where(core == 0, first_row + rows, first_row - HALO)
    for m in range(main + 1):
        for copy in copies[2 * m : 2 * m + 2]:
            copy.wait()
        parts = []
        for n in range(2):
            for ch in range(0, chans, BLK):
                block = feat[n, m, ch : ch + BLK].reshape(BLK * BLK, cols)
                parts.append(mm(turn_mid if m == main else turn, block).astype(BF))
        at = mid_start if m == main else first_row + m * BLK
        for r in range(HALO if m == main else BLK):
            x = jnp.concatenate([p[r * BLK : (r + 1) * BLK] for p in parts], axis=0)
            put(xs, at + r, x, 1)

    base = side + core * (rows // side)
    total_steps = rows // side + 1
    tiles = 3 if total_steps % 3 == 0 else 1
    group = tiles * side

    def lines(step, ahead):
        return [mask[pl.ds(base + step * tiles + k - 1, 1), :] for k in range(tiles + ahead)]

    pa_ref[...] = jnp.zeros(pa_ref.shape, F32)
    pb_ref[...] = jnp.zeros(pb_ref.shape, F32)

    def first(step, carry):
        pa, pb = pa_ref[0], pb_ref[0]
        flag = lines(step, 1)
        for j in range(group):
            q = step * group + j
            y = mm(w1[...], xs[q])
            total = pa + y[2 * allc :]
            pa = pb + y[allc : 2 * allc]
            pb = y[:allc]
            h = jnp.maximum(total * flag[(j + 2) // side], 0.0)
            put(hs, q, h.astype(BF), 2)
        pa_ref[0] = pa
        pb_ref[0] = pb
        return carry

    lax.fori_loop(0, total_steps // tiles, first, 0)

    pa_ref[0] = jnp.zeros((allc, cols), F32)
    pb_ref[0] = jnp.zeros((allc, cols), F32)
    half = cols // 2
    lane = iota((cols, cols), 1)
    pick = ones_where(iota((cols, cols), 0) == 2 * (lane % half) + lane // half)

    def out_copy(tile):
        at = pl.multiple_of(tile * side, side)
        return pltpu.make_async_copy(
            es.at[pl.ds(at + side, side)], es_hbm.at[pl.ds(at, side)], out_sem
        )

    def second(step, carry):
        pa, pb = [pa_ref[0], pa_ref[1]], [pb_ref[0], pb_ref[1]]
        flag = lines(step, 0)
        for t in range(tiles):
            rows_e = []
            for j in range(t * side, (t + 1) * side):
                q = step * group + j
                i = j % 2
                z = mm(w2[...], hs[q])
                total = pa[i] + z[2 * allc :]
                pa[i] = pb[i] + z[allc : 2 * allc]
                pb[i] = z[:allc]
                x = xs[jnp.maximum(q - 3, 0), allc : 2 * allc, :].astype(F32)
                e = (flag[t] * (x + total)).astype(BF)
                es[q] = e
                rows_e.append(e)
            tile = jnp.maximum(step * tiles + t - 1, 0)
            s = mm(jnp.concatenate(rows_e, axis=0), pick).astype(BF)
            pairs = []
            for k in range(side // 2):
                sp = s[k * 2 * allc : (k + 1) * 2 * allc]
                pairs.append(jnp.concatenate([sp[:, :half], sp[:, half:]], axis=0))
            for k in range(0, side // 2, 2):
                both = mm(wm[...], jnp.concatenate(pairs[k : k + 2], axis=1)).astype(BF)
                for n in range(2):
                    u = (side // 2) * (tile % 2) + k + n
                    at_u = pl.ds(pl.multiple_of(u * chans, chans), chans)
                    at_g = pl.ds(pl.multiple_of((tile // 2) * half, half), half)
                    piece = both[:, n * half : (n + 1) * half]
                    mown_ref[at_u, at_g] = piece[:chans]
                    moth_ref[at_u, at_g] = piece[chans:]
        for i in range(2):
            pa_ref[i] = pa[i]
            pb_ref[i] = pb[i]
        return carry

    lax.fori_loop(0, total_steps // tiles, second, 0)
    whole = pltpu.make_async_copy(es.at[pl.ds(side, rows)], es_hbm, out_sem)
    whole.start()
    whole.wait()


def restore_kernel(place_ref, es_ref, enh_hbm, eoth_ref, own, sem):
    core = place_ref[0]
    rows, allc, cols = es_ref.shape
    chans = allc // 2
    turn = swap_matrix(BLK, BLK)
    for c0 in list(range(chans, allc, BLK)) + list(range(0, chans, BLK)):
        ref = own if c0 < chans else eoth_ref
        ch = c0 % chans
        for at in range(0, rows, BLK):
            block = es_ref[at : at + BLK, c0 : c0 + BLK, :].reshape(BLK * BLK, cols)
            ref[ch : ch + BLK, at : at + BLK, :] = mm(turn, block).astype(BF).reshape(BLK, BLK, cols)
    copy = pltpu.make_async_copy(
        own, enh_hbm.at[:, pl.ds(pl.multiple_of(core * rows, rows), rows), :], sem
    )
    copy.start()
    copy.wait()


def fill_kernel(place_ref, recv_ref, held_hbm, enh_hbm, sem):
    core = place_ref[0]
    rows = recv_ref.shape[1]
    copy = pltpu.make_async_copy(
        recv_ref, enh_hbm.at[:, pl.ds(pl.multiple_of((1 - core) * rows, rows), rows), :], sem
    )
    copy.start()
    copy.wait()


def pack_kernel(side, slots, place_ref, owner_ref, mown_ref, mrecv_ref, out_ref, code_ref):
    core, turn = place_ref[0], place_ref[1]
    count = owner_ref.shape[1]
    rows, width = mown_ref.shape
    blocks, all_rows, lanes = out_ref.shape
    per = side * slots
    row = jnp.broadcast_to(owner_ref[...].astype(F32), (lanes, count))
    owner = jnp.transpose(row).astype(jnp.int32)
    is_owner = owner == iota((count, lanes), 1)
    lower = ones_where(iota((count, count), 0) > iota((count, count), 1))
    earlier = mm(lower, ones_where(is_owner))
    within = jnp.sum(jnp.where(is_owner, earlier, 0.0), axis=1, keepdims=True)
    code = (owner * per).astype(F32) + within
    wide = jnp.broadcast_to(code[:, None, :], (count, side, lanes))
    step_v = ((iota((count, side, lanes), 1) + turn) % side * slots).astype(F32)
    code_ref[...] = (wide + step_v).reshape(count * side, lanes).astype(jnp.int32)
    own_at = pl.multiple_of(core * width, width)
    oth_at = pl.multiple_of((1 - core) * width, width)
    data = jnp.concatenate([mown_ref[...], mrecv_ref[...]], axis=1)
    codes = jnp.concatenate(
        [code_ref[pl.ds(own_at, width), :], code_ref[pl.ds(oth_at, width), :]], axis=0
    )
    code_ref[...] = codes
    lane = iota((2 * width, lanes), 1)
    for step in range(0, blocks, 2):
        codes = code_ref[...]
        spots = [ones_where(codes == lane + at * lanes) for at in (step, step + 1)]
        total = mm(data, jnp.concatenate(spots, axis=1)).astype(BF)
        for n in range(2):
            at = step + n
            out_ref[at, 0:rows, :] = total[:, n * lanes : (n + 1) * lanes]
            goal = (iota((count, lanes), 1) + at * lanes) // per
            tally = mm(jnp.ones((all_rows - rows, count), BF), ones_where(owner == goal))
            out_ref[at, rows:all_rows, :] = tally.astype(BF)


def places(tallies, room, lanes, group, slots):
    lane0, lane1 = iota((lanes, lanes), 0), iota((lanes, lanes), 1)
    heads = lane0 % group == 0
    before = ones_where(heads & (lane0 // group < lane1 // group))
    every = ones_where(heads)
    slot = (iota((room, lanes), 1) % slots).astype(F32)
    goal = iota((room, lanes), 0).astype(F32)
    running = jnp.zeros((1, lanes), F32)
    outs = []
    for tally in tallies:
        inside, whole = mm(tally, before)[0:1], mm(tally, every)[0:1]
        live = slot < jnp.broadcast_to(tally.astype(F32)[0:1], (room, lanes))
        outs.append(jnp.where(live & (goal == running + inside + slot), 1.0, 0.0))
        running = running + whole
    return outs


def unpack_kernel(side, slots, got_ref, out_ref, picked):
    blocks, all_rows, lanes = got_ref.shape
    chans, cells, cap = out_ref.shape
    rows = side * chans
    per = side * slots
    room = picked.shape[2]
    if per == lanes:
        halves = blocks // side
        group = iota((all_rows - rows, lanes), 1) // slots
        tallies = []
        for h in range(halves):
            tally = got_ref[h * side, rows:all_rows, :].astype(F32)
            for s in range(1, side):
                other = got_ref[h * side + s, rows:all_rows, :].astype(F32)
                tally = jnp.where(group == s, other, tally)
            tallies.append(tally.astype(BF))
        spots = places(tallies, room, lanes, slots, slots)
        lane = iota((rows, lanes), 1) // slots
        data = []
        for h in range(halves):
            now = [got_ref[h * side + s, 0:rows, :] for s in range(side)]
            bit = 1
            while bit < side:
                odd = lane // bit % 2 == 1
                now = [jnp.where(odd, now[(j + bit) % side], now[j]) for j in range(side)]
                bit *= 2
            data.append(now)
        for v in range(side):
            lhs = jnp.concatenate([data[h][-v % side] for h in range(halves)], axis=1)
            rhs = [pltpu.roll(s, v * slots, 1) if v else s for s in spots]
            picked[v] = mm_nt(lhs, jnp.concatenate(rhs, axis=1).astype(BF)).astype(BF)
    else:
        tallies = [got_ref[b, rows:all_rows, :] for b in range(blocks)]
        spots = jnp.concatenate(places(tallies, room, lanes, per, slots), axis=1).astype(BF)
        for v in range(side):
            keep = iota((rows, lanes), 1) % per // slots == v
            lhs = jnp.concatenate(
                [jnp.where(keep, got_ref[b, 0:rows, :], jnp.zeros((rows, lanes), BF)) for b in range(blocks)],
                axis=1,
            )
            picked[v] = mm_nt(lhs, spots).astype(BF)
    two = BLK // side
    n = BLK * BLK
    row, col = iota((n, n), 0), iota((n, n), 1)
    turn = ones_where(
        (row // BLK == col % BLK)
        & (row // side % two == col // BLK % two)
        & (row % side == col // (BLK * two))
    )
    for u in range(0, side, two):
        for ch in range(0, chans, BLK):
            block = jnp.concatenate(
                [
                    picked[v, (u + w) * chans + ch : (u + w) * chans + ch + BLK, :]
                    for v in range(side)
                    for w in range(two)
                ],
                axis=0,
            )
            done = mm(turn, block).astype(BF).reshape(BLK, BLK, room)
            out_ref[ch : ch + BLK, u * side : (u + two) * side, :] = done[:, :, :cap]


def on_device(features, tile_valid, parent_owner, w_first, w_second, w_merge):
    chans, row_count, col_count = features.shape
    tile_rows, tile_cols = tile_valid.shape
    side = row_count // tile_rows
    parents_dev = parent_owner.shape[0]
    devices = lax.axis_size("tiles")
    slots = 2 * max(1, parents_dev // devices)
    own_cap = 3 * parents_dev // 2
    rows = row_count // 2
    allc = 2 * chans
    lanes = 128
    blocks = devices * slots * side // lanes
    fold = devices // blocks
    core = lax.axis_index("chan")
    turn = lax.axis_index("tiles") % side if fold == 1 else jnp.zeros_like(core)
    place = jnp.stack([core, turn]).astype(jnp.int32)
    swap = [(0, 1), (1, 0)]
    vmem = pl.BlockSpec(memory_space=pltpu.VMEM)
    smem = pl.BlockSpec(memory_space=pltpu.SMEM)
    hbm = pl.BlockSpec(memory_space=pl.ANY)

    def limit(mib):
        return pltpu.CompilerParams(vmem_limit_bytes=mib << 20)

    flat = chans * HALO
    feat_oth = lax.ppermute(features, "chan", swap)
    w_own = jnp.concatenate([w_first, w_second, jnp.swapaxes(w_merge, 1, 2)], axis=0)
    w_oth = lax.ppermute(w_own, "chan", swap)
    edge_one, edge_two = pl.pallas_call(
        functools.partial(edges_kernel, side),
        out_shape=(jax.ShapeDtypeStruct((flat, col_count), BF),) * 2,
        in_specs=[smem, hbm, vmem],
        out_specs=(vmem,) * 2,
        scratch_shapes=[
            pltpu.VMEM((2, chans, BLK, col_count), BF),
            pltpu.SemaphoreType.DMA((2,)),
        ],
        compiler_params=limit(6),
        name="edges",
    )(place, features, tile_valid)
    down_up = [(2 * t, 2 * t + 2) for t in range(devices - 1)]
    down_up += [(2 * t + 1, 2 * t - 1) for t in range(1, devices)]
    cross = [(2 * t + 1, 2 * t + 2) for t in range(devices - 1)]
    cross += [(2 * t, 2 * t - 1) for t in range(1, devices)]
    out_own = lax.ppermute(edge_one, ("tiles", "chan"), down_up)
    out_oth = lax.ppermute(edge_two, ("tiles", "chan"), cross)
    w1, w2, wm = pl.pallas_call(
        weights_kernel,
        out_shape=(
            jax.ShapeDtypeStruct((3 * allc, 3 * allc), BF),
            jax.ShapeDtypeStruct((3 * allc, 3 * allc), BF),
            jax.ShapeDtypeStruct((allc, 4 * allc), BF),
        ),
        in_specs=[smem, vmem, vmem],
        out_specs=(vmem,) * 3,
        compiler_params=limit(6),
        name="weights",
    )(place, w_own, w_oth)

    width = parents_dev * side // 2
    es, m_own, m_oth = pl.pallas_call(
        functools.partial(conv_kernel, side),
        out_shape=(
            jax.ShapeDtypeStruct((rows, allc, col_count), BF),
            jax.ShapeDtypeStruct((side * chans, width), BF),
            jax.ShapeDtypeStruct((side * chans, width), BF),
        ),
        in_specs=[smem, hbm, hbm] + [vmem] * 6,
        out_specs=(hbm, vmem, vmem),
        scratch_shapes=[
            pltpu.VMEM((2, rows // BLK + 1, chans, BLK, col_count), BF),
            pltpu.VMEM((rows + 16, 3 * allc, col_count), BF),
            pltpu.VMEM((rows + side, 3 * allc, col_count), BF),
            pltpu.VMEM((rows + side, allc, col_count), BF),
            pltpu.VMEM((tile_rows + 2 * side, col_count), F32),
            pltpu.VMEM((2, allc, col_count), F32),
            pltpu.VMEM((2, allc, col_count), F32),
            pltpu.SemaphoreType.DMA((2, rows // BLK + 1)),
            pltpu.SemaphoreType.DMA,
        ],
        compiler_params=limit(36),
        name="conv",
    )(place, features, feat_oth, out_own, out_oth, tile_valid, w1, w2, wm)

    m_recv = lax.ppermute(m_oth, "chan", swap)
    all_rows = side * chans + 8
    packed = pl.pallas_call(
        functools.partial(pack_kernel, side, slots),
        out_shape=jax.ShapeDtypeStruct((blocks, all_rows, lanes), BF),
        in_specs=[smem, vmem, vmem, vmem],
        out_specs=vmem,
        scratch_shapes=[pltpu.VMEM((parents_dev * side, lanes), jnp.int32)],
        compiler_params=limit(16),
        name="pack",
    )(place, parent_owner[None, :], m_own, m_recv)

    def to_peers(x):
        if fold > 1:
            x = x.reshape(blocks, all_rows, fold, lanes // fold)
            x = x.transpose(0, 2, 1, 3).reshape(devices, all_rows, lanes // fold)
        x = lax.all_to_all(x, "tiles", split_axis=0, concat_axis=0, tiled=True)
        if fold > 1:
            x = x.reshape(blocks, fold, all_rows, lanes // fold)
            x = x.transpose(0, 2, 1, 3).reshape(blocks, all_rows, lanes)
        return x

    es, packed = lax.optimization_barrier((es, packed))
    got = to_peers(packed)
    held, e_oth = pl.pallas_call(
        restore_kernel,
        out_shape=(
            jax.ShapeDtypeStruct((chans, row_count, col_count), BF),
            jax.ShapeDtypeStruct((chans, rows, col_count), BF),
        ),
        in_specs=[smem, vmem],
        out_specs=(hbm, vmem),
        scratch_shapes=[pltpu.VMEM((chans, rows, col_count), BF), pltpu.SemaphoreType.DMA],
        compiler_params=limit(12),
        name="restore",
    )(place, es)
    e_recv = lax.ppermute(e_oth, "chan", swap)
    enhanced = pl.pallas_call(
        fill_kernel,
        out_shape=jax.ShapeDtypeStruct((chans, row_count, col_count), BF),
        in_specs=[smem, vmem, hbm],
        out_specs=hbm,
        scratch_shapes=[pltpu.SemaphoreType.DMA],
        input_output_aliases={2: 0},
        compiler_params=limit(6),
        name="fill",
    )(place, e_recv, held)
    room = pl.cdiv(own_cap, lanes) * lanes
    parents = pl.pallas_call(
        functools.partial(unpack_kernel, side, slots),
        out_shape=jax.ShapeDtypeStruct((chans, side * side, own_cap), BF),
        in_specs=[vmem],
        out_specs=vmem,
        scratch_shapes=[pltpu.VMEM((side, side * chans, room), BF)],
        compiler_params=limit(24),
        name="unpack",
    )(got)
    return enhanced, jnp.swapaxes(parents, 1, 2)


def solution(mesh):
    return jax.shard_map(
        on_device,
        mesh=mesh,
        in_specs=(
            P("chan", "tiles", None),
            P("tiles", None),
            P("tiles"),
            P(None, "chan", None),
            P(None, "chan", None),
            P(None, None, "chan"),
        ),
        out_specs=(P("chan", "tiles", None), P("chan", "tiles", None)),
        check_vma=False,
    )
```

time: 86.2 us -> 69.5 us (0.81)
  Pallas kernels: 31.9 us -> 23 us
  local copies, waits for them, and re-layouts: 8.57 us -> 3.62 us
  other arithmetic: 2.3 us -> 1.06 us
  waiting for transfers between devices: 29 us -> 28 us
    pallas_call x1, Pallas kernels: 18.3 us -> 11.4 us  [on_device(): pl.pallas_call(functools.partial(conv_kernel, side), out_shape=(jax.Shape...]
    pallas_call x1, Pallas kernels: 8.52 us -> 2.2 us  [on_device(): pl.pallas_call(functools.partial(unpack_kernel, side, slots), out_shape=j...]
    pallas_call x0 -> x4, Pallas kernels: none -> 5.8 us  [the longest x1 2.24 us: on_device(): pl.pallas_call(restore_kernel, out_shape=(jax.ShapeDtypeStruct((chans, ro...]
    dynamic_slice x2 -> x0, local copies, waits for them, and re-layouts: 2.4 us -> none  [the longest x1 1.35 us: on_device(): send_main = lax.dynamic_slice_in_dim(features, (1 - core) * rows, rows, 1)]
    select_n x3 -> x0, other arithmetic: 2.24 us -> none  [the longest x1 2.08 us: on_device(): jnp.where(core == 0, jnp.concatenate([e_own, e_recv], axis=1), jnp.concat...]
    all_to_all x1, waiting for transfers between devices: 21.7 us -> 20 us  [to_peers(): x = lax.all_to_all(x, 'tiles', split_axis=0, concat_axis=0, tiled=True)]
    pallas_call x1, Pallas kernels: 5.08 us -> 3.6 us  [on_device(): pl.pallas_call(functools.partial(pack_kernel, side, slots), out_shape=jax...]
    broadcast_in_dim x7 -> x0, local copies, waits for them, and re-layouts: 1.11 us -> none  [the longest x1 0.73 us: on_device(): parent_owner[:, None]]
  transfers between devices with their start and end apart: 8 -> 7, of which waited for: 5 -> 5; matrix products, arithmetic and copies ran while one was open for 8% -> 2% of each run, Pallas kernels for 0% -> 8%
where the time goes in v2:
time: 69.5 us; the launch traced here: 69.1 us
  waiting for transfers between devices  28 us (40%)
  Pallas kernels  23 us (33%)
  starting transfers between devices  12.7 us (18%)
  local copies, waits for them, and re-layouts  3.62 us (5%)
  other arithmetic  1.06 us (2%)
  between operations  0.75 us (1%)
    all_to_all x1, waiting for transfers between devices, to_peers(): x = lax.all_to_all(x, 'tiles', split_axis=0, concat_axis=0, tiled=True)  20 us
    pallas_call x1, Pallas kernels, on_device(): pl.pallas_call(functools.partial(conv_kernel, side), out_shape=(jax.Shape...  11.4 us
    all_to_all x1, starting transfers between devices, to_peers(): x = lax.all_to_all(x, 'tiles', split_axis=0, concat_axis=0, tiled=True)  5.91 us
    unnamed x14, local copies, waits for them, and re-layouts  3.62 us
    pallas_call x1, Pallas kernels, on_device(): pl.pallas_call(functools.partial(pack_kernel, side, slots), out_shape=jax...  3.6 us
    ppermute x1, starting transfers between devices, on_device(): out_own = lax.ppermute(edge_one, ('tiles', 'chan'), down_up)  3.4 us
    ppermute x1, waiting for transfers between devices, on_device(): out_oth = lax.ppermute(edge_two, ('tiles', 'chan'), cross)  2.83 us
    ppermute x1, waiting for transfers between devices, on_device(): e_recv = lax.ppermute(e_oth, 'chan', swap)  2.65 us
  transfers between devices with their start and end apart: 7, of which 5 were waited for; matrix products, arithmetic and copies ran while one was open for 2% of the time, Pallas kernels for 8%

profile of v2, /device:TPU:8, one launch (start us, length us, event | category | flops | bytes accessed | tf_op | source)
XLA Modules:
  0.0 69.1 jit_solution(13930006166303858308)
XLA Ops:
  0.6 0.1 collective-permute-start
  0.7 1.0 %pad_maximum_fusion.wown_ref = bf16[22,32,64]{2,1,0:T(8,128)(2,1)S(1)} fusion(bf16[4,32,64]{2,1,0:T(8,128)(2,1)} %bitcast.7, bf16[9,32,64]{2,1,0:T(8,128)(2,1)} %param.10, bf16[9,32,64]{2,1,0:T(8,128)(2,1)} %param.9), kind=kLoop, calls=%fused_computation | loop fusion | flops 90112 | bytes 180224 | tf_op jit(solution)/shard_map/concatenate | solution.py:452
  1.7 0.6 collective-permute-start.3
  2.3 0.1 pad_add_fusion.place_ref
  2.3 1.6 %copy-done = bf16[32,128,256]{2,1,0:T(8,128)(2,1)S(1)} copy-done((bf16[32,128,256]{2,1,0:T(8,128)(2,1)S(1)}, bf16[32,128,256]{2,1,0:T(8,128)(2,1)}, u32[]{:S(2)}) %copy-start) | copy-done | bytes 2097176
  3.9 0.7 %copy-done.4 = s32[16,32]{1,0:T(8,128)S(1)} copy-done((s32[16,32]{1,0:T(8,128)S(1)}, s32[16,32]{1,0:T(8,128)}, u32[]{:S(2)}) %copy-start.4) | copy-done | bytes 2072
  4.6 1.2 %edges.1 = (bf16[128,256]{1,0:T(8,128)(2,1)S(1)}, bf16[128,256]{1,0:T(8,128)(2,1)S(1)}) custom-call(s32[2]{0:T(128)S(1)} %pad_add_fusion.place_ref, bf16[32,128,256]{2,1,0:T(8,128)(2,1)S(1)} %copy-done, s32[16,32]{1,0:T(8,128)S(1)} %copy-done.4), custom_call_target="tpu_custom_call" | custom-call | tf_op jit(solution)/shard_map/edges/pallas_call | solution.py:454
  5.8 3.4 %collective-permute-start.1 = (bf16[128,256]{1,0:T(8,128)(2,1)S(1)}, bf16[128,256]{1,0:T(8,128)(2,1)S(1)}, u32[]{:S(2)}, u32[]{:S(2)}) collective-permute-start(bf16[128,256]{1,0:T(8,128)(2,1)S(1)} %get-tuple-element.14), channel_id=1, source_target_pairs={{0,2},{2,4},{4,6},{6,8},{8,10},{10,12},{12,14},{14,16},{16,18},{18... | collective-permute-start | bytes 196616 | tf_op jit(solution)/shard_map/ppermute | solution.py:470
  9.2 2.6 %collective-permute-start.2 = (bf16[128,256]{1,0:T(8,128)(2,1)S(1)}, bf16[128,256]{1,0:T(8,128)(2,1)S(1)}, u32[]{:S(2)}, u32[]{:S(2)}) collective-permute-start(bf16[128,256]{1,0:T(8,128)(2,1)S(1)} %get-tuple-element.15), channel_id=1, source_target_pairs={{1,2},{3,4},{5,6},{7,8},{9,10},{11,12},{13,14},{15,16},{17,18},{19... | collective-permute-start | bytes 196616 | tf_op jit(solution)/shard_map/ppermute | solution.py:471
  11.9 0.9 %weights.1 = (bf16[192,192]{1,0:T(8,128)(2,1)S(1)}, bf16[192,192]{1,0:T(8,128)(2,1)S(1)}, bf16[64,256]{1,0:T(8,128)(2,1)S(1)}) custom-call(s32[2]{0:T(128)S(1)} %pad_add_fusion.place_ref, bf16[22,32,64]{2,1,0:T(8,128)(2,1)S(1)} %pad_maximum_fusion.wown_ref, bf16[22,32,64]{2,1,0:T(8,128)(2,1)S(1)} %collective-permute-done.3.woth_ref), custom_call_target="tpu_custom_call" | custom-call | tf_op jit(solution)/shard_map/weights/pallas_call | solution.py:472
  12.8 1.0 %collective-permute-done.1.out_own_ref = bf16[128,256]{1,0:T(8,128)(2,1)S(1)} collective-permute-done((bf16[128,256]{1,0:T(8,128)(2,1)S(1)}, bf16[128,256]{1,0:T(8,128)(2,1)S(1)}, u32[]{:S(2)}, u32[]{:S(2)}) %collective-permute-start.1) | collective-permute-done | bytes 65568 | tf_op jit(solution)/shard_map/ppermute | solution.py:470
  13.8 2.8 %collective-permute-done.2.out_oth_ref = bf16[128,256]{1,0:T(8,128)(2,1)S(1)} collective-permute-done((bf16[128,256]{1,0:T(8,128)(2,1)S(1)}, bf16[128,256]{1,0:T(8,128)(2,1)S(1)}, u32[]{:S(2)}, u32[]{:S(2)}) %collective-permute-start.2) | collective-permute-done | bytes 65568 | tf_op jit(solution)/shard_map/ppermute | solution.py:471
  16.6 0.0 copy-start.6
  16.6 11.4 %conv.1 = (bf16[64,64,256]{2,1,0:T(8,128)(2,1)S(1)}, bf16[256,512]{1,0:T(8,128)(2,1)S(1)}, bf16[256,512]{1,0:T(8,128)(2,1)S(1)}) custom-call(s32[2]{0:T(128)S(1)} %pad_add_fusion.place_ref, bf16[32,128,256]{2,1,0:T(8,128)(2,1)S(1)} %copy-done.1, bf16[32,128,256]{2,1,0:T(8,128)(2,1)S(1)} %collective-permute-done.oth_hbm, ...), custom_call_target="tpu_custom_call" | custom-call | tf_op jit(solution)/shard_map/conv/pallas_call | solution.py:486
  28.1 1.3 %copy-done.2 = bf16[64,64,256]{2,1,0:T(8,128)(2,1)} copy-done((bf16[64,64,256]{2,1,0:T(8,128)(2,1)}, bf16[64,64,256]{2,1,0:T(8,128)(2,1)S(1)}, u32[]{:S(2)}) %copy-start.2) | copy-done | bytes 2097176
  29.4 1.5 %collective-permute-done.4.mrecv_ref = bf16[256,512]{1,0:T(8,128)(2,1)S(1)} collective-permute-done((bf16[256,512]{1,0:T(8,128)(2,1)S(1)}, bf16[256,512]{1,0:T(8,128)(2,1)S(1)}, u32[]{:S(2)}, u32[]{:S(2)}) %collective-permute-start.4) | collective-permute-done | bytes 262176 | tf_op jit(solution)/shard_map/ppermute | solution.py:510
  30.9 3.6 %pack.1 = bf16[16,264,128]{2,1,0:T(8,128)(2,1)} custom-call(s32[2]{0:T(128)S(1)} %pad_add_fusion.place_ref, s32[1,128]{1,0:T(1,128)S(1)} %bitcast.5, bf16[256,512]{1,0:T(8,128)(2,1)S(1)} %get-tuple-element.20.mown_ref, bf16[256,512]{1,0:T(8,128)(2,1)S(1)} %collective-permute-done.4.mrecv_ref), custom_call_target="tpu_custom_call" | custom-call | tf_op jit(solution)/shard_map/pack/pallas_call | solution.py:512
  34.5 5.9 %all-to-all-start = ((bf16[16,264,128]{2,1,0:T(8,128)(2,1)}), bf16[16,264,128]{2,1,0:T(8,128)(2,1)S(1)}, u32[]{:S(2)}, u32[]{:S(2)}) async-start(bf16[16,264,128]{2,1,0:T(8,128)(2,1)} %pack.1), calls=%async_computation | async-start | bytes 2162688 | tf_op jit(solution)/shard_map/all_to_all | solution.py:526
  40.4 2.2 %restore.1 = (bf16[32,128,256]{2,1,0:T(8,128)(2,1)}, bf16[32,64,256]{2,1,0:T(8,128)(2,1)S(1)}) custom-call(s32[2]{0:T(128)S(1)} %pad_add_fusion.place_ref, bf16[64,64,256]{2,1,0:T(8,128)(2,1)S(1)} %copy-done.3), custom_call_target="tpu_custom_call" | custom-call | tf_op jit(solution)/shard_map/restore/pallas_call | solution.py:534
  42.7 0.1 collective-permute-start.5
  42.8 2.6 %collective-permute-done.5.recv_ref = bf16[32,64,256]{2,1,0:T(8,128)(2,1)S(1)} collective-permute-done((bf16[32,64,256]{2,1,0:T(8,128)(2,1)S(1)}, bf16[32,64,256]{2,1,0:T(8,128)(2,1)S(1)}, u32[]{:S(2)}, u32[]{:S(2)}) %collective-permute-start.5) | collective-permute-done | bytes 1048608 | tf_op jit(solution)/shard_map/ppermute | solution.py:546
  45.4 1.5 %fill.1 = bf16[32,128,256]{2,1,0:T(8,128)(2,1)} custom-call(s32[2]{0:T(128)S(1)} %pad_add_fusion.place_ref, bf16[32,64,256]{2,1,0:T(8,128)(2,1)S(1)} %collective-permute-done.5.recv_ref, bf16[32,128,256]{2,1,0:T(8,128)(2,1)} %get-tuple-element.24.held_hbm), custom_call_target="tpu_custom_call", output_to_operand_aliasing={{}: (2, {})} | custom-call | tf_op jit(solution)/shard_map/fill/pallas_call | solution.py:547
  46.9 20.0 %all-to-all-done.got_ref = bf16[16,264,128]{2,1,0:T(8,128)(2,1)S(1)} async-done(((bf16[16,264,128]{2,1,0:T(8,128)(2,1)}), bf16[16,264,128]{2,1,0:T(8,128)(2,1)S(1)}, u32[]{:S(2)}, u32[]{:S(2)}) %all-to-all-start) | async-done | bytes 1081376 | tf_op jit(solution)/shard_map/all_to_all | solution.py:526
  66.9 2.2 %unpack.1 = bf16[32,64,192]{2,1,0:T(8,128)(2,1)} custom-call(bf16[16,264,128]{2,1,0:T(8,128)(2,1)S(1)} %all-to-all-done.got_ref), custom_call_target="tpu_custom_call" | custom-call | tf_op jit(solution)/shard_map/unpack/pallas_call | solution.py:558
  (13 shorter events, 0.0 us)
Async XLA Ops:
  0.6 16.0 %copy-start.5 = (s32[16,32]{1,0:T(8,128)S(1)}, s32[16,32]{1,0:T(8,128)}, u32[]{:S(2)}) copy-start(s32[16,32]{1,0:T(8,128)} %valid_ref.3) | copy-start | bytes 6148
  0.6 16.0 %collective-permute-start = (bf16[32,128,256]{2,1,0:T(8,128)(2,1)}, bf16[32,128,256]{2,1,0:T(8,128)(2,1)S(1)}, u32[]{:S(2)}, u32[]{:S(2)}) collective-permute-start(bf16[32,128,256]{2,1,0:T(8,128)(2,1)} %own_hbm.1), channel_id=1, source_target_pairs={{0,1},{1,0},{2,3},{3,2},{4,5},{5,4},{6,7},{7,6},{8,9},{9,8},{10,11... | collective-permute-start | bytes 6291464 | tf_op jit(solution)/shard_map/ppermute | solution.py:451
  1.7 10.2 %collective-permute-start.3 = (bf16[22,32,64]{2,1,0:T(8,128)(2,1)S(1)}, bf16[22,32,64]{2,1,0:T(8,128)(2,1)S(1)}, u32[]{:S(2)}, u32[]{:S(2)}) collective-permute-start(bf16[22,32,64]{2,1,0:T(8,128)(2,1)S(1)} %pad_maximum_fusion.wown_ref), channel_id=1, source_target_pairs={{0,1},{1,0},{2,3},{3,2},{4,5},{5,4},{6,7},{7,6},{8,9},{9,8},{10,11... | collective-permute-start | bytes 270344 | tf_op jit(solution)/shard_map/ppermute | solution.py:453
  2.3 1.6 %copy-start = (bf16[32,128,256]{2,1,0:T(8,128)(2,1)S(1)}, bf16[32,128,256]{2,1,0:T(8,128)(2,1)}, u32[]{:S(2)}) copy-start(bf16[32,128,256]{2,1,0:T(8,128)(2,1)} %own_hbm.1) | copy-start | bytes 6291460
  3.9 0.7 %copy-start.4 = (s32[16,32]{1,0:T(8,128)S(1)}, s32[16,32]{1,0:T(8,128)}, u32[]{:S(2)}) copy-start(s32[16,32]{1,0:T(8,128)} %valid_ref.3) | copy-start | bytes 6148
  4.6 12.0 %copy-start.1 = (bf16[32,128,256]{2,1,0:T(8,128)(2,1)S(1)}, bf16[32,128,256]{2,1,0:T(8,128)(2,1)}, u32[]{:S(2)}) copy-start(bf16[32,128,256]{2,1,0:T(8,128)(2,1)} %own_hbm.1) | copy-start | bytes 6291460
  5.8 8.0 %collective-permute-start.1 = (bf16[128,256]{1,0:T(8,128)(2,1)S(1)}, bf16[128,256]{1,0:T(8,128)(2,1)S(1)}, u32[]{:S(2)}, u32[]{:S(2)}) collective-permute-start(bf16[128,256]{1,0:T(8,128)(2,1)S(1)} %get-tuple-element.14), channel_id=1, source_target_pairs={{0,2},{2,4},{4,6},{6,8},{8,10},{10,12},{12,14},{14,16},{16,18},{18... | collective-permute-start | bytes 196616 | tf_op jit(solution)/shard_map/ppermute | solution.py:470
  9.2 7.4 %collective-permute-start.2 = (bf16[128,256]{1,0:T(8,128)(2,1)S(1)}, bf16[128,256]{1,0:T(8,128)(2,1)S(1)}, u32[]{:S(2)}, u32[]{:S(2)}) collective-permute-start(bf16[128,256]{1,0:T(8,128)(2,1)S(1)} %get-tuple-element.15), channel_id=1, source_target_pairs={{1,2},{3,4},{5,6},{7,8},{9,10},{11,12},{13,14},{15,16},{17,18},{19... | collective-permute-start | bytes 196616 | tf_op jit(solution)/shard_map/ppermute | solution.py:471
  16.6 14.3 %copy-start.6 = (s32[128]{0:T(128)S(1)}, s32[128]{0:T(128)}, u32[]{:S(2)}) copy-start(s32[128]{0:T(128)} %param.8) | copy-start | bytes 1540
  28.1 1.3 %copy-start.2 = (bf16[64,64,256]{2,1,0:T(8,128)(2,1)}, bf16[64,64,256]{2,1,0:T(8,128)(2,1)S(1)}, u32[]{:S(2)}) copy-start(bf16[64,64,256]{2,1,0:T(8,128)(2,1)S(1)} %get-tuple-element.22.es_ref) | copy-start | bytes 6291460
  29.4 11.1 %copy-start.3 = (bf16[64,64,256]{2,1,0:T(8,128)(2,1)S(1)}, bf16[64,64,256]{2,1,0:T(8,128)(2,1)}, u32[]{:S(2)}) copy-start(bf16[64,64,256]{2,1,0:T(8,128)(2,1)} %copy-done.2) | copy-start | bytes 6291460
  29.4 1.5 %collective-permute-start.4 = (bf16[256,512]{1,0:T(8,128)(2,1)S(1)}, bf16[256,512]{1,0:T(8,128)(2,1)S(1)}, u32[]{:S(2)}, u32[]{:S(2)}) collective-permute-start(bf16[256,512]{1,0:T(8,128)(2,1)S(1)} %get-tuple-element.21), channel_id=1, source_target_pairs={{0,1},{1,0},{2,3},{3,2},{4,5},{5,4},{6,7},{7,6},{8,9},{9,8},{10,11... | collective-permute-start | bytes 786440 | tf_op jit(solution)/shard_map/ppermute | solution.py:510
  34.5 32.4 %all-to-all-start = ((bf16[16,264,128]{2,1,0:T(8,128)(2,1)}), bf16[16,264,128]{2,1,0:T(8,128)(2,1)S(1)}, u32[]{:S(2)}, u32[]{:S(2)}) async-start(bf16[16,264,128]{2,1,0:T(8,128)(2,1)} %pack.1), calls=%async_computation | async-start | bytes 2162688 | tf_op jit(solution)/shard_map/all_to_all | solution.py:526
  42.7 2.7 %collective-permute-start.5 = (bf16[32,64,256]{2,1,0:T(8,128)(2,1)S(1)}, bf16[32,64,256]{2,1,0:T(8,128)(2,1)S(1)}, u32[]{:S(2)}, u32[]{:S(2)}) collective-permute-start(bf16[32,64,256]{2,1,0:T(8,128)(2,1)S(1)} %get-tuple-element.23), channel_id=1, source_target_pairs={{0,1},{1,0},{2,3},{3,2},{4,5},{5,4},{6,7},{7,6},{8,9},{9,8},{10,11... | collective-permute-start | bytes 3145736 | tf_op jit(solution)/shard_map/ppermute | solution.py:546

commit v3 on v2

v3 whole, which is shorter than its diff:
```python
import functools

import jax
import jax.numpy as jnp
from jax import lax
from jax.experimental import pallas as pl
from jax.experimental.pallas import tpu as pltpu
from jax.sharding import PartitionSpec as P

BF = jnp.bfloat16
F32 = jnp.float32
HALO = 4
BLK = 16


def iota(shape, dim):
    return lax.broadcasted_iota(jnp.int32, shape, dim)


def div(x, n):
    return x >> (n.bit_length() - 1) if n & (n - 1) == 0 else lax.div(x, jnp.int32(n))


def mod(x, n):
    return x & (n - 1) if n & (n - 1) == 0 else lax.rem(x, jnp.int32(n))


def ones_where(cond):
    return jnp.where(cond, 1.0, 0.0).astype(BF)


def mm(a, b):
    return jnp.dot(a, b, preferred_element_type=F32)


def mm_nt(a, b):
    return lax.dot_general(a, b, (((1,), (1,)), ((), ())), preferred_element_type=F32)


def swap_matrix(outer, inner):
    n = outer * inner
    row, col = iota((n, n), 0), iota((n, n), 1)
    return ones_where((mod(row, inner) == div(col, outer)) & (div(row, inner) == mod(col, outer)))


def shifted(x, amount):
    lanes = 128
    parts = [x[:, at : at + lanes] for at in range(0, x.shape[1], lanes)]
    turned = [pltpu.roll(p, amount % lanes, 1) for p in parts]
    lane = iota(parts[0].shape, 1)
    zero = jnp.zeros_like(parts[0])
    outs = []
    for n in range(len(parts)):
        if amount > 0:
            edge = turned[n - 1] if n else zero
            outs.append(jnp.where(lane < amount, edge, turned[n]))
        else:
            edge = turned[n + 1] if n + 1 < len(parts) else zero
            outs.append(jnp.where(lane >= lanes + amount, edge, turned[n]))
    return jnp.concatenate(outs, axis=1)


def widen_matrix(tiles_c, cols, side):
    return ones_where(div(iota((tiles_c, cols), 1), side) == iota((tiles_c, cols), 0))


def as_bf(x):
    return x.astype(F32).astype(BF)


def edges_kernel(
    side, place_ref, head_ref, tail_ref, valid_ref, wa_ref, wb_ref, wc_ref, send_ref, keep_ref
):
    core = place_ref[0]
    chans, _, cols = head_ref.shape
    flat = chans * HALO
    lanes = send_ref.shape[1]
    at = flat * cols // lanes
    for ref in (wa_ref, wb_ref, wc_ref):
        taps, outs, ins = ref.shape
        body = ref[...].reshape(taps * outs, ins)
        send_ref[at : at + taps * outs, :] = jnp.concatenate(
            [body, jnp.zeros((taps * outs, lanes - ins), BF)], axis=1
        )
        at += taps * outs
    tiles_r, tiles_c = valid_ref.shape
    masks = mm(as_bf(valid_ref[...]), widen_matrix(tiles_c, cols, side))
    row, col = iota((flat, chans * BLK), 0), iota((flat, chans * BLK), 1)
    same = div(row, HALO) == div(col, BLK)
    spot = mod(iota((flat, cols), 0), HALO)
    made = []
    for n, ref in enumerate((head_ref, tail_ref)):
        if n == 0:
            hit = same & (mod(row, HALO) == mod(col, BLK)) & (mod(row, HALO) < HALO - 1)
            flag, line = spot == HALO - 1, masks[0:1]
        else:
            hit = same & (mod(row, HALO) + BLK - HALO == mod(col, BLK)) & (mod(row, HALO) > 0)
            flag, line = spot == 0, masks[tiles_r - 1 : tiles_r]
        take = ones_where(hit)
        body = mm(take, ref[...].reshape(chans * BLK, cols))
        made.append(jnp.where(flag, jnp.broadcast_to(line, (flat, cols)), body).astype(BF))
    low = core == 0
    send = jnp.where(low, made[1], made[0])
    keep = jnp.where(low, made[0], made[1])
    for n in range(cols // lanes):
        send_ref[n * flat : (n + 1) * flat, :] = send[:, n * lanes : (n + 1) * lanes]
        keep_ref[n * flat : (n + 1) * flat, :] = keep[:, n * lanes : (n + 1) * lanes]


def weights_kernel(at, chans, place_ref, own_ref, oth_ref, w1_ref, w2_ref, wm_ref):
    core = place_ref[0]
    allc = 2 * chans

    def tap(k):
        return [ref[at + k * chans : at + (k + 1) * chans, 0:allc] for ref in (own_ref, oth_ref)]

    for dst, base in ((w1_ref, 0), (w2_ref, 9)):
        total = None
        for b in range(3):
            tall = jnp.concatenate(sum([tap(base + 3 * a + b) for a in range(3)], []), axis=0)
            src, pos = iota((allc, 3 * allc), 0), iota((allc, 3 * allc), 1)
            place = ones_where(pos == b * allc + mod(src + chans * core, allc))
            part = mm(tall, place)
            total = part if total is None else total + part
        dst[...] = total.astype(BF)
    tall = jnp.concatenate(
        sum([tap(18 + 2 * a + b) for b in range(2) for a in range(2)], []), axis=0
    )
    order = ones_where(iota((allc, allc), 1) == mod(iota((allc, allc), 0) + chans * core, allc))
    wm_ref[...] = mm_nt(order, tall).astype(BF)


def conv_kernel(
    side,
    place_ref,
    own_hbm,
    oth_hbm,
    outer_ref,
    valid_ref,
    w1,
    w2,
    wm,
    es_hbm,
    mown_ref,
    moth_ref,
    feat,
    xs,
    hs,
    es_ref,
    mask,
    pa_ref,
    pb_ref,
    in_sems,
    out_sem,
):
    core = place_ref[0]
    rows, allc, cols = es_ref.shape
    chans = allc // 2
    main = rows // BLK
    copies = []
    for m in range(main + 1):
        at = rows - BLK * core if m == main else rows * core + BLK * m
        for n, ref in enumerate((own_hbm, oth_hbm)):
            copy = pltpu.make_async_copy(
                ref.at[:, pl.ds(pl.multiple_of(at, BLK), BLK), :], feat.at[n, m], in_sems.at[n, m]
            )
            copy.start()
            copies.append(copy)
    lanes = outer_ref.shape[1]

    tiles_r, tiles_c = valid_ref.shape
    mask[pl.ds(side, tiles_r), :] = mm(as_bf(valid_ref[...]), widen_matrix(tiles_c, cols, side))

    def put(dst, index, x, amount):
        dst[index, 0:allc, :] = shifted(x, amount).astype(BF)
        dst[index, allc : 2 * allc, :] = x.astype(BF)
        dst[index, 2 * allc : 3 * allc, :] = shifted(x, -amount).astype(BF)

    first_row = 5
    turn4 = swap_matrix(HALO, chans)
    flat = HALO * chans
    pieces = [outer_ref[k * flat : (k + 1) * flat, :] for k in range(2 * cols // lanes)]
    oth, own = [
        mm(turn4, jnp.concatenate(pieces[n * cols // lanes : (n + 1) * cols // lanes], axis=1))
        for n in range(2)
    ]
    start = jnp.where(core == 0, first_row - HALO, first_row + rows)
    for r in range(HALO):
        at = slice(r * chans, (r + 1) * chans)
        put(xs, start + r, jnp.concatenate([own[at], oth[at]], axis=0), 1)
    top = own[0:1, :]
    bottom = own[(HALO - 1) * chans : (HALO - 1) * chans + 1, :]

    @pl.when(core == 0)
    def _():
        mask[pl.ds(side - 1, 1), :] = top

    @pl.when(core == 1)
    def _():
        mask[pl.ds(side + tiles_r, 1), :] = bottom

    xs[0] = jnp.zeros(xs.shape[1:], BF)
    turn = swap_matrix(BLK, BLK)
    few = HALO * BLK
    row, col = iota((few, BLK * BLK), 0), iota((few, BLK * BLK), 1)
    turn_mid = ones_where(
        (mod(row, BLK) == div(col, BLK)) & (div(row, BLK) + (BLK - HALO) * core == mod(col, BLK))
    )
    mid_start = jnp.where(core == 0, first_row + rows, first_row - HALO)
    for m in range(main + 1):
        for copy in copies[2 * m : 2 * m + 2]:
            copy.wait()
        parts = []
        for n in range(2):
            for ch in range(0, chans, BLK):
                block = feat[n, m, ch : ch + BLK].reshape(BLK * BLK, cols)
                parts.append(mm(turn_mid if m == main else turn, block))
        at = mid_start if m == main else first_row + m * BLK
        for r in range(HALO if m == main else BLK):
            x = jnp.concatenate([p[r * BLK : (r + 1) * BLK] for p in parts], axis=0)
            put(xs, at + r, x, 1)

    base = side + core * (rows // side)
    total_steps = rows // side + 1
    tiles = 3 if total_steps % 3 == 0 else 1
    group = tiles * side

    def lines(step, ahead):
        return [mask[pl.ds(base + step * tiles + k - 1, 1), :] for k in range(tiles + ahead)]

    pa_ref[...] = jnp.zeros(pa_ref.shape, F32)
    pb_ref[...] = jnp.zeros(pb_ref.shape, F32)

    def first(step, carry):
        pa, pb = pa_ref[0], pb_ref[0]
        flag = lines(step, 1)
        for j in range(group):
            q = step * group + j
            y = mm(w1[...], xs[q])
            total = pa + y[2 * allc :]
            pa = pb + y[allc : 2 * allc]
            pb = y[:allc]
            h = jnp.maximum(total * flag[(j + 2) // side], 0.0)
            put(hs, q, h.astype(BF), 2)
        pa_ref[0] = pa
        pb_ref[0] = pb
        return carry

    lax.fori_loop(0, total_steps // tiles, first, 0)

    pa_ref[0] = jnp.zeros((allc, cols), F32)
    pb_ref[0] = jnp.zeros((allc, cols), F32)

    def second(step, carry):
        pa, pb = [pa_ref[0], pa_ref[1]], [pb_ref[0], pb_ref[1]]
        flag = lines(step, 0)
        for j in range(group):
            q = step * group + j
            i = j % 2
            z = mm(w2[...], hs[q])
            total = pa[i] + z[2 * allc :]
            pa[i] = pb[i] + z[allc : 2 * allc]
            pb[i] = z[:allc]
            x = xs[jnp.maximum(q - 3, 0), allc : 2 * allc, :].astype(F32)
            es_ref[jnp.maximum(q - side, 0)] = (flag[j // side] * (x + total)).astype(BF)
        for i in range(2):
            pa_ref[i] = pa[i]
            pb_ref[i] = pb[i]
        return carry

    lax.fori_loop(0, total_steps // tiles, second, 0)

    out = pltpu.make_async_copy(es_ref, es_hbm, out_sem)
    out.start()

    half = cols // 2
    wide = half // side
    lane = iota((cols, cols), 1)
    spot = mod(lane, half)
    want = 2 * (mod(spot, wide) * side + div(spot, wide)) + div(lane, half)
    pick = ones_where(iota((cols, cols), 0) == want)
    picked = hs.reshape(hs.shape[0] * hs.shape[1], cols)
    for tile in range(rows // side):
        tall = es_ref[tile * side : (tile + 1) * side].reshape(side * allc, cols)
        picked[tile * side * allc : (tile + 1) * side * allc, :] = mm(tall, pick).astype(BF)
    for tile in range(rows // side):
        g = tile // 2 + core * (rows // (2 * side))
        for k in range(0, side // 2, 2):
            pairs = []
            for n in range(2):
                at = (tile * side + 2 * (k + n)) * allc
                sp = picked[at : at + 2 * allc, :]
                pairs.append(jnp.concatenate([sp[:, :half], sp[:, half:]], axis=0))
            both = mm(wm[...], jnp.concatenate(pairs, axis=1))
            for n in range(2):
                u = (side // 2) * (tile % 2) + k + n
                piece = pltpu.roll(both[:, n * half : (n + 1) * half], g * wide, 1).astype(BF)
                mown_ref[tile // 2, u * chans : (u + 1) * chans, :] = piece[:chans]
                moth_ref[tile // 2, u * chans : (u + 1) * chans, :] = piece[chans:]
    out.wait()


def restore_kernel(place_ref, es_ref, after_hbm, enh_hbm, eoth_ref, own, sem):
    core = place_ref[0]
    rows, allc, cols = es_ref.shape
    chans = allc // 2
    turn = swap_matrix(BLK, BLK)
    for c0 in list(range(chans, allc, BLK)) + list(range(0, chans, BLK)):
        ref = own if c0 < chans else eoth_ref
        ch = c0 % chans
        for at in range(0, rows, BLK):
            block = es_ref[at : at + BLK, c0 : c0 + BLK, :].reshape(BLK * BLK, cols)
            ref[ch : ch + BLK, at : at + BLK, :] = mm(turn, block).astype(BF).reshape(BLK, BLK, cols)
    copy = pltpu.make_async_copy(
        own, enh_hbm.at[:, pl.ds(pl.multiple_of(core * rows, rows), rows), :], sem
    )
    copy.start()
    copy.wait()


def fill_kernel(place_ref, recv_ref, held_hbm, enh_hbm, sem):
    core = place_ref[0]
    rows = recv_ref.shape[1]
    copy = pltpu.make_async_copy(
        recv_ref, enh_hbm.at[:, pl.ds(pl.multiple_of((1 - core) * rows, rows), rows), :], sem
    )
    copy.start()
    copy.wait()


def deal(now, width):
    n = len(now)
    group = div(iota(now[0].shape, 1), width)
    bit = 1
    while bit < n:
        odd = group & bit != 0
        now = [jnp.where(odd, now[(j + bit) % n], now[j]) for j in range(n)]
        bit *= 2
    return now


def pack_kernel(
    side, slots, place_ref, owner_ref, mown_ref, mrecv_ref, out_ref, arr, lhs, mid, code_ref
):
    core, tile = place_ref[0], place_ref[1]
    count = owner_ref.shape[1]
    mine, rows, lanes = mown_ref.shape
    blocks, all_rows, _ = out_ref.shape
    per = side * slots
    wide = lanes // side
    for k in range(mine):
        arr[core * mine + k] = mown_ref[k]
        arr[(1 - core) * mine + k] = mrecv_ref[k]
    line = jnp.broadcast_to(owner_ref[...].astype(F32), (lanes, count))
    owner = jnp.transpose(line).astype(jnp.int32)
    is_owner = owner == iota((count, lanes), 1)
    marks = ones_where(is_owner)
    lower = ones_where(iota((count, count), 0) > iota((count, count), 1))
    earlier = mm(lower, marks)
    within = jnp.sum(jnp.where(is_owner, earlier, 0.0), axis=1, keepdims=True).astype(jnp.int32)
    if per == lanes:
        code = (owner * slots + within).astype(F32).astype(BF)
        code_ref[0:count, :] = code
        code_ref[count : 2 * count, :] = code

        def by_column(step, carry):
            at = pl.ds(pl.multiple_of(step * BLK, BLK), BLK)
            done = deal([arr[g, at, :] for g in range(side)], wide)
            for j in range(side):
                lhs[-j % side, at, :] = done[j]
            return carry

        lax.fori_loop(0, rows // BLK, by_column, 0, unroll=4)
        halves = blocks // side
        lane = iota((1, halves * lanes), 1)
        block, group, slot = div(lane, lanes), div(mod(lane, lanes), wide), mod(lane, wide)
        for i in range(side):
            v = lax.rem(i + side - lax.rem(tile, side), side)
            at = pl.multiple_of(count - wide * v, wide)
            codes = code_ref[pl.ds(at, count), :]
            want = (block * side + mod(group - i + side, side)) * slots + slot
            want = jnp.broadcast_to(want.astype(F32).astype(BF), (count, halves * lanes))
            same = jnp.concatenate([codes] * halves, axis=1) == want
            take = jnp.where(same, jnp.ones_like(want), jnp.zeros_like(want))
            got = mm(lhs[v], take).astype(BF)
            for h in range(halves):
                mid[h * side + i] = got[:, h * lanes : (h + 1) * lanes]
        for h in range(halves):

            def by_owner(step, carry, h=h):
                at = pl.ds(pl.multiple_of(step * BLK, BLK), BLK)
                done = deal([mid[h * side + i, at, :] for i in range(side)], wide)
                for j in range(side):
                    out_ref[h * side + -j % side, at, :] = done[j]
                return carry

            lax.fori_loop(0, rows // BLK, by_owner, 0, unroll=4)
        tally = mm(jnp.ones((all_rows - rows, count), BF), marks)
        for d in range(blocks):
            out_ref[d, rows:all_rows, :] = jnp.broadcast_to(
                tally[:, d : d + 1], (all_rows - rows, lanes)
            ).astype(BF)
    else:
        code = owner * per + within
        lane = iota((wide, lanes), 1)
        for g in range(2 * mine):
            for x in range(side):
                at = (g * side + x) * wide
                code_ref[at : at + wide, :] = (
                    code[g * wide : (g + 1) * wide] + (x - g) % side * slots
                )
        data = jnp.concatenate([arr[g] for g in range(2 * mine)], axis=1)
        lane = iota((count * side, lanes), 1)
        for step in range(0, blocks, 2):
            codes = code_ref[...]
            spots = [ones_where(codes == lane + at * lanes) for at in (step, step + 1)]
            total = mm(data, jnp.concatenate(spots, axis=1)).astype(BF)
            for n in range(2):
                at = step + n
                out_ref[at, 0:rows, :] = total[:, n * lanes : (n + 1) * lanes]
                goal = div(iota((count, lanes), 1) + at * lanes, per)
                tally = mm(jnp.ones((all_rows - rows, count), BF), ones_where(owner == goal))
                out_ref[at, rows:all_rows, :] = tally.astype(BF)


def targets(tallies, lanes, group, slots):
    lane0, lane1 = iota((lanes, lanes), 0), iota((lanes, lanes), 1)
    heads = mod(lane0, group) == 0
    before = ones_where(heads & (div(lane0, group) < div(lane1, group)))
    every = ones_where(heads)
    slot = mod(iota((1, lanes), 1), slots).astype(F32)
    running = jnp.zeros((1, lanes), F32)
    outs = []
    for tally in tallies:
        inside, whole = mm(tally, before)[0:1], mm(tally, every)[0:1]
        live = slot < tally.astype(F32)[0:1]
        outs.append(jnp.where(live, running + inside + slot, -1.0))
        running = running + whole
    return outs


def hits(target, room):
    shape = (room, target.shape[1])
    goal = iota(shape, 0).astype(F32).astype(BF)
    same = goal == jnp.broadcast_to(target.astype(BF), shape)
    return jnp.where(same, jnp.ones_like(goal), jnp.zeros_like(goal))


def unpack_kernel(side, slots, place_ref, got_ref, out_ref, picked, data):
    tile = place_ref[1]
    blocks, all_rows, lanes = got_ref.shape
    chans, cells, cap = out_ref.shape
    rows = side * chans
    per = side * slots
    room = picked.shape[2]
    if per == lanes:
        halves = blocks // side
        group = div(iota((all_rows - rows, lanes), 1), slots)
        tallies = []
        for h in range(halves):
            tally = got_ref[h * side, rows:all_rows, :].astype(F32)
            for s in range(1, side):
                other = got_ref[h * side + s, rows:all_rows, :].astype(F32)
                tally = jnp.where(group == s, other, tally)
            tallies.append(tally.astype(BF))
        spots = targets(tallies, lanes, slots, slots)
        for h in range(halves):

            def turn_rows(step, carry, h=h):
                at = pl.ds(pl.multiple_of(step * BLK, BLK), BLK)
                done = deal([got_ref[h * side + s, at, :] for s in range(side)], slots)
                for j in range(side):
                    data[h, j, at, :] = done[j]
                return carry

            lax.fori_loop(0, rows // BLK, turn_rows, 0, unroll=4)
        for j in range(side):
            v = lax.rem(2 * side - j - lax.rem(tile, side), side)
            left = jnp.concatenate([data[h, j] for h in range(halves)], axis=1)
            right = []
            for spot in spots:
                line = jnp.broadcast_to(spot, (side, lanes))
                line = pltpu.roll(line, (side - j) * slots, 1) if j else line
                right.append(hits(line[0:1], room))
            picked[v] = mm_nt(left, jnp.concatenate(right, axis=1)).astype(BF)
    else:
        tallies = [got_ref[b, rows:all_rows, :] for b in range(blocks)]
        spots = [hits(t, room) for t in targets(tallies, lanes, per, slots)]
        spots = jnp.concatenate(spots, axis=1)
        for v in range(side):
            keep = div(mod(iota((rows, lanes), 1), per), slots) == v
            left = jnp.concatenate(
                [jnp.where(keep, got_ref[b, 0:rows, :], jnp.zeros((rows, lanes), BF)) for b in range(blocks)],
                axis=1,
            )
            picked[v] = mm_nt(left, spots).astype(BF)
    two = BLK // side
    n = BLK * BLK
    row, col = iota((n, n), 0), iota((n, n), 1)
    turn = ones_where(
        (div(row, BLK) == mod(col, BLK))
        & (mod(div(row, side), two) == mod(div(col, BLK), two))
        & (mod(row, side) == div(col, BLK * two))
    )
    for u in range(0, side, two):
        for ch in range(0, chans, BLK):
            block = jnp.concatenate(
                [
                    picked[v, (u + w) * chans + ch : (u + w) * chans + ch + BLK, :]
                    for v in range(side)
                    for w in range(two)
                ],
                axis=0,
            )
            done = mm(turn, block).astype(BF).reshape(BLK, BLK, room)
            out_ref[ch : ch + BLK, u * side : (u + two) * side, :] = done[:, :, :cap]


def on_device(features, tile_valid, parent_owner, w_first, w_second, w_merge):
    chans, row_count, col_count = features.shape
    tile_rows, tile_cols = tile_valid.shape
    side = row_count // tile_rows
    parents_dev = parent_owner.shape[0]
    devices = lax.axis_size("tiles")
    slots = 2 * max(1, parents_dev // devices)
    own_cap = 3 * parents_dev // 2
    rows = row_count // 2
    allc = 2 * chans
    lanes = 128
    blocks = devices * slots * side // lanes
    fold = devices // blocks
    core = lax.axis_index("chan")
    place = jnp.stack([core, lax.axis_index("tiles")]).astype(jnp.int32)
    swap = [(0, 1), (1, 0)]
    vmem = pl.BlockSpec(memory_space=pltpu.VMEM)
    smem = pl.BlockSpec(memory_space=pltpu.SMEM)
    hbm = pl.BlockSpec(memory_space=pltpu.HBM)

    def limit(mib):
        return pltpu.CompilerParams(vmem_limit_bytes=mib << 20)

    feat_oth = lax.ppermute(features, "chan", swap)
    w_mergt = jnp.swapaxes(w_merge, 1, 2)
    edge_rows = chans * HALO * col_count // lanes
    tap_rows = (w_first.shape[0] + w_second.shape[0] + w_merge.shape[0]) * chans
    send, keep = pl.pallas_call(
        functools.partial(edges_kernel, side),
        out_shape=(
            jax.ShapeDtypeStruct((edge_rows + tap_rows, lanes), BF),
            jax.ShapeDtypeStruct((edge_rows, lanes), BF),
        ),
        in_specs=[smem] + [vmem] * 6,
        out_specs=(vmem,) * 2,
        compiler_params=limit(6),
        name="edges",
    )(place, features[:, :BLK], features[:, row_count - BLK :], tile_valid, w_first, w_second, w_mergt)
    sent = lax.ppermute(send, "chan", swap)
    cross = [(2 * t + 1, 2 * t + 2) for t in range(devices - 1)]
    cross += [(2 * t, 2 * t - 1) for t in range(1, devices)]
    outer = lax.ppermute(
        jnp.concatenate([keep, sent[:edge_rows]], axis=0), ("tiles", "chan"), cross
    )
    w1, w2, wm = pl.pallas_call(
        functools.partial(weights_kernel, edge_rows, chans),
        out_shape=(
            jax.ShapeDtypeStruct((3 * allc, 3 * allc), BF),
            jax.ShapeDtypeStruct((3 * allc, 3 * allc), BF),
            jax.ShapeDtypeStruct((allc, 4 * allc), BF),
        ),
        in_specs=[smem, vmem, vmem],
        out_specs=(vmem,) * 3,
        compiler_params=limit(6),
        name="weights",
    )(place, send, sent)

    parent_rows = tile_rows // 4
    es, m_own, m_oth = pl.pallas_call(
        functools.partial(conv_kernel, side),
        out_shape=(
            jax.ShapeDtypeStruct((rows, allc, col_count), BF),
            jax.ShapeDtypeStruct((parent_rows, side * chans, col_count // 2), BF),
            jax.ShapeDtypeStruct((parent_rows, side * chans, col_count // 2), BF),
        ),
        in_specs=[smem, hbm, hbm] + [vmem] * 5,
        out_specs=(hbm, vmem, vmem),
        scratch_shapes=[
            pltpu.VMEM((2, rows // BLK + 1, chans, BLK, col_count), BF),
            pltpu.VMEM((rows + 16, 3 * allc, col_count), BF),
            pltpu.VMEM((rows + side, 3 * allc, col_count), BF),
            pltpu.VMEM((rows, allc, col_count), BF),
            pltpu.VMEM((tile_rows + 2 * side, col_count), F32),
            pltpu.VMEM((2, allc, col_count), F32),
            pltpu.VMEM((2, allc, col_count), F32),
            pltpu.SemaphoreType.DMA((2, rows // BLK + 1)),
            pltpu.SemaphoreType.DMA,
        ],
        compiler_params=limit(34),
        name="conv",
    )(place, features, feat_oth, outer, tile_valid, w1, w2, wm)

    m_recv = lax.ppermute(m_oth, "chan", swap)
    all_rows = side * chans + 8
    packed = pl.pallas_call(
        functools.partial(pack_kernel, side, slots),
        out_shape=jax.ShapeDtypeStruct((blocks, all_rows, lanes), BF),
        in_specs=[smem, vmem, vmem, vmem],
        out_specs=vmem,
        scratch_shapes=[
            pltpu.VMEM((2 * parent_rows, side * chans, lanes), BF),
            pltpu.VMEM((side, side * chans, lanes), BF),
            pltpu.VMEM((blocks, side * chans, lanes), BF),
            pltpu.VMEM((parents_dev * side, lanes), BF if fold == 1 else jnp.int32),
        ],
        compiler_params=limit(16),
        name="pack",
    )(place, parent_owner[None, :], m_own, m_recv)

    def to_peers(x):
        if fold > 1:
            x = x.reshape(blocks, all_rows, fold, lanes // fold)
            x = x.transpose(0, 2, 1, 3).reshape(devices, all_rows, lanes // fold)
        x = lax.all_to_all(x, "tiles", split_axis=0, concat_axis=0, tiled=True)
        if fold > 1:
            x = x.reshape(blocks, fold, all_rows, lanes // fold)
            x = x.transpose(0, 2, 1, 3).reshape(blocks, all_rows, lanes)
        return x

    got = to_peers(packed)
    held, e_oth = pl.pallas_call(
        restore_kernel,
        out_shape=(
            jax.ShapeDtypeStruct((chans, row_count, col_count), BF),
            jax.ShapeDtypeStruct((chans, rows, col_count), BF),
        ),
        in_specs=[smem, vmem, hbm],
        out_specs=(hbm, vmem),
        scratch_shapes=[pltpu.VMEM((chans, rows, col_count), BF), pltpu.SemaphoreType.DMA],
        compiler_params=limit(12),
        name="restore",
    )(place, es, packed)
    e_recv = lax.ppermute(e_oth, "chan", swap)
    enhanced = pl.pallas_call(
        fill_kernel,
        out_shape=jax.ShapeDtypeStruct((chans, row_count, col_count), BF),
        in_specs=[smem, vmem, hbm],
        out_specs=hbm,
        scratch_shapes=[pltpu.SemaphoreType.DMA],
        input_output_aliases={2: 0},
        compiler_params=limit(6),
        name="fill",
    )(place, e_recv, held)
    room = pl.cdiv(own_cap, lanes) * lanes
    parents = pl.pallas_call(
        functools.partial(unpack_kernel, side, slots),
        out_shape=jax.ShapeDtypeStruct((chans, side * side, own_cap), BF),
        in_specs=[smem, vmem],
        out_specs=vmem,
        scratch_shapes=[
            pltpu.VMEM((side, side * chans, room), BF),
            pltpu.VMEM((2, side, side * chans, lanes), BF),
        ],
        compiler_params=limit(24),
        name="unpack",
    )(place, got)
    return enhanced, jnp.swapaxes(parents, 1, 2)


def solution(mesh):
    return jax.shard_map(
        on_device,
        mesh=mesh,
        in_specs=(
            P("chan", "tiles", None),
            P("tiles", None),
            P("tiles"),
            P(None, "chan", None),
            P(None, "chan", None),
            P(None, None, "chan"),
        ),
        out_specs=(P("chan", "tiles", None), P("chan", "tiles", None)),
        check_vma=False,
    )
```

time: 69.5 us -> 69 us (level)
  local copies, waits for them, and re-layouts: 3.62 us -> 6.43 us
  starting transfers between devices: 12.7 us -> 11.1 us
  Pallas kernels: 23 us -> 21.6 us
  other arithmetic: 1.06 us -> 0.09 us
    ppermute x3 -> x2, starting transfers between devices: 6.6 us -> 4.65 us  [the longest x1 4.22 us: on_device(): lax.ppermute(jnp.concatenate([keep, sent[:edge_rows]], axis=0), ('tiles',...]
    unnamed x14 -> x18, local copies, waits for them, and re-layouts: 3.62 us -> 5.24 us
    slice x0 -> x2, local copies, waits for them, and re-layouts: none -> 1.19 us  [the longest x1 1.19 us: on_device(): features[:, row_count - BLK:]]
    pallas_call x1, Pallas kernels: 11.4 us -> 10.3 us  [on_device(): pl.pallas_call(functools.partial(conv_kernel, side), out_shape=(jax.Shape...]
    concatenate x1, other arithmetic: 0.98 us -> 0.01 us  [on_device(): jnp.concatenate([keep, sent[:edge_rows]], axis=0)]
    pallas_call x1, Pallas kernels: 2.2 us -> 2.95 us  [on_device(): pl.pallas_call(functools.partial(unpack_kernel, side, slots), out_shape=j...]
    ppermute x3 -> x2, waiting for transfers between devices: 3.86 us -> 4.26 us  [the longest x1 3.12 us: on_device(): lax.ppermute(jnp.concatenate([keep, sent[:edge_rows]], axis=0), ('tiles',...]
  transfers between devices with their start and end apart: 7 -> 6, of which waited for: 5 -> 5; matrix products, arithmetic and copies ran while one was open for 2% -> 2% of each run, Pallas kernels for 8% -> 8%
where the time goes in v3:
time: 69 us; the launch traced here: 68.5 us
  waiting for transfers between devices  28.5 us (41%)
  Pallas kernels  21.6 us (31%)
  starting transfers between devices  11.1 us (16%)
  local copies, waits for them, and re-layouts  6.43 us (9%)
  between operations  0.75 us (1%)
    all_to_all x1, waiting for transfers between devices, to_peers(): x = lax.all_to_all(x, 'tiles', split_axis=0, concat_axis=0, tiled=True)  20.1 us
    pallas_call x1, Pallas kernels, on_device(): pl.pallas_call(functools.partial(conv_kernel, side), out_shape=(jax.Shape...  10.3 us
    all_to_all x1, starting transfers between devices, to_peers(): x = lax.all_to_all(x, 'tiles', split_axis=0, concat_axis=0, tiled=True)  6.29 us
    unnamed x18, local copies, waits for them, and re-layouts  5.24 us
    ppermute x1, starting transfers between devices, on_device(): lax.ppermute(jnp.concatenate([keep, sent[:edge_rows]], axis=0), ('tiles',...  4.22 us
    ppermute x1, waiting for transfers between devices, on_device(): lax.ppermute(jnp.concatenate([keep, sent[:edge_rows]], axis=0), ('tiles',...  3.12 us
    pallas_call x1, Pallas kernels, on_device(): pl.pallas_call(functools.partial(pack_kernel, side, slots), out_shape=jax...  2.99 us
    pallas_call x1, Pallas kernels, on_device(): pl.pallas_call(functools.partial(unpack_kernel, side, slots), out_shape=j...  2.95 us
  transfers between devices with their start and end apart: 6, of which 5 were waited for; matrix products, arithmetic and copies ran while one was open for 2% of the time, Pallas kernels for 8%

profile of v3, /device:TPU:8, one launch (start us, length us, event | category | flops | bytes accessed | tf_op | source)
XLA Modules:
  0.0 68.5 jit_solution(4797027130627918447)
XLA Ops:
  0.6 0.1 collective-permute-start
  0.7 0.1 pad_add_fusion.place_ref
  0.8 1.2 %fusion = (bf16[32,16,256]{2,1,0:T(8,128)(2,1)S(1)}, bf16[32,16,256]{2,1,0:T(8,128)(2,1)S(1)}) fusion(bf16[32,128,256]{2,1,0:T(8,128)(2,1)} %own_hbm.1), kind=kLoop, calls=%fused_computation.2 | loop fusion | bytes 1048576 | tf_op jit(solution)/shard_map/slice | solution.py:556
  2.0 0.9 %copy-done.3 = bf16[9,32,64]{2,1,0:T(8,128)(2,1)S(1)} copy-done((bf16[9,32,64]{2,1,0:T(8,128)(2,1)S(1)}, bf16[9,32,64]{2,1,0:T(8,128)(2,1)}, u32[]{:S(2)}) %copy-start.3) | copy-done | bytes 36888
  2.9 0.9 %copy-done.4 = bf16[9,32,64]{2,1,0:T(8,128)(2,1)S(1)} copy-done((bf16[9,32,64]{2,1,0:T(8,128)(2,1)S(1)}, bf16[9,32,64]{2,1,0:T(8,128)(2,1)}, u32[]{:S(2)}) %copy-start.4) | copy-done | bytes 36888
  3.8 0.7 %copy-done.5 = s32[16,32]{1,0:T(8,128)S(1)} copy-done((s32[16,32]{1,0:T(8,128)S(1)}, s32[16,32]{1,0:T(8,128)}, u32[]{:S(2)}) %copy-start.5) | copy-done | bytes 2072
  4.5 0.8 %copy-done.7 = bf16[4,64,32]{1,2,0:T(8,128)(2,1)S(1)} copy-done((bf16[4,64,32]{1,2,0:T(8,128)(2,1)S(1)}, bf16[4,64,32]{1,2,0:T(8,128)(2,1)}, u32[]{:S(2)}) %copy-start.7) | copy-done | bytes 16408
  5.2 0.8 %edges.1 = (bf16[960,128]{1,0:T(8,128)(2,1)S(1)}, bf16[256,128]{1,0:T(8,128)(2,1)S(1)}) custom-call(s32[2]{0:T(128)S(1)} %pad_add_fusion.place_ref, bf16[32,16,256]{2,1,0:T(8,128)(2,1)S(1)} %get-tuple-element.23.head_ref, bf16[32,16,256]{2,1,0:T(8,128)(2,1)S(1)} %get-tuple-element.22.tail_ref, s32[16,32]{1,0:T(8,128)S(1)} %copy-done.5, ...), custom_call_target="tpu_custom_call" | custom-call | tf_op jit(solution)/shard_map/edges/pallas_call | solution.py:546
  6.0 0.4 collective-permute-start.1
  6.5 1.1 %collective-permute-done.1.oth_ref = bf16[960,128]{1,0:T(8,128)(2,1)S(1)} collective-permute-done((bf16[960,128]{1,0:T(8,128)(2,1)S(1)}, bf16[960,128]{1,0:T(8,128)(2,1)S(1)}, u32[]{:S(2)}, u32[]{:S(2)}) %collective-permute-start.1) | collective-permute-done | bytes 245792 | tf_op jit(solution)/shard_map/ppermute | solution.py:557
  7.6 4.2 %collective-permute-start.2 = (bf16[512,128]{1,0:T(8,128)(2,1)S(1)}, bf16[512,128]{1,0:T(8,128)(2,1)S(1)}, u32[]{:S(2)}, u32[]{:S(2)}) collective-permute-start(bf16[512,128]{1,0:T(8,128)(2,1)S(1)} %pad_maximum_fusion), channel_id=1, source_target_pairs={{1,2},{3,4},{5,6},{7,8},{9,10},{11,12},{13,14},{15,16},{17,18},{19... | collective-permute-start | bytes 393224 | tf_op jit(solution)/shard_map/ppermute | solution.py:560
  11.9 0.8 %weights.1 = (bf16[192,192]{1,0:T(8,128)(2,1)S(1)}, bf16[192,192]{1,0:T(8,128)(2,1)S(1)}, bf16[64,256]{1,0:T(8,128)(2,1)S(1)}) custom-call(s32[2]{0:T(128)S(1)} %pad_add_fusion.place_ref, bf16[960,128]{1,0:T(8,128)(2,1)S(1)} %get-tuple-element.13.own_ref, bf16[960,128]{1,0:T(8,128)(2,1)S(1)} %collective-permute-done.1.oth_ref), custom_call_target="tpu_custom_call" | custom-call | tf_op jit(solution)/shard_map/weights/pallas_call | solution.py:563
  12.7 3.1 %collective-permute-done.2.outer_ref = bf16[512,128]{1,0:T(8,128)(2,1)S(1)} collective-permute-done((bf16[512,128]{1,0:T(8,128)(2,1)S(1)}, bf16[512,128]{1,0:T(8,128)(2,1)S(1)}, u32[]{:S(2)}, u32[]{:S(2)}) %collective-permute-start.2) | collective-permute-done | bytes 131104 | tf_op jit(solution)/shard_map/ppermute | solution.py:560
  15.8 0.7 %copy-done.6 = s32[16,32]{1,0:T(8,128)S(1)} copy-done((s32[16,32]{1,0:T(8,128)S(1)}, s32[16,32]{1,0:T(8,128)}, u32[]{:S(2)}) %copy-start.6) | copy-done | bytes 2072
  16.5 10.3 %conv.1 = (bf16[64,64,256]{2,1,0:T(8,128)(2,1)S(1)}, bf16[4,256,128]{2,1,0:T(8,128)(2,1)S(1)}, bf16[4,256,128]{2,1,0:T(8,128)(2,1)S(1)}) custom-call(s32[2]{0:T(128)S(1)} %pad_add_fusion.place_ref, bf16[32,128,256]{2,1,0:T(8,128)(2,1)S(1)} %copy-done, bf16[32,128,256]{2,1,0:T(8,128)(2,1)} %collective-permute-done.oth_hbm, ...), custom_call_target="tpu_custom_call" | custom-call | tf_op jit(solution)/shard_map/conv/pallas_call | solution.py:577
  26.8 1.3 %copy-done.1 = bf16[64,64,256]{2,1,0:T(8,128)(2,1)} copy-done((bf16[64,64,256]{2,1,0:T(8,128)(2,1)}, bf16[64,64,256]{2,1,0:T(8,128)(2,1)S(1)}, u32[]{:S(2)}) %copy-start.1) | copy-done | bytes 2097176
  28.2 1.5 %collective-permute-done.3.mrecv_ref = bf16[4,256,128]{2,1,0:T(8,128)(2,1)S(1)} collective-permute-done((bf16[4,256,128]{2,1,0:T(8,128)(2,1)S(1)}, bf16[4,256,128]{2,1,0:T(8,128)(2,1)S(1)}, u32[]{:S(2)}, u32[]{:S(2)}) %collective-permute-start.3) | collective-permute-done | bytes 262176 | tf_op jit(solution)/shard_map/ppermute | solution.py:601
  29.7 3.0 %pack.1.after_hbm = bf16[16,264,128]{2,1,0:T(8,128)(2,1)} custom-call(s32[2]{0:T(128)S(1)} %pad_add_fusion.place_ref, s32[1,128]{1,0:T(1,128)S(1)} %bitcast.6, bf16[4,256,128]{2,1,0:T(8,128)(2,1)S(1)} %get-tuple-element.18.mown_ref, bf16[4,256,128]{2,1,0:T(8,128)(2,1)S(1)} %collective-permute-done.3.mrecv_ref), custom_call_target="tpu_custom_call" | custom-call | tf_op jit(solution)/shard_map/pack/pallas_call | solution.py:603
  32.7 6.3 %all-to-all-start = ((bf16[16,264,128]{2,1,0:T(8,128)(2,1)}), bf16[16,264,128]{2,1,0:T(8,128)(2,1)S(1)}, u32[]{:S(2)}, u32[]{:S(2)}) async-start(bf16[16,264,128]{2,1,0:T(8,128)(2,1)} %pack.1.after_hbm), calls=%async_computation | async-start | bytes 2162688 | tf_op jit(solution)/shard_map/all_to_all | solution.py:622
  39.0 2.2 %restore.1 = (bf16[32,128,256]{2,1,0:T(8,128)(2,1)}, bf16[32,64,256]{2,1,0:T(8,128)(2,1)S(1)}) custom-call(s32[2]{0:T(128)S(1)} %pad_add_fusion.place_ref, bf16[64,64,256]{2,1,0:T(8,128)(2,1)S(1)} %copy-done.2, bf16[16,264,128]{2,1,0:T(8,128)(2,1)} %pack.1.after_hbm), custom_call_target="tpu_custom_call" | custom-call | tf_op jit(solution)/shard_map/restore/pallas_call | solution.py:629
  41.3 2.6 %collective-permute-done.4.recv_ref = bf16[32,64,256]{2,1,0:T(8,128)(2,1)S(1)} collective-permute-done((bf16[32,64,256]{2,1,0:T(8,128)(2,1)S(1)}, bf16[32,64,256]{2,1,0:T(8,128)(2,1)S(1)}, u32[]{:S(2)}, u32[]{:S(2)}) %collective-permute-start.4) | collective-permute-done | bytes 1048608 | tf_op jit(solution)/shard_map/ppermute | solution.py:641
  44.0 1.5 %fill.1 = bf16[32,128,256]{2,1,0:T(8,128)(2,1)} custom-call(s32[2]{0:T(128)S(1)} %pad_add_fusion.place_ref, bf16[32,64,256]{2,1,0:T(8,128)(2,1)S(1)} %collective-permute-done.4.recv_ref, bf16[32,128,256]{2,1,0:T(8,128)(2,1)} %get-tuple-element.21.held_hbm), custom_call_target="tpu_custom_call", output_to_operand_aliasing={{}: (2, {})} | custom-call | tf_op jit(solution)/shard_map/fill/pallas_call | solution.py:642
  45.5 20.1 %all-to-all-done.got_ref = bf16[16,264,128]{2,1,0:T(8,128)(2,1)S(1)} async-done(((bf16[16,264,128]{2,1,0:T(8,128)(2,1)}), bf16[16,264,128]{2,1,0:T(8,128)(2,1)S(1)}, u32[]{:S(2)}, u32[]{:S(2)}) %all-to-all-start) | async-done | bytes 1081376 | tf_op jit(solution)/shard_map/all_to_all | solution.py:622
  65.5 2.9 %unpack.1 = bf16[32,64,192]{2,1,0:T(8,128)(2,1)} custom-call(s32[2]{0:T(128)S(1)} %pad_add_fusion.place_ref, bf16[16,264,128]{2,1,0:T(8,128)(2,1)S(1)} %all-to-all-done.got_ref), custom_call_target="tpu_custom_call" | custom-call | tf_op jit(solution)/shard_map/unpack/pallas_call | solution.py:653
  (17 shorter events, 0.1 us)
Async XLA Ops:
  0.6 15.2 %copy-start = (bf16[32,128,256]{2,1,0:T(8,128)(2,1)S(1)}, bf16[32,128,256]{2,1,0:T(8,128)(2,1)}, u32[]{:S(2)}) copy-start(bf16[32,128,256]{2,1,0:T(8,128)(2,1)} %own_hbm.1) | copy-start | bytes 6291460
  0.6 15.2 %collective-permute-start = (bf16[32,128,256]{2,1,0:T(8,128)(2,1)}, bf16[32,128,256]{2,1,0:T(8,128)(2,1)}, u32[]{:S(2)}, u32[]{:S(2)}) collective-permute-start(bf16[32,128,256]{2,1,0:T(8,128)(2,1)} %own_hbm.1), channel_id=1, source_target_pairs={{0,1},{1,0},{2,3},{3,2},{4,5},{5,4},{6,7},{7,6},{8,9},{9,8},{10,11... | collective-permute-start | bytes 6291464 | tf_op jit(solution)/shard_map/ppermute | solution.py:542
  2.0 0.9 %copy-start.3 = (bf16[9,32,64]{2,1,0:T(8,128)(2,1)S(1)}, bf16[9,32,64]{2,1,0:T(8,128)(2,1)}, u32[]{:S(2)}) copy-start(bf16[9,32,64]{2,1,0:T(8,128)(2,1)} %wa_ref.1) | copy-start | bytes 110596
  2.9 0.9 %copy-start.4 = (bf16[9,32,64]{2,1,0:T(8,128)(2,1)S(1)}, bf16[9,32,64]{2,1,0:T(8,128)(2,1)}, u32[]{:S(2)}) copy-start(bf16[9,32,64]{2,1,0:T(8,128)(2,1)} %wb_ref.1) | copy-start | bytes 110596
  3.8 0.7 %copy-start.5 = (s32[16,32]{1,0:T(8,128)S(1)}, s32[16,32]{1,0:T(8,128)}, u32[]{:S(2)}) copy-start(s32[16,32]{1,0:T(8,128)} %valid_ref.3) | copy-start | bytes 6148
  4.5 0.8 %copy-start.7 = (bf16[4,64,32]{1,2,0:T(8,128)(2,1)S(1)}, bf16[4,64,32]{1,2,0:T(8,128)(2,1)}, u32[]{:S(2)}) copy-start(bf16[4,64,32]{1,2,0:T(8,128)(2,1)} %param.11) | copy-start | bytes 49156
  6.0 1.6 %collective-permute-start.1 = (bf16[960,128]{1,0:T(8,128)(2,1)S(1)}, bf16[960,128]{1,0:T(8,128)(2,1)S(1)}, u32[]{:S(2)}, u32[]{:S(2)}) collective-permute-start(bf16[960,128]{1,0:T(8,128)(2,1)S(1)} %get-tuple-element.13.own_ref), channel_id=1, source_target_pairs={{0,1},{1,0},{2,3},{3,2},{4,5},{5,4},{6,7},{7,6},{8,9},{9,8},{10,11... | collective-permute-start | bytes 737288 | tf_op jit(solution)/shard_map/ppermute | solution.py:557
  7.6 8.2 %collective-permute-start.2 = (bf16[512,128]{1,0:T(8,128)(2,1)S(1)}, bf16[512,128]{1,0:T(8,128)(2,1)S(1)}, u32[]{:S(2)}, u32[]{:S(2)}) collective-permute-start(bf16[512,128]{1,0:T(8,128)(2,1)S(1)} %pad_maximum_fusion), channel_id=1, source_target_pairs={{1,2},{3,4},{5,6},{7,8},{9,10},{11,12},{13,14},{15,16},{17,18},{19... | collective-permute-start | bytes 393224 | tf_op jit(solution)/shard_map/ppermute | solution.py:560
  15.8 0.7 %copy-start.6 = (s32[16,32]{1,0:T(8,128)S(1)}, s32[16,32]{1,0:T(8,128)}, u32[]{:S(2)}) copy-start(s32[16,32]{1,0:T(8,128)} %valid_ref.3) | copy-start | bytes 6148
  16.5 13.2 %copy-start.8 = (s32[128]{0:T(128)S(1)}, s32[128]{0:T(128)}, u32[]{:S(2)}) copy-start(s32[128]{0:T(128)} %param.8) | copy-start | bytes 1540
  26.8 1.3 %copy-start.1 = (bf16[64,64,256]{2,1,0:T(8,128)(2,1)}, bf16[64,64,256]{2,1,0:T(8,128)(2,1)S(1)}, u32[]{:S(2)}) copy-start(bf16[64,64,256]{2,1,0:T(8,128)(2,1)S(1)} %get-tuple-element.17.es_ref) | copy-start | bytes 6291460
  28.2 10.8 %copy-start.2 = (bf16[64,64,256]{2,1,0:T(8,128)(2,1)S(1)}, bf16[64,64,256]{2,1,0:T(8,128)(2,1)}, u32[]{:S(2)}) copy-start(bf16[64,64,256]{2,1,0:T(8,128)(2,1)} %copy-done.1) | copy-start | bytes 6291460
  28.2 1.5 %collective-permute-start.3 = (bf16[4,256,128]{2,1,0:T(8,128)(2,1)S(1)}, bf16[4,256,128]{2,1,0:T(8,128)(2,1)S(1)}, u32[]{:S(2)}, u32[]{:S(2)}) collective-permute-start(bf16[4,256,128]{2,1,0:T(8,128)(2,1)S(1)} %get-tuple-element.19), channel_id=1, source_target_pairs={{0,1},{1,0},{2,3},{3,2},{4,5},{5,4},{6,7},{7,6},{8,9},{9,8},{10,11... | collective-permute-start | bytes 786440 | tf_op jit(solution)/shard_map/ppermute | solution.py:601
  32.7 32.8 %all-to-all-start = ((bf16[16,264,128]{2,1,0:T(8,128)(2,1)}), bf16[16,264,128]{2,1,0:T(8,128)(2,1)S(1)}, u32[]{:S(2)}, u32[]{:S(2)}) async-start(bf16[16,264,128]{2,1,0:T(8,128)(2,1)} %pack.1.after_hbm), calls=%async_computation | async-start | bytes 2162688 | tf_op jit(solution)/shard_map/all_to_all | solution.py:622
  41.2 2.7 %collective-permute-start.4 = (bf16[32,64,256]{2,1,0:T(8,128)(2,1)S(1)}, bf16[32,64,256]{2,1,0:T(8,128)(2,1)S(1)}, u32[]{:S(2)}, u32[]{:S(2)}) collective-permute-start(bf16[32,64,256]{2,1,0:T(8,128)(2,1)S(1)} %get-tuple-element.20), channel_id=1, source_target_pairs={{0,1},{1,0},{2,3},{3,2},{4,5},{5,4},{6,7},{7,6},{8,9},{9,8},{10,11... | collective-permute-start | bytes 3145736 | tf_op jit(solution)/shard_map/ppermute | solution.py:641

commit v4 on v3

--- a/solution.py
+++ b/solution.py
@@ -69,10 +69,15 @@
 
 
 def edges_kernel(
-    side, place_ref, head_ref, tail_ref, valid_ref, wa_ref, wb_ref, wc_ref, send_ref, keep_ref
+    side, place_ref, feat_hbm, valid_ref, wa_ref, wb_ref, wc_ref, send_ref, keep_ref, edge, sems
 ):
     core = place_ref[0]
-    chans, _, cols = head_ref.shape
+    chans, feat_rows, cols = feat_hbm.shape
+    copies = []
+    for n, at in enumerate((0, feat_rows - BLK)):
+        copy = pltpu.make_async_copy(feat_hbm.at[:, at : at + BLK, :], edge.at[n], sems.at[n])
+        copy.start()
+        copies.append(copy)
     flat = chans * HALO
     lanes = send_ref.shape[1]
     at = flat * cols // lanes
@@ -85,11 +90,15 @@
         at += taps * outs
     tiles_r, tiles_c = valid_ref.shape
     masks = mm(as_bf(valid_ref[...]), widen_matrix(tiles_c, cols, side))
+    for n in range(cols // lanes):
+        send_ref[at + n * tiles_r : at + (n + 1) * tiles_r, :] = masks[
+            :, n * lanes : (n + 1) * lanes
+        ].astype(BF)
     row, col = iota((flat, chans * BLK), 0), iota((flat, chans * BLK), 1)
     same = div(row, HALO) == div(col, BLK)
     spot = mod(iota((flat, cols), 0), HALO)
     made = []
-    for n, ref in enumerate((head_ref, tail_ref)):
+    for n in range(2):
         if n == 0:
             hit = same & (mod(row, HALO) == mod(col, BLK)) & (mod(row, HALO) < HALO - 1)
             flag, line = spot == HALO - 1, masks[0:1]
@@ -97,7 +106,8 @@
             hit = same & (mod(row, HALO) + BLK - HALO == mod(col, BLK)) & (mod(row, HALO) > 0)
             flag, line = spot == 0, masks[tiles_r - 1 : tiles_r]
         take = ones_where(hit)
-        body = mm(take, ref[...].reshape(chans * BLK, cols))
+        copies[n].wait()
+        body = mm(take, edge[n].reshape(chans * BLK, cols))
         made.append(jnp.where(flag, jnp.broadcast_to(line, (flat, cols)), body).astype(BF))
     low = core == 0
     send = jnp.where(low, made[1], made[0])
@@ -107,7 +117,7 @@
         keep_ref[n * flat : (n + 1) * flat, :] = keep[:, n * lanes : (n + 1) * lanes]
 
 
-def weights_kernel(at, chans, place_ref, own_ref, oth_ref, w1_ref, w2_ref, wm_ref):
+def weights_kernel(at, chans, place_ref, own_ref, oth_ref, w1_ref, w2_ref, wm_ref, mask_ref):
     core = place_ref[0]
     allc = 2 * chans
 
@@ -128,6 +138,37 @@
     )
     order = ones_where(iota((allc, allc), 1) == mod(iota((allc, allc), 0) + chans * core, allc))
     wm_ref[...] = mm_nt(order, tall).astype(BF)
+    tiles_r = mask_ref.shape[0]
+    lanes = own_ref.shape[1]
+    at = own_ref.shape[0] - tiles_r * mask_ref.shape[1] // lanes
+    for n in range(mask_ref.shape[1] // lanes):
+        part = own_ref[at + n * tiles_r : at + (n + 1) * tiles_r, :]
+        mask_ref[:, n * lanes : (n + 1) * lanes] = part.astype(F32)
+
+
+def put(dst, index, x, amount):
+    allc = x.shape[0]
+    dst[index, 0:allc, :] = shifted(x, amount).astype(BF)
+    dst[index, allc : 2 * allc, :] = x.astype(BF)
+    dst[index, 2 * allc : 3 * allc, :] = shifted(x, -amount).astype(BF)
+
+
+def pick_matrix(cols, side):
+    half = cols // 2
+    wide = half // side
+    lane = iota((cols, cols), 1)
+    spot = mod(lane, half)
+    want = 2 * (mod(spot, wide) * side + div(spot, wide)) + div(lane, half)
+    return ones_where(iota((cols, cols), 0) == want)
+
+
+def merge_pairs(wm, rows_of, pairs, turn, half):
+    rhs = []
+    for n in pairs:
+        sp = rows_of(n)
+        rhs.append(jnp.concatenate([sp[:, :half], sp[:, half:]], axis=0))
+    both = mm(wm, jnp.concatenate(rhs, axis=1))
+    return [pltpu.roll(both[:, n * half : (n + 1) * half], turn, 1) for n in range(2)]
 
 
 def conv_kernel(
@@ -135,14 +176,16 @@
     place_ref,
     own_hbm,
     oth_hbm,
-    outer_ref,
-    valid_ref,
+    masks_ref,
     w1,
     w2,
     wm,
     es_hbm,
     mown_ref,
     moth_ref,
+    xa_ref,
+    ha_ref,
+    ea_ref,
     feat,
     xs,
     hs,
@@ -166,39 +209,15 @@
             )
             copy.start()
             copies.append(copy)
-    lanes = outer_ref.shape[1]
-
-    tiles_r, tiles_c = valid_ref.shape
-    mask[pl.ds(side, tiles_r), :] = mm(as_bf(valid_ref[...]), widen_matrix(tiles_c, cols, side))
-
-    def put(dst, index, x, amount):
-        dst[index, 0:allc, :] = shifted(x, amount).astype(BF)
-        dst[index, allc : 2 * allc, :] = x.astype(BF)
-        dst[index, 2 * allc : 3 * allc, :] = shifted(x, -amount).astype(BF)
+
+    tiles_r = masks_ref.shape[0]
+    mask[...] = jnp.zeros(mask.shape, F32)
+    mask[pl.ds(side, tiles_r), :] = masks_ref[...]
 
     first_row = 5
-    turn4 = swap_matrix(HALO, chans)
-    flat = HALO * chans
-    pieces = [outer_ref[k * flat : (k + 1) * flat, :] for k in range(2 * cols // lanes)]
-    oth, own = [
-        mm(turn4, jnp.concatenate(pieces[n * cols // lanes : (n + 1) * cols // lanes], axis=1))
-        for n in range(2)
-    ]
-    start = jnp.where(core == 0, first_row - HALO, first_row + rows)
+    outer_start = jnp.where(core == 0, first_row - HALO, first_row + rows)
     for r in range(HALO):
-        at = slice(r * chans, (r + 1) * chans)
-        put(xs, start + r, jnp.concatenate([own[at], oth[at]], axis=0), 1)
-    top = own[0:1, :]
-    bottom = own[(HALO - 1) * chans : (HALO - 1) * chans + 1, :]
-
-    @pl.when(core == 0)
-    def _():
-        mask[pl.ds(side - 1, 1), :] = top
-
-    @pl.when(core == 1)
-    def _():
-        mask[pl.ds(side + tiles_r, 1), :] = bottom
-
+        xs[outer_start + r] = jnp.zeros(xs.shape[1:], BF)
     xs[0] = jnp.zeros(xs.shape[1:], BF)
     turn = swap_matrix(BLK, BLK)
     few = HALO * BLK
@@ -270,45 +289,141 @@
 
     lax.fori_loop(0, total_steps // tiles, second, 0)
 
-    out = pltpu.make_async_copy(es_ref, es_hbm, out_sem)
+    out = pltpu.make_async_copy(es_ref, es_hbm.at[pl.ds(0, rows)], out_sem)
     out.start()
+
+    for k in range(3):
+        xa_ref[k] = xs[first_row + (rows - 3) * core + k]
+    for k in range(4):
+        ha_ref[k] = hs[jnp.where(core == 0, 7, rows + 1) + k]
+    ea_ref[0] = es_ref[jnp.where(core == 0, 3, rows - 4)]
 
     half = cols // 2
     wide = half // side
-    lane = iota((cols, cols), 1)
-    spot = mod(lane, half)
-    want = 2 * (mod(spot, wide) * side + div(spot, wide)) + div(lane, half)
-    pick = ones_where(iota((cols, cols), 0) == want)
+    pick = pick_matrix(cols, side)
     picked = hs.reshape(hs.shape[0] * hs.shape[1], cols)
     for tile in range(rows // side):
         tall = es_ref[tile * side : (tile + 1) * side].reshape(side * allc, cols)
         picked[tile * side * allc : (tile + 1) * side * allc, :] = mm(tall, pick).astype(BF)
     for tile in range(rows // side):
         g = tile // 2 + core * (rows // (2 * side))
+
+        def rows_of(k, tile=tile):
+            at = (tile * side + 2 * k) * allc
+            return picked[at : at + 2 * allc, :]
+
         for k in range(0, side // 2, 2):
-            pairs = []
-            for n in range(2):
-                at = (tile * side + 2 * (k + n)) * allc
-                sp = picked[at : at + 2 * allc, :]
-                pairs.append(jnp.concatenate([sp[:, :half], sp[:, half:]], axis=0))
-            both = mm(wm[...], jnp.concatenate(pairs, axis=1))
-            for n in range(2):
+            for n, piece in enumerate(merge_pairs(wm[...], rows_of, (k, k + 1), g * wide, half)):
                 u = (side // 2) * (tile % 2) + k + n
-                piece = pltpu.roll(both[:, n * half : (n + 1) * half], g * wide, 1).astype(BF)
-                mown_ref[tile // 2, u * chans : (u + 1) * chans, :] = piece[:chans]
-                moth_ref[tile // 2, u * chans : (u + 1) * chans, :] = piece[chans:]
+                mown_ref[tile // 2, u * chans : (u + 1) * chans, :] = piece[:chans].astype(BF)
+                moth_ref[tile // 2, u * chans : (u + 1) * chans, :] = piece[chans:].astype(BF)
     out.wait()
 
 
-def restore_kernel(place_ref, es_ref, after_hbm, enh_hbm, eoth_ref, own, sem):
+def border_kernel(
+    rows,
+    place_ref,
+    outer_ref,
+    masks_ref,
+    w1,
+    w2,
+    wm,
+    xa_ref,
+    ha_ref,
+    ea_ref,
+    mown_in,
+    moth_in,
+    es_in,
+    es_hbm,
+    mown_ref,
+    moth_ref,
+    x5,
+    h7,
+    e4,
+    sem,
+):
+    core = place_ref[0]
+    _, allc, cols = ea_ref.shape
+    chans = allc // 2
+    lanes = outer_ref.shape[1]
+    tiles_r = masks_ref.shape[0]
+    masks = masks_ref[...]
+    top = core == 0
+    turn4 = swap_matrix(HALO, chans)
+    flat = HALO * chans
+    pieces = [outer_ref[k * flat : (k + 1) * flat, :] for k in range(2 * cols // lanes)]
+    oth, own = [
+        mm(turn4, jnp.concatenate(pieces[n * cols // lanes : (n + 1) * cols // lanes], axis=1))
+        for n in range(2)
+    ]
+    halo = [
+        jnp.concatenate([p[r * chans : (r + 1) * chans] for p in (own, oth)], axis=0)
+        for r in range(HALO)
+    ]
+    outer_mask = jnp.where(top, halo[0][0:1], halo[HALO - 1][0:1])
+    tile_mask = jnp.where(top, masks[0:1], masks[tiles_r - 1 : tiles_r])
+    for k in range(3):
+        put(x5, jnp.where(top, k, k + 2), jnp.where(top, halo[k + 1], halo[k]), 1)
+    for k in range(2):
+        x5[jnp.where(top, k + 3, k)] = xa_ref[jnp.where(top, k, k + 1)]
+    for k in range(4):
+        h7[jnp.where(top, k + 3, k)] = ha_ref[k]
+    y = [mm(w1[...], x5[k]) for k in range(5)]
+    for k in range(3):
+        total = y[k][:allc] + y[k + 1][allc : 2 * allc] + y[k + 2][2 * allc :]
+        if k == 1:
+            line = outer_mask
+        else:
+            line = jnp.where(top if k == 0 else core == 1, outer_mask, tile_mask)
+        h = jnp.maximum(total * line, 0.0)
+        put(h7, jnp.where(top, k, k + 4), h, 2)
+    z = [mm(w2[...], h7[k]) for k in range(7)]
+    e4[jnp.where(top, 3, 0)] = ea_ref[0]
+    for k in range(3):
+        total = z[k][:allc] + z[k + 2][allc : 2 * allc] + z[k + 4][2 * allc :]
+        x = xa_ref[k, allc : 2 * allc, :].astype(F32)
+        e4[jnp.where(top, k, k + 1)] = (tile_mask * (x + total)).astype(BF)
+    copy = pltpu.make_async_copy(
+        e4.at[pl.ds(core, 3)], es_hbm.at[pl.ds((rows - 3) * core, 3)], sem
+    )
+    copy.start()
+    mown_ref[...] = mown_in[...]
+    moth_ref[...] = moth_in[...]
+    half = cols // 2
+    parent_rows = mown_ref.shape[0]
+    side = mown_ref.shape[1] // chans
+    wide = half // side
+    s = mm(e4[...].reshape(4 * allc, cols), pick_matrix(cols, side)).astype(BF)
+    g = jnp.where(top, 0, 2 * parent_rows - 1)
+    at_g = jnp.where(top, 0, parent_rows - 1)
+
+    def rows_of(k):
+        return s[k * 2 * allc : (k + 1) * 2 * allc]
+
+    for n, piece in enumerate(merge_pairs(wm[...], rows_of, (0, 1), g * wide, half)):
+        u = jnp.where(top, n, side - 2 + n)
+        at_u = pl.ds(pl.multiple_of(u * chans, chans), chans)
+        mown_ref[at_g, at_u, :] = piece[:chans].astype(BF)
+        moth_ref[at_g, at_u, :] = piece[chans:].astype(BF)
+    copy.wait()
+
+
+def restore_kernel(place_ref, es_hbm, after_hbm, enh_hbm, eoth_ref, es_ref, own, sem, in_sems):
     core = place_ref[0]
     rows, allc, cols = es_ref.shape
     chans = allc // 2
+    copies = []
+    for m in range(rows // BLK):
+        at = pl.ds(m * BLK, BLK)
+        copies.append(pltpu.make_async_copy(es_hbm.at[at], es_ref.at[at], in_sems.at[m]))
+        copies[-1].start()
     turn = swap_matrix(BLK, BLK)
-    for c0 in list(range(chans, allc, BLK)) + list(range(0, chans, BLK)):
-        ref = own if c0 < chans else eoth_ref
-        ch = c0 % chans
-        for at in range(0, rows, BLK):
+    for m in range(rows // BLK):
+        copies[m].wait()
+        at = m * BLK
+        for c0 in range(0, allc, BLK):
+            ref = own if c0 < chans else eoth_ref
+            ch = c0 % chans
             block = es_ref[at : at + BLK, c0 : c0 + BLK, :].reshape(BLK * BLK, cols)
             ref[ch : ch + BLK, at : at + BLK, :] = mm(turn, block).astype(BF).reshape(BLK, BLK, cols)
     copy = pltpu.make_async_copy(
@@ -473,7 +588,7 @@
                     data[h, j, at, :] = done[j]
                 return carry
 
-            lax.fori_loop(0, rows // BLK, turn_rows, 0, unroll=4)
+            lax.fori_loop(0, rows // BLK, turn_rows, 0, unroll=True)
         for j in range(side):
             v = lax.rem(2 * side - j - lax.rem(tile, side), side)
             left = jnp.concatenate([data[h, j] for h in range(halves)], axis=1)
@@ -537,52 +652,62 @@
     hbm = pl.BlockSpec(memory_space=pltpu.HBM)
 
     def limit(mib):
-        return pltpu.CompilerParams(vmem_limit_bytes=mib << 20)
+        return pltpu.CompilerParams(vmem_limit_bytes=int(mib * 1024) << 10)
 
     feat_oth = lax.ppermute(features, "chan", swap)
     w_mergt = jnp.swapaxes(w_merge, 1, 2)
     edge_rows = chans * HALO * col_count // lanes
     tap_rows = (w_first.shape[0] + w_second.shape[0] + w_merge.shape[0]) * chans
+    mask_rows = tile_rows * col_count // lanes
     send, keep = pl.pallas_call(
         functools.partial(edges_kernel, side),
         out_shape=(
-            jax.ShapeDtypeStruct((edge_rows + tap_rows, lanes), BF),
+            jax.ShapeDtypeStruct((edge_rows + tap_rows + mask_rows, lanes), BF),
             jax.ShapeDtypeStruct((edge_rows, lanes), BF),
         ),
-        in_specs=[smem] + [vmem] * 6,
+        in_specs=[smem, hbm] + [vmem] * 4,
         out_specs=(vmem,) * 2,
-        compiler_params=limit(6),
+        scratch_shapes=[
+            pltpu.VMEM((2, chans, BLK, col_count), BF),
+            pltpu.SemaphoreType.DMA((2,)),
+        ],
+        compiler_params=limit(63.9),
         name="edges",
-    )(place, features[:, :BLK], features[:, row_count - BLK :], tile_valid, w_first, w_second, w_mergt)
+    )(place, features, tile_valid, w_first, w_second, w_mergt)
     sent = lax.ppermute(send, "chan", swap)
     cross = [(2 * t + 1, 2 * t + 2) for t in range(devices - 1)]
     cross += [(2 * t, 2 * t - 1) for t in range(1, devices)]
     outer = lax.ppermute(
         jnp.concatenate([keep, sent[:edge_rows]], axis=0), ("tiles", "chan"), cross
     )
-    w1, w2, wm = pl.pallas_call(
+    w1, w2, wm, masks = pl.pallas_call(
         functools.partial(weights_kernel, edge_rows, chans),
         out_shape=(
             jax.ShapeDtypeStruct((3 * allc, 3 * allc), BF),
             jax.ShapeDtypeStruct((3 * allc, 3 * allc), BF),
             jax.ShapeDtypeStruct((allc, 4 * allc), BF),
+            jax.ShapeDtypeStruct((tile_rows, col_count), F32),
         ),
         in_specs=[smem, vmem, vmem],
-        out_specs=(vmem,) * 3,
+        out_specs=(vmem,) * 4,
         compiler_params=limit(6),
         name="weights",
     )(place, send, sent)
 
     parent_rows = tile_rows // 4
-    es, m_own, m_oth = pl.pallas_call(
+    held_rows = rows * pl.cdiv(44 << 20, rows * allc * col_count * 2)
+    es, m_own, m_oth, xa, ha, ea = pl.pallas_call(
         functools.partial(conv_kernel, side),
         out_shape=(
-            jax.ShapeDtypeStruct((rows, allc, col_count), BF),
+            jax.ShapeDtypeStruct((held_rows, allc, col_count), BF),
             jax.ShapeDtypeStruct((parent_rows, side * chans, col_count // 2), BF),
             jax.ShapeDtypeStruct((parent_rows, side * chans, col_count // 2), BF),
+            jax.ShapeDtypeStruct((3, 3 * allc, col_count), BF),
+            jax.ShapeDtypeStruct((4, 3 * allc, col_count), BF),
+            jax.ShapeDtypeStruct((1, allc, col_count), BF),
         ),
-        in_specs=[smem, hbm, hbm] + [vmem] * 5,
-        out_specs=(hbm, vmem, vmem),
+        in_specs=[smem, hbm, hbm] + [vmem] * 4,
+        out_specs=(hbm,) + (vmem,) * 5,
         scratch_shapes=[
             pltpu.VMEM((2, rows // BLK + 1, chans, BLK, col_count), BF),
             pltpu.VMEM((rows + 16, 3 * allc, col_count), BF),
@@ -594,10 +719,28 @@
             pltpu.SemaphoreType.DMA((2, rows // BLK + 1)),
             pltpu.SemaphoreType.DMA,
         ],
-        compiler_params=limit(34),
+        compiler_params=limit(52),
         name="conv",
-    )(place, features, feat_oth, outer, tile_valid, w1, w2, wm)
-
+    )(place, features, feat_oth, masks, w1, w2, wm)
+    es, m_own, m_oth = pl.pallas_call(
+        functools.partial(border_kernel, rows),
+        out_shape=(
+            jax.ShapeDtypeStruct(es.shape, BF),
+            jax.ShapeDtypeStruct((parent_rows, side * chans, col_count // 2), BF),
+            jax.ShapeDtypeStruct((parent_rows, side * chans, col_count // 2), BF),
+        ),
+        in_specs=[smem] + [vmem] * 10 + [hbm],
+        out_specs=(hbm, vmem, vmem),
+        scratch_shapes=[
+            pltpu.VMEM((5, 3 * allc, col_count), BF),
+            pltpu.VMEM((7, 3 * allc, col_count), BF),
+            pltpu.VMEM((4, allc, col_count), BF),
+            pltpu.SemaphoreType.DMA,
+        ],
+        input_output_aliases={11: 0},
+        compiler_params=limit(16),
+        name="border",
+    )(place, outer, masks, w1, w2, wm, xa, ha, ea, m_own, m_oth, es)
     m_recv = lax.ppermute(m_oth, "chan", swap)
     all_rows = side * chans + 8
     packed = pl.pallas_call(
@@ -632,9 +775,14 @@
             jax.ShapeDtypeStruct((chans, row_count, col_count), BF),
             jax.ShapeDtypeStruct((chans, rows, col_count), BF),
         ),
-        in_specs=[smem, vmem, hbm],
+        in_specs=[smem, hbm, hbm],
         out_specs=(hbm, vmem),
-        scratch_shapes=[pltpu.VMEM((chans, rows, col_count), BF), pltpu.SemaphoreType.DMA],
+        scratch_shapes=[
+            pltpu.VMEM((rows, allc, col_count), BF),
+            pltpu.VMEM((chans, rows, col_count), BF),
+            pltpu.SemaphoreType.DMA,
+            pltpu.SemaphoreType.DMA((rows // BLK,)),
+        ],
         compiler_params=limit(12),
         name="restore",
     )(place, es, packed)

time: 69 us -> 67 us (0.971)
  Pallas kernels: 21.6 us -> 29 us
  local copies, waits for them, and re-layouts: 6.43 us -> 0.96 us
  waiting for transfers between devices: 28.5 us -> 24 us
  other arithmetic: 0.09 us -> 1.47 us
  starting transfers between devices: 11.1 us -> 10.4 us
    unnamed x18 -> x6, local copies, waits for them, and re-layouts: 5.24 us -> 0.95 us
    ppermute x1, waiting for transfers between devices: 3.12 us -> 0.01 us  [on_device(): lax.ppermute(jnp.concatenate([keep, sent[:edge_rows]], axis=0), ('tiles',...]
    pallas_call x0 -> x1, Pallas kernels: none -> 2.51 us  [on_device(): pl.pallas_call(functools.partial(border_kernel, rows), out_shape=(jax.Sha...]
    pallas_call x1, Pallas kernels: 0.8 us -> 3.09 us  [on_device(): pl.pallas_call(functools.partial(edges_kernel, side), out_shape=(jax.Shap...]
    all_to_all x1, waiting for transfers between devices: 20.1 us -> 18.5 us  [to_peers(): x = lax.all_to_all(x, 'tiles', split_axis=0, concat_axis=0, tiled=True)]
    pallas_call x1, Pallas kernels: 2.24 us -> 3.74 us  [on_device(): pl.pallas_call(restore_kernel, out_shape=(jax.ShapeDtypeStruct((chans, ro...]
    slice x1 -> x0, local copies, waits for them, and re-layouts: 1.19 us -> none  [on_device(): features[:, row_count - BLK:]]
    pallas_call x1, Pallas kernels: 10.3 us -> 11.4 us  [on_device(): pl.pallas_call(functools.partial(conv_kernel, side), out_shape=(jax.Shape...]
  transfers between devices with their start and end apart: 6 -> 6, of which waited for: 5 -> 4; matrix products, arithmetic and copies ran while one was open for 2% -> 2% of each run, Pallas kernels for 8% -> 31%
where the time goes in v4:
time: 67 us; the launch traced here: 66.6 us
  Pallas kernels  29 us (43%)
  waiting for transfers between devices  24 us (36%)
  starting transfers between devices  10.4 us (16%)
  other arithmetic  1.47 us (2%)
  local copies, waits for them, and re-layouts  0.96 us (1%)
  between operations  0.76 us (1%)
    all_to_all x1, waiting for transfers between devices, to_peers(): x = lax.all_to_all(x, 'tiles', split_axis=0, concat_axis=0, tiled=True)  18.5 us
    pallas_call x1, Pallas kernels, on_device(): pl.pallas_call(functools.partial(conv_kernel, side), out_shape=(jax.Shape...  11.4 us
    all_to_all x1, starting transfers between devices, to_peers(): x = lax.all_to_all(x, 'tiles', split_axis=0, concat_axis=0, tiled=True)  5.43 us
    ppermute x1, starting transfers between devices, on_device(): lax.ppermute(jnp.concatenate([keep, sent[:edge_rows]], axis=0), ('tiles',...  4.22 us
    pallas_call x1, Pallas kernels, on_device(): pl.pallas_call(restore_kernel, out_shape=(jax.ShapeDtypeStruct((chans, ro...  3.74 us
    pallas_call x1, Pallas kernels, on_device(): pl.pallas_call(functools.partial(edges_kernel, side), out_shape=(jax.Shap...  3.09 us
    pallas_call x1, Pallas kernels, on_device(): pl.pallas_call(functools.partial(pack_kernel, side, slots), out_shape=jax...  2.98 us
    pallas_call x1, Pallas kernels, on_device(): pl.pallas_call(functools.partial(unpack_kernel, side, slots), out_shape=j...  2.95 us
  transfers between devices with their start and end apart: 6, of which 4 were waited for; matrix products, arithmetic and copies ran while one was open for 2% of the time, Pallas kernels for 31%

profile of v4, /device:TPU:8, one launch (start us, length us, event | category | flops | bytes accessed | tf_op | source)
XLA Modules:
  0.0 66.6 jit_solution(10035536856103067525)
XLA Ops:
  0.6 0.1 collective-permute-start.2
  0.7 0.6 pad_add_fusion.place_ref
  1.3 3.1 %edges.1 = (bf16[992,128]{1,0:T(8,128)(2,1)}, bf16[256,128]{1,0:T(8,128)(2,1)}) custom-call(s32[2]{0:T(128)} %pad_add_fusion.place_ref, bf16[32,128,256]{2,1,0:T(8,128)(2,1)} %own_hbm.1, s32[16,32]{1,0:T(8,128)} %valid_ref.1, bf16[9,32,64]{2,1,0:T(8,128)(2,1)} %wa_ref.1, bf16[9,32,64]{2,1,0:T(8,128)(2,1)} %wb_ref.1, bf16[4,32,64]{2,1,0:T(8,128)(2,1)} %bitcast.7), custom_call_target="tpu_custom_call" | custom-call | tf_op jit(solution)/shard_map/edges/pallas_call | solution.py:662
  4.4 0.6 collective-permute-start
  5.0 1.4 %collective-permute-done.oth_ref = bf16[992,128]{1,0:T(8,128)(2,1)S(1)} collective-permute-done((bf16[992,128]{1,0:T(8,128)(2,1)}, bf16[992,128]{1,0:T(8,128)(2,1)S(1)}, u32[]{:S(2)}, u32[]{:S(2)}) %collective-permute-start) | collective-permute-done | bytes 253984 | tf_op jit(solution)/shard_map/ppermute | solution.py:677
  6.4 0.8 %pad_maximum_fusion = bf16[512,128]{1,0:T(8,128)(2,1)S(1)} fusion(bf16[256,128]{1,0:T(8,128)(2,1)S(1)} %slice.4, bf16[256,128]{1,0:T(8,128)(2,1)} %get-tuple-element.19), kind=kLoop, calls=%fused_computation | loop fusion | flops 262144 | bytes 262144 | tf_op jit(solution)/shard_map/concatenate | solution.py:681
  7.2 4.2 %collective-permute-start.1 = (bf16[512,128]{1,0:T(8,128)(2,1)S(1)}, bf16[512,128]{1,0:T(8,128)(2,1)S(1)}, u32[]{:S(2)}, u32[]{:S(2)}) collective-permute-start(bf16[512,128]{1,0:T(8,128)(2,1)S(1)} %pad_maximum_fusion), channel_id=1, source_target_pairs={{1,2},{3,4},{5,6},{7,8},{9,10},{11,12},{13,14},{15,16},{17,18},{19... | collective-permute-start | bytes 393224 | tf_op jit(solution)/shard_map/ppermute | solution.py:680
  11.4 0.0 copy-start
  11.5 0.9 %copy-done = bf16[992,128]{1,0:T(8,128)(2,1)S(1)} copy-done((bf16[992,128]{1,0:T(8,128)(2,1)S(1)}, bf16[992,128]{1,0:T(8,128)(2,1)}, u32[]{:S(2)}) %copy-start) | copy-done | bytes 253976
  12.4 0.8 %weights.1 = (bf16[192,192]{1,0:T(8,128)(2,1)S(1)}, bf16[192,192]{1,0:T(8,128)(2,1)S(1)}, bf16[64,256]{1,0:T(8,128)(2,1)S(1)}, f32[16,256]{1,0:T(8,128)S(1)}) custom-call(s32[2]{0:T(128)S(1)} %copy-done.1, bf16[992,128]{1,0:T(8,128)(2,1)S(1)} %copy-done, bf16[992,128]{1,0:T(8,128)(2,1)S(1)} %collective-permute-done.oth_ref), custom_call_target="tpu_custom_call" | custom-call | tf_op jit(solution)/shard_map/weights/pallas_call | solution.py:683
  13.2 0.0 collective-permute-done.2.oth_hbm
  13.3 11.4 %conv.1 = (bf16[1408,64,256]{2,1,0:T(8,128)(2,1)}, bf16[4,256,128]{2,1,0:T(8,128)(2,1)S(1)}, bf16[4,256,128]{2,1,0:T(8,128)(2,1)S(1)}, bf16[3,192,256]{2,1,0:T(8...) custom-call(s32[2]{0:T(128)S(1)} %copy-done.1, bf16[32,128,256]{2,1,0:T(8,128)(2,1)} %own_hbm.1, ...), custom_call_target="tpu_custom_call" | custom-call | tf_op jit(solution)/shard_map/conv/pallas_call | solution.py:699
  24.6 0.0 copy-start.2
  24.7 2.5 %border.1 = (bf16[1408,64,256]{2,1,0:T(8,128)(2,1)}, bf16[4,256,128]{2,1,0:T(8,128)(2,1)S(1)}, bf16[4,256,128]{2,1,0:T(8,128)(2,1)S(1)}) custom-call(s32[2]{0:T(128)S(1)} %copy-done.1, bf16[512,128]{1,0:T(8,128)(2,1)S(1)} %collective-permute-done.1.outer_ref, f32[16,256]{1,0:T(8,128)S(1)} %get-tuple-element.21.masks_ref, ...), custom_call_target="tpu_custom_call", output_to_operand_aliasing={{0}: (11, {})} | custom-call | tf_op jit(solution)/shard_map/border/pallas_call | solution.py:725
  27.2 0.1 collective-permute-start.3
  27.3 1.5 %collective-permute-done.3.mrecv_ref = bf16[4,256,128]{2,1,0:T(8,128)(2,1)S(1)} collective-permute-done((bf16[4,256,128]{2,1,0:T(8,128)(2,1)S(1)}, bf16[4,256,128]{2,1,0:T(8,128)(2,1)S(1)}, u32[]{:S(2)}, u32[]{:S(2)}) %collective-permute-start.3) | collective-permute-done | bytes 262176 | tf_op jit(solution)/shard_map/ppermute | solution.py:744
  28.8 3.0 %pack.1.after_hbm = bf16[16,264,128]{2,1,0:T(8,128)(2,1)} custom-call(s32[2]{0:T(128)S(1)} %copy-done.1, s32[1,128]{1,0:T(1,128)S(1)} %bitcast.5, bf16[4,256,128]{2,1,0:T(8,128)(2,1)S(1)} %get-tuple-element.32.mown_ref, bf16[4,256,128]{2,1,0:T(8,128)(2,1)S(1)} %collective-permute-done.3.mrecv_ref), custom_call_target="tpu_custom_call" | custom-call | tf_op jit(solution)/shard_map/pack/pallas_call | solution.py:746
  31.8 5.4 %all-to-all-start = ((bf16[16,264,128]{2,1,0:T(8,128)(2,1)}), bf16[16,264,128]{2,1,0:T(8,128)(2,1)S(1)}, u32[]{:S(2)}, u32[]{:S(2)}) async-start(bf16[16,264,128]{2,1,0:T(8,128)(2,1)} %pack.1.after_hbm), calls=%async_computation | async-start | bytes 2162688 | tf_op jit(solution)/shard_map/all_to_all | solution.py:765
  37.2 3.7 %restore.1 = (bf16[32,128,256]{2,1,0:T(8,128)(2,1)}, bf16[32,64,256]{2,1,0:T(8,128)(2,1)S(1)}) custom-call(s32[2]{0:T(128)S(1)} %copy-done.1, bf16[1408,64,256]{2,1,0:T(8,128)(2,1)} %get-tuple-element.31.es_hbm, bf16[16,264,128]{2,1,0:T(8,128)(2,1)} %pack.1.after_hbm), custom_call_target="tpu_custom_call" | custom-call | tf_op jit(solution)/shard_map/restore/pallas_call | solution.py:772
  40.9 0.1 collective-permute-start.4
  41.0 2.6 %collective-permute-done.4.recv_ref = bf16[32,64,256]{2,1,0:T(8,128)(2,1)S(1)} collective-permute-done((bf16[32,64,256]{2,1,0:T(8,128)(2,1)S(1)}, bf16[32,64,256]{2,1,0:T(8,128)(2,1)S(1)}, u32[]{:S(2)}, u32[]{:S(2)}) %collective-permute-start.4) | collective-permute-done | bytes 1048608 | tf_op jit(solution)/shard_map/ppermute | solution.py:789
  43.7 1.5 %fill.1 = bf16[32,128,256]{2,1,0:T(8,128)(2,1)} custom-call(s32[2]{0:T(128)S(1)} %copy-done.1, bf16[32,64,256]{2,1,0:T(8,128)(2,1)S(1)} %collective-permute-done.4.recv_ref, bf16[32,128,256]{2,1,0:T(8,128)(2,1)} %get-tuple-element.35.held_hbm), custom_call_target="tpu_custom_call", output_to_operand_aliasing={{}: (2, {})} | custom-call | tf_op jit(solution)/shard_map/fill/pallas_call | solution.py:790
  45.2 18.5 %all-to-all-done.got_ref = bf16[16,264,128]{2,1,0:T(8,128)(2,1)S(1)} async-done(((bf16[16,264,128]{2,1,0:T(8,128)(2,1)}), bf16[16,264,128]{2,1,0:T(8,128)(2,1)S(1)}, u32[]{:S(2)}, u32[]{:S(2)}) %all-to-all-start) | async-done | bytes 1081376 | tf_op jit(solution)/shard_map/all_to_all | solution.py:765
  63.7 3.0 %unpack.1 = bf16[32,64,192]{2,1,0:T(8,128)(2,1)} custom-call(s32[2]{0:T(128)S(1)} %copy-done.1, bf16[16,264,128]{2,1,0:T(8,128)(2,1)S(1)} %all-to-all-done.got_ref), custom_call_target="tpu_custom_call" | custom-call | tf_op jit(solution)/shard_map/unpack/pallas_call | solution.py:801
  (5 shorter events, 0.0 us)
Async XLA Ops:
  0.6 12.6 %collective-permute-start.2 = (bf16[32,128,256]{2,1,0:T(8,128)(2,1)}, bf16[32,128,256]{2,1,0:T(8,128)(2,1)}, u32[]{:S(2)}, u32[]{:S(2)}) collective-permute-start(bf16[32,128,256]{2,1,0:T(8,128)(2,1)} %own_hbm.1), channel_id=1, source_target_pairs={{0,1},{1,0},{2,3},{3,2},{4,5},{5,4},{6,7},{7,6},{8,9},{9,8},{10,11... | collective-permute-start | bytes 6291464 | tf_op jit(solution)/shard_map/ppermute | solution.py:657
  1.3 10.1 %copy-start.1 = (s32[2]{0:T(128)S(1)}, s32[2]{0:T(128)}, u32[]{:S(2)}) copy-start(s32[2]{0:T(128)} %pad_add_fusion.place_ref) | copy-start | bytes 28
  4.4 1.9 %collective-permute-start = (bf16[992,128]{1,0:T(8,128)(2,1)}, bf16[992,128]{1,0:T(8,128)(2,1)S(1)}, u32[]{:S(2)}, u32[]{:S(2)}) collective-permute-start(bf16[992,128]{1,0:T(8,128)(2,1)} %get-tuple-element.20.own_ref), channel_id=1, source_target_pairs={{0,1},{1,0},{2,3},{3,2},{4,5},{5,4},{6,7},{7,6},{8,9},{9,8},{10,11... | collective-permute-start | bytes 761864 | tf_op jit(solution)/shard_map/ppermute | solution.py:677
  7.2 17.4 %collective-permute-start.1 = (bf16[512,128]{1,0:T(8,128)(2,1)S(1)}, bf16[512,128]{1,0:T(8,128)(2,1)S(1)}, u32[]{:S(2)}, u32[]{:S(2)}) collective-permute-start(bf16[512,128]{1,0:T(8,128)(2,1)S(1)} %pad_maximum_fusion), channel_id=1, source_target_pairs={{1,2},{3,4},{5,6},{7,8},{9,10},{11,12},{13,14},{15,16},{17,18},{19... | collective-permute-start | bytes 393224 | tf_op jit(solution)/shard_map/ppermute | solution.py:680
  11.4 1.0 %copy-start = (bf16[992,128]{1,0:T(8,128)(2,1)S(1)}, bf16[992,128]{1,0:T(8,128)(2,1)}, u32[]{:S(2)}) copy-start(bf16[992,128]{1,0:T(8,128)(2,1)} %get-tuple-element.20.own_ref) | copy-start | bytes 761860
  24.6 4.1 %copy-start.2 = (s32[128]{0:T(128)S(1)}, s32[128]{0:T(128)}, u32[]{:S(2)}) copy-start(s32[128]{0:T(128)} %param.8) | copy-start | bytes 1540
  27.2 1.6 %collective-permute-start.3 = (bf16[4,256,128]{2,1,0:T(8,128)(2,1)S(1)}, bf16[4,256,128]{2,1,0:T(8,128)(2,1)S(1)}, u32[]{:S(2)}, u32[]{:S(2)}) collective-permute-start(bf16[4,256,128]{2,1,0:T(8,128)(2,1)S(1)} %get-tuple-element.33), channel_id=1, source_target_pairs={{0,1},{1,0},{2,3},{3,2},{4,5},{5,4},{6,7},{7,6},{8,9},{9,8},{10,11... | collective-permute-start | bytes 786440 | tf_op jit(solution)/shard_map/ppermute | solution.py:744
  31.8 31.9 %all-to-all-start = ((bf16[16,264,128]{2,1,0:T(8,128)(2,1)}), bf16[16,264,128]{2,1,0:T(8,128)(2,1)S(1)}, u32[]{:S(2)}, u32[]{:S(2)}) async-start(bf16[16,264,128]{2,1,0:T(8,128)(2,1)} %pack.1.after_hbm), calls=%async_computation | async-start | bytes 2162688 | tf_op jit(solution)/shard_map/all_to_all | solution.py:765
  40.9 2.7 %collective-permute-start.4 = (bf16[32,64,256]{2,1,0:T(8,128)(2,1)S(1)}, bf16[32,64,256]{2,1,0:T(8,128)(2,1)S(1)}, u32[]{:S(2)}, u32[]{:S(2)}) collective-permute-start(bf16[32,64,256]{2,1,0:T(8,128)(2,1)S(1)} %get-tuple-element.34), channel_id=1, source_target_pairs={{0,1},{1,0},{2,3},{3,2},{4,5},{5,4},{6,7},{7,6},{8,9},{9,8},{10,11... | collective-permute-start | bytes 3145736 | tf_op jit(solution)/shard_map/ppermute | solution.py:789

commit v5 on v4

--- a/solution.py
+++ b/solution.py
@@ -68,10 +68,8 @@
     return x.astype(F32).astype(BF)
 
 
-def edges_kernel(
-    side, place_ref, feat_hbm, valid_ref, wa_ref, wb_ref, wc_ref, send_ref, keep_ref, edge, sems
-):
-    core = place_ref[0]
+def edges_kernel(side, tiles_r, tiles_c, feat_hbm, extra_ref, send_ref, keep_ref, edge, sems):
+    core = lax.axis_index("chan")
     chans, feat_rows, cols = feat_hbm.shape
     copies = []
     for n, at in enumerate((0, feat_rows - BLK)):
@@ -80,20 +78,8 @@
         copies.append(copy)
     flat = chans * HALO
     lanes = send_ref.shape[1]
-    at = flat * cols // lanes
-    for ref in (wa_ref, wb_ref, wc_ref):
-        taps, outs, ins = ref.shape
-        body = ref[...].reshape(taps * outs, ins)
-        send_ref[at : at + taps * outs, :] = jnp.concatenate(
-            [body, jnp.zeros((taps * outs, lanes - ins), BF)], axis=1
-        )
-        at += taps * outs
-    tiles_r, tiles_c = valid_ref.shape
-    masks = mm(as_bf(valid_ref[...]), widen_matrix(tiles_c, cols, side))
-    for n in range(cols // lanes):
-        send_ref[at + n * tiles_r : at + (n + 1) * tiles_r, :] = masks[
-            :, n * lanes : (n + 1) * lanes
-        ].astype(BF)
+    last = extra_ref.shape[0] - 1
+    masks = mm(extra_ref[last, 0:tiles_r, 0:tiles_c], widen_matrix(tiles_c, cols, side))
     row, col = iota((flat, chans * BLK), 0), iota((flat, chans * BLK), 1)
     same = div(row, HALO) == div(col, BLK)
     spot = mod(iota((flat, cols), 0), HALO)
@@ -117,12 +103,12 @@
         keep_ref[n * flat : (n + 1) * flat, :] = keep[:, n * lanes : (n + 1) * lanes]
 
 
-def weights_kernel(at, chans, place_ref, own_ref, oth_ref, w1_ref, w2_ref, wm_ref, mask_ref):
-    core = place_ref[0]
-    allc = 2 * chans
+def weights_kernel(side, tiles_c, own_ref, oth_ref, w1_ref, w2_ref, wm_ref, mask_ref):
+    core = lax.axis_index("chan")
+    chans, allc = own_ref.shape[1:]
 
     def tap(k):
-        return [ref[at + k * chans : at + (k + 1) * chans, 0:allc] for ref in (own_ref, oth_ref)]
+        return [ref[k] for ref in (own_ref, oth_ref)]
 
     for dst, base in ((w1_ref, 0), (w2_ref, 9)):
         total = None
@@ -138,12 +124,9 @@
     )
     order = ones_where(iota((allc, allc), 1) == mod(iota((allc, allc), 0) + chans * core, allc))
     wm_ref[...] = mm_nt(order, tall).astype(BF)
-    tiles_r = mask_ref.shape[0]
-    lanes = own_ref.shape[1]
-    at = own_ref.shape[0] - tiles_r * mask_ref.shape[1] // lanes
-    for n in range(mask_ref.shape[1] // lanes):
-        part = own_ref[at + n * tiles_r : at + (n + 1) * tiles_r, :]
-        mask_ref[:, n * lanes : (n + 1) * lanes] = part.astype(F32)
+    tiles_r, cols = mask_ref.shape
+    last = own_ref.shape[0] - 1
+    mask_ref[...] = mm(own_ref[last, 0:tiles_r, 0:tiles_c], widen_matrix(tiles_c, cols, side))
 
 
 def put(dst, index, x, amount):
@@ -173,9 +156,8 @@
 
 def conv_kernel(
     side,
-    place_ref,
-    own_hbm,
-    oth_hbm,
+    own_ref,
+    oth_ref,
     masks_ref,
     w1,
     w2,
@@ -186,30 +168,17 @@
     xa_ref,
     ha_ref,
     ea_ref,
-    feat,
     xs,
     hs,
     es_ref,
     mask,
-    pa_ref,
-    pb_ref,
-    in_sems,
+    picked,
     out_sem,
 ):
-    core = place_ref[0]
+    core = lax.axis_index("chan")
     rows, allc, cols = es_ref.shape
     chans = allc // 2
     main = rows // BLK
-    copies = []
-    for m in range(main + 1):
-        at = rows - BLK * core if m == main else rows * core + BLK * m
-        for n, ref in enumerate((own_hbm, oth_hbm)):
-            copy = pltpu.make_async_copy(
-                ref.at[:, pl.ds(pl.multiple_of(at, BLK), BLK), :], feat.at[n, m], in_sems.at[n, m]
-            )
-            copy.start()
-            copies.append(copy)
-
     tiles_r = masks_ref.shape[0]
     mask[...] = jnp.zeros(mask.shape, F32)
     mask[pl.ds(side, tiles_r), :] = masks_ref[...]
@@ -218,111 +187,112 @@
     outer_start = jnp.where(core == 0, first_row - HALO, first_row + rows)
     for r in range(HALO):
         xs[outer_start + r] = jnp.zeros(xs.shape[1:], BF)
-    xs[0] = jnp.zeros(xs.shape[1:], BF)
+    zero_row = jnp.zeros(xs.shape[1:], BF)
+    xs[0] = zero_row
     turn = swap_matrix(BLK, BLK)
     few = HALO * BLK
     row, col = iota((few, BLK * BLK), 0), iota((few, BLK * BLK), 1)
     turn_mid = ones_where(
         (mod(row, BLK) == div(col, BLK)) & (div(row, BLK) + (BLK - HALO) * core == mod(col, BLK))
     )
+    half = cols // 2
+    wide = half // side
+    pick = pick_matrix(cols, side)
+    base = side + core * (rows // side)
+    tiles = rows // side
+
+    def lay_block(m):
+        at = rows - BLK * core if m == main else rows * core + BLK * m
+        parts = []
+        for ref in (own_ref, oth_ref):
+            for ch in range(0, chans, BLK):
+                block = ref[ch : ch + BLK, pl.ds(pl.multiple_of(at, BLK), BLK), :]
+                parts.append(mm(turn_mid if m == main else turn, block.reshape(BLK * BLK, cols)))
+        return parts
+
+    def lay_row(parts, r, at):
+        put(xs, at, jnp.concatenate([p[r * BLK : (r + 1) * BLK] for p in parts], axis=0), 1)
+
     mid_start = jnp.where(core == 0, first_row + rows, first_row - HALO)
-    for m in range(main + 1):
-        for copy in copies[2 * m : 2 * m + 2]:
-            copy.wait()
-        parts = []
-        for n in range(2):
-            for ch in range(0, chans, BLK):
-                block = feat[n, m, ch : ch + BLK].reshape(BLK * BLK, cols)
-                parts.append(mm(turn_mid if m == main else turn, block))
-        at = mid_start if m == main else first_row + m * BLK
-        for r in range(HALO if m == main else BLK):
-            x = jnp.concatenate([p[r * BLK : (r + 1) * BLK] for p in parts], axis=0)
-            put(xs, at + r, x, 1)
-
-    base = side + core * (rows // side)
-    total_steps = rows // side + 1
-    tiles = 3 if total_steps % 3 == 0 else 1
-    group = tiles * side
-
-    def lines(step, ahead):
-        return [mask[pl.ds(base + step * tiles + k - 1, 1), :] for k in range(tiles + ahead)]
-
-    pa_ref[...] = jnp.zeros(pa_ref.shape, F32)
-    pb_ref[...] = jnp.zeros(pb_ref.shape, F32)
-
-    def first(step, carry):
-        pa, pb = pa_ref[0], pb_ref[0]
-        flag = lines(step, 1)
-        for j in range(group):
-            q = step * group + j
-            y = mm(w1[...], xs[q])
-            total = pa + y[2 * allc :]
-            pa = pb + y[allc : 2 * allc]
-            pb = y[:allc]
-            h = jnp.maximum(total * flag[(j + 2) // side], 0.0)
-            put(hs, q, h.astype(BF), 2)
-        pa_ref[0] = pa
-        pb_ref[0] = pb
-        return carry
-
-    lax.fori_loop(0, total_steps // tiles, first, 0)
-
-    pa_ref[0] = jnp.zeros((allc, cols), F32)
-    pb_ref[0] = jnp.zeros((allc, cols), F32)
-
-    def second(step, carry):
-        pa, pb = [pa_ref[0], pa_ref[1]], [pb_ref[0], pb_ref[1]]
-        flag = lines(step, 0)
-        for j in range(group):
-            q = step * group + j
-            i = j % 2
-            z = mm(w2[...], hs[q])
-            total = pa[i] + z[2 * allc :]
-            pa[i] = pb[i] + z[allc : 2 * allc]
-            pb[i] = z[:allc]
-            x = xs[jnp.maximum(q - 3, 0), allc : 2 * allc, :].astype(F32)
-            es_ref[jnp.maximum(q - side, 0)] = (flag[j // side] * (x + total)).astype(BF)
-        for i in range(2):
-            pa_ref[i] = pa[i]
-            pb_ref[i] = pb[i]
-        return carry
-
-    lax.fori_loop(0, total_steps // tiles, second, 0)
-
-    out = pltpu.make_async_copy(es_ref, es_hbm.at[pl.ds(0, rows)], out_sem)
-    out.start()
+    parts = lay_block(main)
+    for r in range(HALO):
+        lay_row(parts, r, mid_start + r)
+
+    def line(k):
+        return mask[pl.ds(base + k, 1), :]
+
+    none = jnp.zeros((allc, cols), F32)
+    first_sums = [none, none]
+    second_sums = [[none, none], [none, none]]
+
+    def first(q):
+        pa, pb = first_sums
+        y = mm(w1[...], xs[q])
+        total = pa + y[2 * allc :]
+        first_sums[:] = [pb + y[allc : 2 * allc], y[:allc]]
+        h = jnp.maximum(total * line((q + 2) // side - 1), 0.0)
+        put(hs, q, h.astype(BF), 2)
+
+    def second(q):
+        pa, pb = second_sums[q % 2]
+        z = mm(w2[...], hs[q])
+        total = pa + z[2 * allc :]
+        second_sums[q % 2] = [pb + z[allc : 2 * allc], z[:allc]]
+        if q >= side:
+            x = xs[q - 3, allc : 2 * allc, :].astype(F32)
+            es_ref[q - side] = (line(q // side - 1) * (x + total)).astype(BF)
+
+    def pick_tile(tile):
+        tall = es_ref[tile * side : (tile + 1) * side].reshape(side * allc, cols)
+        picked[tile * side * allc : (tile + 1) * side * allc, :] = mm(tall, pick).astype(BF)
+
+    def merge_tile(tile, k):
+        g = tile // 2 + core * (rows // (2 * side))
+
+        def rows_of(n):
+            at = (tile * side + 2 * n) * allc
+            return picked[at : at + 2 * allc, :]
+
+        for n, piece in enumerate(merge_pairs(wm[...], rows_of, (k, k + 1), g * wide, half)):
+            u = (side // 2) * (tile % 2) + k + n
+            mown_ref[tile // 2, u * chans : (u + 1) * chans, :] = piece[:chans].astype(BF)
+            moth_ref[tile // 2, u * chans : (u + 1) * chans, :] = piece[chans:].astype(BF)
+
+    outs = []
+    lag = 4
+    total_rows = rows + side
+    for s in range(-1, total_rows + 3 * lag + 2 * side):
+        if 0 <= s < rows:
+            if s % BLK == 0:
+                parts = lay_block(s // BLK)
+            lay_row(parts, s % BLK, first_row + s)
+        q = s + first_row - lag
+        if 0 <= q < total_rows:
+            first(q)
+        q -= lag
+        if 0 <= q < total_rows:
+            second(q)
+        done = q - 2 * side
+        if done >= 0 and done % side == 2 and done // side < tiles:
+            at = pl.ds(done // side * side, side)
+            out = pltpu.make_async_copy(es_ref.at[at], es_hbm.at[at], out_sem.at[done // side])
+            out.start()
+            outs.append(out)
+            pick_tile(done // side)
+        if done >= 0 and done % side in (4, 6) and done // side < tiles:
+            merge_tile(done // side, 0 if done % side == 4 else 2)
 
     for k in range(3):
         xa_ref[k] = xs[first_row + (rows - 3) * core + k]
     for k in range(4):
         ha_ref[k] = hs[jnp.where(core == 0, 7, rows + 1) + k]
     ea_ref[0] = es_ref[jnp.where(core == 0, 3, rows - 4)]
-
-    half = cols // 2
-    wide = half // side
-    pick = pick_matrix(cols, side)
-    picked = hs.reshape(hs.shape[0] * hs.shape[1], cols)
-    for tile in range(rows // side):
-        tall = es_ref[tile * side : (tile + 1) * side].reshape(side * allc, cols)
-        picked[tile * side * allc : (tile + 1) * side * allc, :] = mm(tall, pick).astype(BF)
-    for tile in range(rows // side):
-        g = tile // 2 + core * (rows // (2 * side))
-
-        def rows_of(k, tile=tile):
-            at = (tile * side + 2 * k) * allc
-            return picked[at : at + 2 * allc, :]
-
-        for k in range(0, side // 2, 2):
-            for n, piece in enumerate(merge_pairs(wm[...], rows_of, (k, k + 1), g * wide, half)):
-                u = (side // 2) * (tile % 2) + k + n
-                mown_ref[tile // 2, u * chans : (u + 1) * chans, :] = piece[:chans].astype(BF)
-                moth_ref[tile // 2, u * chans : (u + 1) * chans, :] = piece[chans:].astype(BF)
-    out.wait()
+    for out in outs:
+        out.wait()
 
 
 def border_kernel(
     rows,
-    place_ref,
     outer_ref,
     masks_ref,
     w1,
@@ -342,7 +312,7 @@
     e4,
     sem,
 ):
-    core = place_ref[0]
+    core = lax.axis_index("chan")
     _, allc, cols = ea_ref.shape
     chans = allc // 2
     lanes = outer_ref.shape[1]
@@ -408,8 +378,8 @@
     copy.wait()
 
 
-def restore_kernel(place_ref, es_hbm, after_hbm, enh_hbm, eoth_ref, es_ref, own, sem, in_sems):
-    core = place_ref[0]
+def restore_kernel(es_hbm, after_hbm, enh_hbm, eoth_ref, es_ref, own, sem, in_sems):
+    core = lax.axis_index("chan")
     rows, allc, cols = es_ref.shape
     chans = allc // 2
     copies = []
@@ -433,8 +403,8 @@
     copy.wait()
 
 
-def fill_kernel(place_ref, recv_ref, held_hbm, enh_hbm, sem):
-    core = place_ref[0]
+def fill_kernel(recv_ref, held_hbm, enh_hbm, sem):
+    core = lax.axis_index("chan")
     rows = recv_ref.shape[1]
     copy = pltpu.make_async_copy(
         recv_ref, enh_hbm.at[:, pl.ds(pl.multiple_of((1 - core) * rows, rows), rows), :], sem
@@ -455,9 +425,9 @@
 
 
 def pack_kernel(
-    side, slots, place_ref, owner_ref, mown_ref, mrecv_ref, out_ref, arr, lhs, mid, code_ref
+    side, slots, owner_ref, mown_ref, mrecv_ref, out_ref, arr, lhs, mid, code_ref
 ):
-    core, tile = place_ref[0], place_ref[1]
+    core, tile = lax.axis_index("chan"), lax.axis_index("tiles")
     count = owner_ref.shape[1]
     mine, rows, lanes = mown_ref.shape
     blocks, all_rows, _ = out_ref.shape
@@ -561,8 +531,8 @@
     return jnp.where(same, jnp.ones_like(goal), jnp.zeros_like(goal))
 
 
-def unpack_kernel(side, slots, place_ref, got_ref, out_ref, picked, data):
-    tile = place_ref[1]
+def unpack_kernel(side, slots, got_ref, out_ref, picked, data):
+    tile = lax.axis_index("tiles")
     blocks, all_rows, lanes = got_ref.shape
     chans, cells, cap = out_ref.shape
     rows = side * chans
@@ -644,55 +614,47 @@
     lanes = 128
     blocks = devices * slots * side // lanes
     fold = devices // blocks
-    core = lax.axis_index("chan")
-    place = jnp.stack([core, lax.axis_index("tiles")]).astype(jnp.int32)
     swap = [(0, 1), (1, 0)]
     vmem = pl.BlockSpec(memory_space=pltpu.VMEM)
-    smem = pl.BlockSpec(memory_space=pltpu.SMEM)
     hbm = pl.BlockSpec(memory_space=pltpu.HBM)
 
     def limit(mib):
         return pltpu.CompilerParams(vmem_limit_bytes=int(mib * 1024) << 10)
 
     feat_oth = lax.ppermute(features, "chan", swap)
-    w_mergt = jnp.swapaxes(w_merge, 1, 2)
+    flags = jnp.pad(tile_valid.astype(BF), ((0, chans - tile_rows), (0, allc - tile_cols)))
+    extra = jnp.concatenate([w_first, w_second, jnp.swapaxes(w_merge, 1, 2), flags[None]], axis=0)
+    extra_oth = lax.ppermute(extra, "chan", swap)
     edge_rows = chans * HALO * col_count // lanes
-    tap_rows = (w_first.shape[0] + w_second.shape[0] + w_merge.shape[0]) * chans
-    mask_rows = tile_rows * col_count // lanes
     send, keep = pl.pallas_call(
-        functools.partial(edges_kernel, side),
-        out_shape=(
-            jax.ShapeDtypeStruct((edge_rows + tap_rows + mask_rows, lanes), BF),
-            jax.ShapeDtypeStruct((edge_rows, lanes), BF),
-        ),
-        in_specs=[smem, hbm] + [vmem] * 4,
+        functools.partial(edges_kernel, side, tile_rows, tile_cols),
+        out_shape=(jax.ShapeDtypeStruct((edge_rows, lanes), BF),) * 2,
+        in_specs=[hbm, vmem],
         out_specs=(vmem,) * 2,
         scratch_shapes=[
             pltpu.VMEM((2, chans, BLK, col_count), BF),
             pltpu.SemaphoreType.DMA((2,)),
         ],
-        compiler_params=limit(63.9),
+        compiler_params=limit(52),
         name="edges",
-    )(place, features, tile_valid, w_first, w_second, w_mergt)
+    )(features, extra)
     sent = lax.ppermute(send, "chan", swap)
     cross = [(2 * t + 1, 2 * t + 2) for t in range(devices - 1)]
     cross += [(2 * t, 2 * t - 1) for t in range(1, devices)]
-    outer = lax.ppermute(
-        jnp.concatenate([keep, sent[:edge_rows]], axis=0), ("tiles", "chan"), cross
-    )
+    outer = lax.ppermute(jnp.concatenate([keep, sent], axis=0), ("tiles", "chan"), cross)
     w1, w2, wm, masks = pl.pallas_call(
-        functools.partial(weights_kernel, edge_rows, chans),
+        functools.partial(weights_kernel, side, tile_cols),
         out_shape=(
             jax.ShapeDtypeStruct((3 * allc, 3 * allc), BF),
             jax.ShapeDtypeStruct((3 * allc, 3 * allc), BF),
             jax.ShapeDtypeStruct((allc, 4 * allc), BF),
             jax.ShapeDtypeStruct((tile_rows, col_count), F32),
         ),
-        in_specs=[smem, vmem, vmem],
+        in_specs=[vmem, vmem],
         out_specs=(vmem,) * 4,
         compiler_params=limit(6),
         name="weights",
-    )(place, send, sent)
+    )(extra, extra_oth)
 
     parent_rows = tile_rows // 4
     held_rows = rows * pl.cdiv(44 << 20, rows * allc * col_count * 2)
@@ -706,22 +668,19 @@
             jax.ShapeDtypeStruct((4, 3 * allc, col_count), BF),
             jax.ShapeDtypeStruct((1, allc, col_count), BF),
         ),
-        in_specs=[smem, hbm, hbm] + [vmem] * 4,
+        in_specs=[vmem] * 6,
         out_specs=(hbm,) + (vmem,) * 5,
         scratch_shapes=[
-            pltpu.VMEM((2, rows // BLK + 1, chans, BLK, col_count), BF),
             pltpu.VMEM((rows + 16, 3 * allc, col_count), BF),
             pltpu.VMEM((rows + side, 3 * allc, col_count), BF),
             pltpu.VMEM((rows, allc, col_count), BF),
             pltpu.VMEM((tile_rows + 2 * side, col_count), F32),
-            pltpu.VMEM((2, allc, col_count), F32),
-            pltpu.VMEM((2, allc, col_count), F32),
-            pltpu.SemaphoreType.DMA((2, rows // BLK + 1)),
-            pltpu.SemaphoreType.DMA,
+            pltpu.VMEM((rows * allc, col_count), BF),
+            pltpu.SemaphoreType.DMA((rows // side,)),
         ],
-        compiler_params=limit(52),
+        compiler_params=limit(36),
         name="conv",
-    )(place, features, feat_oth, masks, w1, w2, wm)
+    )(features, feat_oth, masks, w1, w2, wm)
     es, m_own, m_oth = pl.pallas_call(
         functools.partial(border_kernel, rows),
         out_shape=(
@@ -729,7 +688,7 @@
             jax.ShapeDtypeStruct((parent_rows, side * chans, col_count // 2), BF),
             jax.ShapeDtypeStruct((parent_rows, side * chans, col_count // 2), BF),
         ),
-        in_specs=[smem] + [vmem] * 10 + [hbm],
+        in_specs=[vmem] * 10 + [hbm],
         out_specs=(hbm, vmem, vmem),
         scratch_shapes=[
             pltpu.VMEM((5, 3 * allc, col_count), BF),
@@ -737,16 +696,16 @@
             pltpu.VMEM((4, allc, col_count), BF),
             pltpu.SemaphoreType.DMA,
         ],
-        input_output_aliases={11: 0},
+        input_output_aliases={10: 0},
         compiler_params=limit(16),
         name="border",
-    )(place, outer, masks, w1, w2, wm, xa, ha, ea, m_own, m_oth, es)
+    )(outer, masks, w1, w2, wm, xa, ha, ea, m_own, m_oth, es)
     m_recv = lax.ppermute(m_oth, "chan", swap)
     all_rows = side * chans + 8
     packed = pl.pallas_call(
         functools.partial(pack_kernel, side, slots),
         out_shape=jax.ShapeDtypeStruct((blocks, all_rows, lanes), BF),
-        in_specs=[smem, vmem, vmem, vmem],
+        in_specs=[vmem, vmem, vmem],
         out_specs=vmem,
         scratch_shapes=[
             pltpu.VMEM((2 * parent_rows, side * chans, lanes), BF),
@@ -756,7 +715,7 @@
         ],
         compiler_params=limit(16),
         name="pack",
-    )(place, parent_owner[None, :], m_own, m_recv)
+    )(parent_owner[None, :], m_own, m_recv)
 
     def to_peers(x):
         if fold > 1:
@@ -775,7 +734,7 @@
             jax.ShapeDtypeStruct((chans, row_count, col_count), BF),
             jax.ShapeDtypeStruct((chans, rows, col_count), BF),
         ),
-        in_specs=[smem, hbm, hbm],
+        in_specs=[hbm, hbm],
         out_specs=(hbm, vmem),
         scratch_shapes=[
             pltpu.VMEM((rows, allc, col_count), BF),
@@ -785,23 +744,23 @@
         ],
         compiler_params=limit(12),
         name="restore",
-    )(place, es, packed)
+    )(es, packed)
     e_recv = lax.ppermute(e_oth, "chan", swap)
     enhanced = pl.pallas_call(
         fill_kernel,
         out_shape=jax.ShapeDtypeStruct((chans, row_count, col_count), BF),
-        in_specs=[smem, vmem, hbm],
+        in_specs=[vmem, hbm],
         out_specs=hbm,
         scratch_shapes=[pltpu.SemaphoreType.DMA],
-        input_output_aliases={2: 0},
+        input_output_aliases={1: 0},
         compiler_params=limit(6),
         name="fill",
-    )(place, e_recv, held)
+    )(e_recv, held)
     room = pl.cdiv(own_cap, lanes) * lanes
     parents = pl.pallas_call(
         functools.partial(unpack_kernel, side, slots),
         out_shape=jax.ShapeDtypeStruct((chans, side * side, own_cap), BF),
-        in_specs=[smem, vmem],
+        in_specs=[vmem],
         out_specs=vmem,
         scratch_shapes=[
             pltpu.VMEM((side, side * chans, room), BF),
@@ -809,7 +768,7 @@
         ],
         compiler_params=limit(24),
         name="unpack",
-    )(place, got)
+    )(got)
     return enhanced, jnp.swapaxes(parents, 1, 2)
 
 

time: 67 us -> 59.2 us (0.88)
  Pallas kernels: 29 us -> 19.8 us
  waiting for transfers between devices: 24 us -> 25.9 us
  local copies, waits for them, and re-layouts: 0.96 us -> 0.02 us
    pallas_call x1, Pallas kernels: 11.4 us -> 7.27 us  [on_device(): pl.pallas_call(functools.partial(conv_kernel, side), out_shape=(jax.Shape...]
    pallas_call x2, Pallas kernels: 3.93 us -> 1.71 us  [the longest x1 1.41 us: on_device(): pl.pallas_call(functools.partial(edges_kernel, side, tile_rows, tile_cols...]
    ppermute x1 -> x2, waiting for transfers between devices: 0.01 us -> 1.42 us  [the longest x1 1.42 us: on_device(): extra_oth = lax.ppermute(extra, 'chan', swap)]
    all_to_all x1, waiting for transfers between devices: 18.5 us -> 19.6 us  [to_peers(): x = lax.all_to_all(x, 'tiles', split_axis=0, concat_axis=0, tiled=True)]
    unnamed x6 -> x4, local copies, waits for them, and re-layouts: 0.95 us -> 0.01 us
    convert_element_type x0 -> x1, other arithmetic: none -> 0.83 us  [on_device(): tile_valid.astype(BF)]
    pallas_call x1, Pallas kernels: 2.51 us -> 1.82 us  [on_device(): pl.pallas_call(functools.partial(border_kernel, rows), out_shape=(jax.Sha...]
    ppermute x1 -> x2, starting transfers between devices: 4.22 us -> 4.27 us  [the longest x1 4.2 us: on_device(): lax.ppermute(jnp.concatenate([keep, sent], axis=0), ('tiles', 'chan'), cr...]
  transfers between devices with their start and end apart: 6 -> 7, of which waited for: 4 -> 5; matrix products, arithmetic and copies ran while one was open for 2% -> 3% of each run, Pallas kernels for 31% -> 22%
where the time goes in v5:
time: 59.2 us; the launch traced here: 58.9 us
  waiting for transfers between devices  25.9 us (44%)
  Pallas kernels  19.8 us (33%)
  starting transfers between devices  10.5 us (18%)
  other arithmetic  1.83 us (3%)
  between operations  0.76 us (1%)
    all_to_all x1, waiting for transfers between devices, to_peers(): x = lax.all_to_all(x, 'tiles', split_axis=0, concat_axis=0, tiled=True)  19.6 us
    pallas_call x1, Pallas kernels, on_device(): pl.pallas_call(functools.partial(conv_kernel, side), out_shape=(jax.Shape...  7.27 us
    all_to_all x1, starting transfers between devices, to_peers(): x = lax.all_to_all(x, 'tiles', split_axis=0, concat_axis=0, tiled=True)  5.42 us
    ppermute x1, starting transfers between devices, on_device(): lax.ppermute(jnp.concatenate([keep, sent], axis=0), ('tiles', 'chan'), cr...  4.2 us
    pallas_call x1, Pallas kernels, on_device(): pl.pallas_call(restore_kernel, out_shape=(jax.ShapeDtypeStruct((chans, ro...  3.21 us
    ppermute x1, waiting for transfers between devices, on_device(): e_recv = lax.ppermute(e_oth, 'chan', swap)  2.65 us
    pallas_call x1, Pallas kernels, on_device(): pl.pallas_call(functools.partial(pack_kernel, side, slots), out_shape=jax...  2.44 us
    pallas_call x1, Pallas kernels, on_device(): pl.pallas_call(functools.partial(unpack_kernel, side, slots), out_shape=j...  2.42 us
  transfers between devices with their start and end apart: 7, of which 5 were waited for; matrix products, arithmetic and copies ran while one was open for 3% of the time, Pallas kernels for 22%

profile of v5, /device:TPU:8, one launch (start us, length us, event | category | flops | bytes accessed | tf_op | source)
XLA Modules:
  0.0 58.9 jit_solution(9501192961181213945)
XLA Ops:
  0.6 0.0 copy-start
  0.6 0.1 collective-permute-start.3
  0.7 0.8 %convert_element_type.5 = bf16[16,32]{1,0:T(8,128)(2,1)S(1)} convert(s32[16,32]{1,0:T(8,128)} %param.7) | non-fusion elementwise | flops 512 | bytes 3072 | tf_op jit(solution)/shard_map/convert_element_type | solution.py:625
  1.6 1.0 %pad_maximum_fusion.extra_ref.own_ref = bf16[23,32,64]{2,1,0:T(8,128)(2,1)S(1)} fusion(bf16[1,32,64]{2,1,0:T(8,128)(2,1)S(1)} %pad_bitcast_fusion, bf16[4,32,64]{2,1,0:T(8,128)(2,1)} %bitcast.7, bf16[9,32,64]{2,1,0:T(8,128)(2,1)} %param.10, bf16[9,32,64]{2,1,0:T(8,128)(2,1)} %param.9), kind=kLoop, calls=%fused_computation | loop fusion | flops 141312 | bytes 188416 | tf_op jit(solution)/shard_map/concatenate | solution.py:626
  2.6 1.4 %edges.1 = (bf16[256,128]{1,0:T(8,128)(2,1)S(1)}, bf16[256,128]{1,0:T(8,128)(2,1)S(1)}) custom-call(bf16[32,128,256]{2,1,0:T(8,128)(2,1)} %own_ref.1, bf16[23,32,64]{2,1,0:T(8,128)(2,1)S(1)} %pad_maximum_fusion.extra_ref.own_ref), custom_call_target="tpu_custom_call" | custom-call | tf_op jit(solution)/shard_map/edges/pallas_call | solution.py:629
  4.0 0.4 collective-permute-start
  4.4 0.9 %collective-permute-done = bf16[256,128]{1,0:T(8,128)(2,1)S(1)} collective-permute-done((bf16[256,128]{1,0:T(8,128)(2,1)S(1)}, bf16[256,128]{1,0:T(8,128)(2,1)S(1)}, u32[]{:S(2)}, u32[]{:S(2)}) %collective-permute-start) | collective-permute-done | bytes 65568 | tf_op jit(solution)/shard_map/ppermute | solution.py:641
  5.3 4.2 %collective-permute-start.1 = (bf16[512,128]{1,0:T(8,128)(2,1)S(1)}, bf16[512,128]{1,0:T(8,128)(2,1)S(1)}, u32[]{:S(2)}, u32[]{:S(2)}) collective-permute-start(bf16[512,128]{1,0:T(8,128)(2,1)S(1)} %pad_maximum_fusion.1), channel_id=1, source_target_pairs={{1,2},{3,4},{5,6},{7,8},{9,10},{11,12},{13,14},{15,16},{17,18},{19... | collective-permute-start | bytes 393224 | tf_op jit(solution)/shard_map/ppermute | solution.py:644
  9.5 0.1 collective-permute-start.2
  9.6 1.4 %collective-permute-done.2.oth_ref = bf16[23,32,64]{2,1,0:T(8,128)(2,1)S(1)} collective-permute-done((bf16[23,32,64]{2,1,0:T(8,128)(2,1)S(1)}, bf16[23,32,64]{2,1,0:T(8,128)(2,1)S(1)}, u32[]{:S(2)}, u32[]{:S(2)}) %collective-permute-start.2) | collective-permute-done | bytes 94240 | tf_op jit(solution)/shard_map/ppermute | solution.py:627
  11.0 0.3 weights.1
  11.4 7.3 %conv.1 = (bf16[1408,64,256]{2,1,0:T(8,128)(2,1)}, bf16[4,256,128]{2,1,0:T(8,128)(2,1)S(1)}, bf16[4,256,128]{2,1,0:T(8,128)(2,1)S(1)}, bf16[3,192,256]{2,1,0:T(8...) custom-call(bf16[32,128,256]{2,1,0:T(8,128)(2,1)S(1)} %copy-done, ...), custom_call_target="tpu_custom_call" | custom-call | tf_op jit(solution)/shard_map/conv/pallas_call | solution.py:661
  18.6 0.0 copy-start.1
  18.7 1.8 %border.1 = (bf16[1408,64,256]{2,1,0:T(8,128)(2,1)}, bf16[4,256,128]{2,1,0:T(8,128)(2,1)S(1)}, bf16[4,256,128]{2,1,0:T(8,128)(2,1)S(1)}) custom-call(bf16[512,128]{1,0:T(8,128)(2,1)S(1)} %collective-permute-done.1.outer_ref, f32[16,256]{1,0:T(8,128)S(1)} %get-tuple-element.21.masks_ref, ...), custom_call_target="tpu_custom_call", output_to_operand_aliasing={{0}: (10, {})} | custom-call | tf_op jit(solution)/shard_map/border/pallas_call | solution.py:684
  20.5 0.2 collective-permute-start.4
  20.7 1.4 %collective-permute-done.4.mrecv_ref = bf16[4,256,128]{2,1,0:T(8,128)(2,1)S(1)} collective-permute-done((bf16[4,256,128]{2,1,0:T(8,128)(2,1)S(1)}, bf16[4,256,128]{2,1,0:T(8,128)(2,1)S(1)}, u32[]{:S(2)}, u32[]{:S(2)}) %collective-permute-start.4) | collective-permute-done | bytes 262176 | tf_op jit(solution)/shard_map/ppermute | solution.py:703
  22.1 2.4 %pack.1.after_hbm = bf16[16,264,128]{2,1,0:T(8,128)(2,1)} custom-call(s32[1,128]{1,0:T(1,128)S(1)} %bitcast.5, bf16[4,256,128]{2,1,0:T(8,128)(2,1)S(1)} %get-tuple-element.32.mown_ref, bf16[4,256,128]{2,1,0:T(8,128)(2,1)S(1)} %collective-permute-done.4.mrecv_ref), custom_call_target="tpu_custom_call" | custom-call | tf_op jit(solution)/shard_map/pack/pallas_call | solution.py:705
  24.5 5.4 %all-to-all-start = ((bf16[16,264,128]{2,1,0:T(8,128)(2,1)}), bf16[16,264,128]{2,1,0:T(8,128)(2,1)S(1)}, u32[]{:S(2)}, u32[]{:S(2)}) async-start(bf16[16,264,128]{2,1,0:T(8,128)(2,1)} %pack.1.after_hbm), calls=%async_computation | async-start | bytes 2162688 | tf_op jit(solution)/shard_map/all_to_all | solution.py:724
  29.9 3.2 %restore.1 = (bf16[32,128,256]{2,1,0:T(8,128)(2,1)}, bf16[32,64,256]{2,1,0:T(8,128)(2,1)S(1)}) custom-call(bf16[1408,64,256]{2,1,0:T(8,128)(2,1)} %get-tuple-element.31.es_hbm, bf16[16,264,128]{2,1,0:T(8,128)(2,1)} %pack.1.after_hbm), custom_call_target="tpu_custom_call" | custom-call | tf_op jit(solution)/shard_map/restore/pallas_call | solution.py:731
  33.2 0.1 collective-permute-start.5
  33.2 2.6 %collective-permute-done.5.recv_ref = bf16[32,64,256]{2,1,0:T(8,128)(2,1)S(1)} collective-permute-done((bf16[32,64,256]{2,1,0:T(8,128)(2,1)S(1)}, bf16[32,64,256]{2,1,0:T(8,128)(2,1)S(1)}, u32[]{:S(2)}, u32[]{:S(2)}) %collective-permute-start.5) | collective-permute-done | bytes 1048608 | tf_op jit(solution)/shard_map/ppermute | solution.py:748
  35.9 1.0 %fill.1 = bf16[32,128,256]{2,1,0:T(8,128)(2,1)} custom-call(bf16[32,64,256]{2,1,0:T(8,128)(2,1)S(1)} %collective-permute-done.5.recv_ref, bf16[32,128,256]{2,1,0:T(8,128)(2,1)} %get-tuple-element.35.held_hbm), custom_call_target="tpu_custom_call", output_to_operand_aliasing={{}: (1, {})} | custom-call | tf_op jit(solution)/shard_map/fill/pallas_call | solution.py:749
  36.9 19.6 %all-to-all-done.got_ref = bf16[16,264,128]{2,1,0:T(8,128)(2,1)S(1)} async-done(((bf16[16,264,128]{2,1,0:T(8,128)(2,1)}), bf16[16,264,128]{2,1,0:T(8,128)(2,1)S(1)}, u32[]{:S(2)}, u32[]{:S(2)}) %all-to-all-start) | async-done | bytes 1081376 | tf_op jit(solution)/shard_map/all_to_all | solution.py:724
  56.5 2.4 %unpack.1 = bf16[32,64,192]{2,1,0:T(8,128)(2,1)} custom-call(bf16[16,264,128]{2,1,0:T(8,128)(2,1)S(1)} %all-to-all-done.got_ref), custom_call_target="tpu_custom_call" | custom-call | tf_op jit(solution)/shard_map/unpack/pallas_call | solution.py:760
  (6 shorter events, 0.0 us)
Async XLA Ops:
  0.6 10.7 %copy-start = (bf16[32,128,256]{2,1,0:T(8,128)(2,1)S(1)}, bf16[32,128,256]{2,1,0:T(8,128)(2,1)}, u32[]{:S(2)}) copy-start(bf16[32,128,256]{2,1,0:T(8,128)(2,1)} %own_ref.1) | copy-start | bytes 6291460
  0.6 10.7 %collective-permute-start.3 = (bf16[32,128,256]{2,1,0:T(8,128)(2,1)}, bf16[32,128,256]{2,1,0:T(8,128)(2,1)S(1)}, u32[]{:S(2)}, u32[]{:S(2)}) collective-permute-start(bf16[32,128,256]{2,1,0:T(8,128)(2,1)} %own_ref.1), channel_id=1, source_target_pairs={{0,1},{1,0},{2,3},{3,2},{4,5},{5,4},{6,7},{7,6},{8,9},{9,8},{10,11... | collective-permute-start | bytes 6291464 | tf_op jit(solution)/shard_map/ppermute | solution.py:624
  4.0 1.3 %collective-permute-start = (bf16[256,128]{1,0:T(8,128)(2,1)S(1)}, bf16[256,128]{1,0:T(8,128)(2,1)S(1)}, u32[]{:S(2)}, u32[]{:S(2)}) collective-permute-start(bf16[256,128]{1,0:T(8,128)(2,1)S(1)} %get-tuple-element.20), channel_id=1, source_target_pairs={{0,1},{1,0},{2,3},{3,2},{4,5},{5,4},{6,7},{7,6},{8,9},{9,8},{10,11... | collective-permute-start | bytes 196616 | tf_op jit(solution)/shard_map/ppermute | solution.py:641
  5.3 13.3 %collective-permute-start.1 = (bf16[512,128]{1,0:T(8,128)(2,1)S(1)}, bf16[512,128]{1,0:T(8,128)(2,1)S(1)}, u32[]{:S(2)}, u32[]{:S(2)}) collective-permute-start(bf16[512,128]{1,0:T(8,128)(2,1)S(1)} %pad_maximum_fusion.1), channel_id=1, source_target_pairs={{1,2},{3,4},{5,6},{7,8},{9,10},{11,12},{13,14},{15,16},{17,18},{19... | collective-permute-start | bytes 393224 | tf_op jit(solution)/shard_map/ppermute | solution.py:644
  9.5 1.5 %collective-permute-start.2 = (bf16[23,32,64]{2,1,0:T(8,128)(2,1)S(1)}, bf16[23,32,64]{2,1,0:T(8,128)(2,1)S(1)}, u32[]{:S(2)}, u32[]{:S(2)}) collective-permute-start(bf16[23,32,64]{2,1,0:T(8,128)(2,1)S(1)} %pad_maximum_fusion.extra_ref.own_ref), channel_id=1, source_target_pairs={{0,1},{1,0},{2,3},{3,2},{4,5},{5,4},{6,7},{7,6},{8,9},{9,8},{10,11... | collective-permute-start | bytes 282632 | tf_op jit(solution)/shard_map/ppermute | solution.py:627
  18.6 3.4 %copy-start.1 = (s32[128]{0:T(128)S(1)}, s32[128]{0:T(128)}, u32[]{:S(2)}) copy-start(s32[128]{0:T(128)} %param.8) | copy-start | bytes 1540
  20.5 1.6 %collective-permute-start.4 = (bf16[4,256,128]{2,1,0:T(8,128)(2,1)S(1)}, bf16[4,256,128]{2,1,0:T(8,128)(2,1)S(1)}, u32[]{:S(2)}, u32[]{:S(2)}) collective-permute-start(bf16[4,256,128]{2,1,0:T(8,128)(2,1)S(1)} %get-tuple-element.33), channel_id=1, source_target_pairs={{0,1},{1,0},{2,3},{3,2},{4,5},{5,4},{6,7},{7,6},{8,9},{9,8},{10,11... | collective-permute-start | bytes 786440 | tf_op jit(solution)/shard_map/ppermute | solution.py:703
  24.5 31.9 %all-to-all-start = ((bf16[16,264,128]{2,1,0:T(8,128)(2,1)}), bf16[16,264,128]{2,1,0:T(8,128)(2,1)S(1)}, u32[]{:S(2)}, u32[]{:S(2)}) async-start(bf16[16,264,128]{2,1,0:T(8,128)(2,1)} %pack.1.after_hbm), calls=%async_computation | async-start | bytes 2162688 | tf_op jit(solution)/shard_map/all_to_all | solution.py:724
  33.2 2.7 %collective-permute-start.5 = (bf16[32,64,256]{2,1,0:T(8,128)(2,1)S(1)}, bf16[32,64,256]{2,1,0:T(8,128)(2,1)S(1)}, u32[]{:S(2)}, u32[]{:S(2)}) collective-permute-start(bf16[32,64,256]{2,1,0:T(8,128)(2,1)S(1)} %get-tuple-element.34), channel_id=1, source_target_pairs={{0,1},{1,0},{2,3},{3,2},{4,5},{5,4},{6,7},{7,6},{8,9},{9,8},{10,11... | collective-permute-start | bytes 3145736 | tf_op jit(solution)/shard_map/ppermute | solution.py:748

commit v6 on v5

--- a/solution.py
+++ b/solution.py
@@ -6,6 +6,7 @@
 from jax.experimental import pallas as pl
 from jax.experimental.pallas import tpu as pltpu
 from jax.sharding import PartitionSpec as P
+
 
 BF = jnp.bfloat16
 F32 = jnp.float32
@@ -68,7 +69,7 @@
     return x.astype(F32).astype(BF)
 
 
-def edges_kernel(side, tiles_r, tiles_c, feat_hbm, extra_ref, send_ref, keep_ref, edge, sems):
+def edges_kernel(side, feat_hbm, valid_ref, send_ref, keep_ref, masks_ref, edge, sems):
     core = lax.axis_index("chan")
     chans, feat_rows, cols = feat_hbm.shape
     copies = []
@@ -78,8 +79,9 @@
         copies.append(copy)
     flat = chans * HALO
     lanes = send_ref.shape[1]
-    last = extra_ref.shape[0] - 1
-    masks = mm(extra_ref[last, 0:tiles_r, 0:tiles_c], widen_matrix(tiles_c, cols, side))
+    tiles_r, tiles_c = valid_ref.shape
+    masks = mm(as_bf(valid_ref[...]), widen_matrix(tiles_c, cols, side))
+    masks_ref[...] = masks
     row, col = iota((flat, chans * BLK), 0), iota((flat, chans * BLK), 1)
     same = div(row, HALO) == div(col, BLK)
     spot = mod(iota((flat, cols), 0), HALO)
@@ -103,7 +105,7 @@
         keep_ref[n * flat : (n + 1) * flat, :] = keep[:, n * lanes : (n + 1) * lanes]
 
 
-def weights_kernel(side, tiles_c, own_ref, oth_ref, w1_ref, w2_ref, wm_ref, mask_ref):
+def weights_kernel(own_ref, oth_ref, w1_ref, w2_ref, wm_ref):
     core = lax.axis_index("chan")
     chans, allc = own_ref.shape[1:]
 
@@ -124,9 +126,6 @@
     )
     order = ones_where(iota((allc, allc), 1) == mod(iota((allc, allc), 0) + chans * core, allc))
     wm_ref[...] = mm_nt(order, tall).astype(BF)
-    tiles_r, cols = mask_ref.shape
-    last = own_ref.shape[0] - 1
-    mask_ref[...] = mm(own_ref[last, 0:tiles_r, 0:tiles_c], widen_matrix(tiles_c, cols, side))
 
 
 def put(dst, index, x, amount):
@@ -293,6 +292,7 @@
 
 def border_kernel(
     rows,
+    devices,
     outer_ref,
     masks_ref,
     w1,
@@ -326,6 +326,9 @@
         mm(turn4, jnp.concatenate(pieces[n * cols // lanes : (n + 1) * cols // lanes], axis=1))
         for n in range(2)
     ]
+    place = lax.axis_index("tiles")
+    inside = place != jnp.where(top, 0, devices - 1)
+    own, oth = jnp.where(inside, own, 0.0), jnp.where(inside, oth, 0.0)
     halo = [
         jnp.concatenate([p[r * chans : (r + 1) * chans] for p in (own, oth)], axis=0)
         for r in range(HALO)
@@ -534,7 +537,7 @@
 def unpack_kernel(side, slots, got_ref, out_ref, picked, data):
     tile = lax.axis_index("tiles")
     blocks, all_rows, lanes = got_ref.shape
-    chans, cells, cap = out_ref.shape
+    chans, _, cap = out_ref.shape
     rows = side * chans
     per = side * slots
     room = picked.shape[2]
@@ -603,7 +606,7 @@
 
 def on_device(features, tile_valid, parent_owner, w_first, w_second, w_merge):
     chans, row_count, col_count = features.shape
-    tile_rows, tile_cols = tile_valid.shape
+    tile_rows, _ = tile_valid.shape
     side = row_count // tile_rows
     parents_dev = parent_owner.shape[0]
     devices = lax.axis_size("tiles")
@@ -622,36 +625,42 @@
         return pltpu.CompilerParams(vmem_limit_bytes=int(mib * 1024) << 10)
 
     feat_oth = lax.ppermute(features, "chan", swap)
-    flags = jnp.pad(tile_valid.astype(BF), ((0, chans - tile_rows), (0, allc - tile_cols)))
-    extra = jnp.concatenate([w_first, w_second, jnp.swapaxes(w_merge, 1, 2), flags[None]], axis=0)
-    extra_oth = lax.ppermute(extra, "chan", swap)
     edge_rows = chans * HALO * col_count // lanes
-    send, keep = pl.pallas_call(
-        functools.partial(edges_kernel, side, tile_rows, tile_cols),
-        out_shape=(jax.ShapeDtypeStruct((edge_rows, lanes), BF),) * 2,
+    send, keep, masks = pl.pallas_call(
+        functools.partial(edges_kernel, side),
+        out_shape=(
+            jax.ShapeDtypeStruct((edge_rows, lanes), BF),
+            jax.ShapeDtypeStruct((edge_rows, lanes), BF),
+            jax.ShapeDtypeStruct((tile_rows, col_count), F32),
+        ),
         in_specs=[hbm, vmem],
-        out_specs=(vmem,) * 2,
+        out_specs=(vmem,) * 3,
         scratch_shapes=[
             pltpu.VMEM((2, chans, BLK, col_count), BF),
             pltpu.SemaphoreType.DMA((2,)),
         ],
         compiler_params=limit(52),
         name="edges",
-    )(features, extra)
+    )(features, tile_valid)
     sent = lax.ppermute(send, "chan", swap)
-    cross = [(2 * t + 1, 2 * t + 2) for t in range(devices - 1)]
-    cross += [(2 * t, 2 * t - 1) for t in range(1, devices)]
-    outer = lax.ppermute(jnp.concatenate([keep, sent], axis=0), ("tiles", "chan"), cross)
-    w1, w2, wm, masks = pl.pallas_call(
-        functools.partial(weights_kernel, side, tile_cols),
+    extra = jnp.concatenate(
+        [w_first, w_second, jnp.swapaxes(w_merge, 1, 2), send[None, :chans, :allc]], axis=0
+    )
+    extra_oth = lax.ppermute(extra, "chan", swap)
+    ends = 2 * devices - 1
+    cross = [(2 * t + 1, 2 * t + 2) for t in range(devices - 1)] + [(ends, 0)]
+    cross += [(2 * t, 2 * t - 1) for t in range(1, devices)] + [(0, ends)]
+    payload = jnp.concatenate([keep, sent], axis=0)
+    outer = lax.ppermute(payload, ("tiles", "chan"), cross)
+    w1, w2, wm = pl.pallas_call(
+        weights_kernel,
         out_shape=(
             jax.ShapeDtypeStruct((3 * allc, 3 * allc), BF),
             jax.ShapeDtypeStruct((3 * allc, 3 * allc), BF),
             jax.ShapeDtypeStruct((allc, 4 * allc), BF),
-            jax.ShapeDtypeStruct((tile_rows, col_count), F32),
         ),
         in_specs=[vmem, vmem],
-        out_specs=(vmem,) * 4,
+        out_specs=(vmem,) * 3,
         compiler_params=limit(6),
         name="weights",
     )(extra, extra_oth)
@@ -682,7 +691,7 @@
         name="conv",
     )(features, feat_oth, masks, w1, w2, wm)
     es, m_own, m_oth = pl.pallas_call(
-        functools.partial(border_kernel, rows),
+        functools.partial(border_kernel, rows, devices),
         out_shape=(
             jax.ShapeDtypeStruct(es.shape, BF),
             jax.ShapeDtypeStruct((parent_rows, side * chans, col_count // 2), BF),

time: 59.2 us -> 58.9 us (level)
  other arithmetic: 1.83 us -> 0.06 us
  waiting for transfers between devices: 25.9 us -> 27.1 us
  local copies, waits for them, and re-layouts: 0.02 us -> 0.85 us
    ppermute x1, starting transfers between devices: 4.2 us -> 2.14 us  [on_device(): outer = lax.ppermute(payload, ('tiles', 'chan'), cross)]
    all_to_all x1, starting transfers between devices: 5.42 us -> 7.11 us  [to_peers(): x = lax.all_to_all(x, 'tiles', split_axis=0, concat_axis=0, tiled=True)]
    concatenate x2, other arithmetic: 1 us -> 0.06 us  [the longest x1 0.05 us: on_device(): jnp.concatenate([w_first, w_second, jnp.swapaxes(w_merge, 1, 2), send[Non...]
    convert_element_type x1 -> x0, other arithmetic: 0.83 us -> none  [on_device(): tile_valid.astype(BF)]
    unnamed x4 -> x12, local copies, waits for them, and re-layouts: 0.01 us -> 0.84 us
    ppermute x1, waiting for transfers between devices: 0.9 us -> 1.73 us  [on_device(): sent = lax.ppermute(send, 'chan', swap)]
  transfers between devices with their start and end apart: 7 -> 7, of which waited for: 5 -> 5; matrix products, arithmetic and copies ran while one was open for 3% -> 0% of each run, Pallas kernels for 22% -> 22%
where the time goes in v6:
time: 58.9 us; the launch traced here: 58.7 us
  waiting for transfers between devices  27.1 us (46%)
  Pallas kernels  19.8 us (34%)
  starting transfers between devices  10.1 us (17%)
  local copies, waits for them, and re-layouts  0.85 us (1%)
  between operations  0.77 us (1%)
    all_to_all x1, waiting for transfers between devices, to_peers(): x = lax.all_to_all(x, 'tiles', split_axis=0, concat_axis=0, tiled=True)  19.9 us
    pallas_call x1, Pallas kernels, on_device(): pl.pallas_call(functools.partial(conv_kernel, side), out_shape=(jax.Shape...  7.18 us
    all_to_all x1, starting transfers between devices, to_peers(): x = lax.all_to_all(x, 'tiles', split_axis=0, concat_axis=0, tiled=True)  7.11 us
    pallas_call x1, Pallas kernels, on_device(): pl.pallas_call(restore_kernel, out_shape=(jax.ShapeDtypeStruct((chans, ro...  3.2 us
    ppermute x1, waiting for transfers between devices, on_device(): e_recv = lax.ppermute(e_oth, 'chan', swap)  2.65 us
    pallas_call x1, Pallas kernels, on_device(): pl.pallas_call(functools.partial(pack_kernel, side, slots), out_shape=jax...  2.44 us
    pallas_call x1, Pallas kernels, on_device(): pl.pallas_call(functools.partial(unpack_kernel, side, slots), out_shape=j...  2.42 us
    ppermute x1, starting transfers between devices, on_device(): outer = lax.ppermute(payload, ('tiles', 'chan'), cross)  2.14 us
  transfers between devices with their start and end apart: 7, of which 5 were waited for; matrix products, arithmetic and copies ran while one was open for 0% of the time, Pallas kernels for 22%

profile of v6, /device:TPU:8, one launch (start us, length us, event | category | flops | bytes accessed | tf_op | source)
XLA Modules:
  0.0 58.7 jit_solution(10630312990759617806)
XLA Ops:
  0.6 0.1 collective-permute-start.3
  0.7 0.8 %copy-done.1 = s32[16,32]{1,0:T(8,128)S(1)} copy-done((s32[16,32]{1,0:T(8,128)S(1)}, s32[16,32]{1,0:T(8,128)}, u32[]{:S(2)}) %copy-start.1) | copy-done | bytes 2072
  1.6 1.4 %edges.1 = (bf16[256,128]{1,0:T(8,128)(2,1)S(1)}, bf16[256,128]{1,0:T(8,128)(2,1)S(1)}, f32[16,256]{1,0:T(8,128)S(1)}) custom-call(bf16[32,128,256]{2,1,0:T(8,128)(2,1)} %own_ref.1, s32[16,32]{1,0:T(8,128)S(1)} %copy-done.1), custom_call_target="tpu_custom_call" | custom-call | tf_op jit(solution)/shard_map/edges/pallas_call | solution.py:629
  3.0 0.4 collective-permute-start
  3.4 1.7 %collective-permute-done = bf16[256,128]{1,0:T(8,128)(2,1)S(1)} collective-permute-done((bf16[256,128]{1,0:T(8,128)(2,1)S(1)}, bf16[256,128]{1,0:T(8,128)(2,1)S(1)}, u32[]{:S(2)}, u32[]{:S(2)}) %collective-permute-start) | collective-permute-done | bytes 65568 | tf_op jit(solution)/shard_map/ppermute | solution.py:645
  5.2 2.1 %collective-permute-start.1 = (bf16[512,128]{1,0:T(8,128)(2,1)S(1)}, bf16[512,128]{1,0:T(8,128)(2,1)S(1)}, u32[]{:S(2)}, u32[]{:S(2)}) collective-permute-start(bf16[512,128]{1,0:T(8,128)(2,1)S(1)} %pad_maximum_fusion.1), channel_id=1, source_target_pairs={{1,2},{3,4},{5,6},{7,8},{9,10},{11,12},{13,14},{15,16},{17,18},{19... | collective-permute-start | bytes 393224 | tf_op jit(solution)/shard_map/ppermute | solution.py:654
  7.3 0.1 pad_maximum_fusion.own_ref
  7.4 0.1 collective-permute-start.2
  7.5 1.4 %collective-permute-done.2.oth_ref = bf16[23,32,64]{2,1,0:T(8,128)(2,1)S(1)} collective-permute-done((bf16[23,32,64]{2,1,0:T(8,128)(2,1)S(1)}, bf16[23,32,64]{2,1,0:T(8,128)(2,1)S(1)}, u32[]{:S(2)}, u32[]{:S(2)}) %collective-permute-start.2) | collective-permute-done | bytes 94240 | tf_op jit(solution)/shard_map/ppermute | solution.py:649
  8.9 0.3 weights.1
  9.2 0.0 collective-permute-done.3.oth_ref
  9.2 7.2 %conv.1 = (bf16[1408,64,256]{2,1,0:T(8,128)(2,1)}, bf16[4,256,128]{2,1,0:T(8,128)(2,1)S(1)}, bf16[4,256,128]{2,1,0:T(8,128)(2,1)S(1)}, bf16[3,192,256]{2,1,0:T(8...) custom-call(bf16[32,128,256]{2,1,0:T(8,128)(2,1)S(1)} %copy-done, ...), custom_call_target="tpu_custom_call" | custom-call | tf_op jit(solution)/shard_map/conv/pallas_call | solution.py:670
  16.4 0.0 copy-start.2
  16.4 1.8 %border.1 = (bf16[1408,64,256]{2,1,0:T(8,128)(2,1)}, bf16[4,256,128]{2,1,0:T(8,128)(2,1)S(1)}, bf16[4,256,128]{2,1,0:T(8,128)(2,1)S(1)}) custom-call(bf16[512,128]{1,0:T(8,128)(2,1)S(1)} %collective-permute-done.1.outer_ref, f32[16,256]{1,0:T(8,128)S(1)} %get-tuple-element.21.masks_ref, ...), custom_call_target="tpu_custom_call", output_to_operand_aliasing={{0}: (10, {})} | custom-call | tf_op jit(solution)/shard_map/border/pallas_call | solution.py:693
  18.3 0.2 collective-permute-start.4
  18.5 1.4 %collective-permute-done.4.mrecv_ref = bf16[4,256,128]{2,1,0:T(8,128)(2,1)S(1)} collective-permute-done((bf16[4,256,128]{2,1,0:T(8,128)(2,1)S(1)}, bf16[4,256,128]{2,1,0:T(8,128)(2,1)S(1)}, u32[]{:S(2)}, u32[]{:S(2)}) %collective-permute-start.4) | collective-permute-done | bytes 262176 | tf_op jit(solution)/shard_map/ppermute | solution.py:712
  19.9 2.4 %pack.1.after_hbm = bf16[16,264,128]{2,1,0:T(8,128)(2,1)} custom-call(s32[1,128]{1,0:T(1,128)S(1)} %bitcast.5, bf16[4,256,128]{2,1,0:T(8,128)(2,1)S(1)} %get-tuple-element.32.mown_ref, bf16[4,256,128]{2,1,0:T(8,128)(2,1)S(1)} %collective-permute-done.4.mrecv_ref), custom_call_target="tpu_custom_call" | custom-call | tf_op jit(solution)/shard_map/pack/pallas_call | solution.py:714
  22.3 7.1 %all-to-all-start = ((bf16[16,264,128]{2,1,0:T(8,128)(2,1)}), bf16[16,264,128]{2,1,0:T(8,128)(2,1)S(1)}, u32[]{:S(2)}, u32[]{:S(2)}) async-start(bf16[16,264,128]{2,1,0:T(8,128)(2,1)} %pack.1.after_hbm), calls=%async_computation | async-start | bytes 2162688 | tf_op jit(solution)/shard_map/all_to_all | solution.py:733
  29.4 3.2 %restore.1 = (bf16[32,128,256]{2,1,0:T(8,128)(2,1)}, bf16[32,64,256]{2,1,0:T(8,128)(2,1)S(1)}) custom-call(bf16[1408,64,256]{2,1,0:T(8,128)(2,1)} %get-tuple-element.31.es_hbm, bf16[16,264,128]{2,1,0:T(8,128)(2,1)} %pack.1.after_hbm), custom_call_target="tpu_custom_call" | custom-call | tf_op jit(solution)/shard_map/restore/pallas_call | solution.py:740
  32.6 0.1 collective-permute-start.5
  32.7 2.6 %collective-permute-done.5.recv_ref = bf16[32,64,256]{2,1,0:T(8,128)(2,1)S(1)} collective-permute-done((bf16[32,64,256]{2,1,0:T(8,128)(2,1)S(1)}, bf16[32,64,256]{2,1,0:T(8,128)(2,1)S(1)}, u32[]{:S(2)}, u32[]{:S(2)}) %collective-permute-start.5) | collective-permute-done | bytes 1048608 | tf_op jit(solution)/shard_map/ppermute | solution.py:757
  35.4 1.0 %fill.1 = bf16[32,128,256]{2,1,0:T(8,128)(2,1)} custom-call(bf16[32,64,256]{2,1,0:T(8,128)(2,1)S(1)} %collective-permute-done.5.recv_ref, bf16[32,128,256]{2,1,0:T(8,128)(2,1)} %get-tuple-element.35.held_hbm), custom_call_target="tpu_custom_call", output_to_operand_aliasing={{}: (1, {})} | custom-call | tf_op jit(solution)/shard_map/fill/pallas_call | solution.py:758
  36.3 19.9 %all-to-all-done.got_ref = bf16[16,264,128]{2,1,0:T(8,128)(2,1)S(1)} async-done(((bf16[16,264,128]{2,1,0:T(8,128)(2,1)}), bf16[16,264,128]{2,1,0:T(8,128)(2,1)S(1)}, u32[]{:S(2)}, u32[]{:S(2)}) %all-to-all-start) | async-done | bytes 1081376 | tf_op jit(solution)/shard_map/all_to_all | solution.py:733
  56.2 2.4 %unpack.1 = bf16[32,64,192]{2,1,0:T(8,128)(2,1)} custom-call(bf16[16,264,128]{2,1,0:T(8,128)(2,1)S(1)} %all-to-all-done.got_ref), custom_call_target="tpu_custom_call" | custom-call | tf_op jit(solution)/shard_map/unpack/pallas_call | solution.py:769
  (13 shorter events, 0.0 us)
Async XLA Ops:
  0.6 8.6 %copy-start = (bf16[32,128,256]{2,1,0:T(8,128)(2,1)S(1)}, bf16[32,128,256]{2,1,0:T(8,128)(2,1)}, u32[]{:S(2)}) copy-start(bf16[32,128,256]{2,1,0:T(8,128)(2,1)} %own_ref.1) | copy-start | bytes 6291460
  0.6 8.6 %collective-permute-start.3 = (bf16[32,128,256]{2,1,0:T(8,128)(2,1)}, bf16[32,128,256]{2,1,0:T(8,128)(2,1)S(1)}, u32[]{:S(2)}, u32[]{:S(2)}) collective-permute-start(bf16[32,128,256]{2,1,0:T(8,128)(2,1)} %own_ref.1), channel_id=1, source_target_pairs={{0,1},{1,0},{2,3},{3,2},{4,5},{5,4},{6,7},{7,6},{8,9},{9,8},{10,11... | collective-permute-start | bytes 6291464 | tf_op jit(solution)/shard_map/ppermute | solution.py:627
  0.7 0.8 %copy-start.1 = (s32[16,32]{1,0:T(8,128)S(1)}, s32[16,32]{1,0:T(8,128)}, u32[]{:S(2)}) copy-start(s32[16,32]{1,0:T(8,128)} %valid_ref.1) | copy-start | bytes 6148
  1.6 5.8 %copy-start.3 = (bf16[9,32,64]{2,1,0:T(8,128)(2,1)S(1)}, bf16[9,32,64]{2,1,0:T(8,128)(2,1)}, u32[]{:S(2)}) copy-start(bf16[9,32,64]{2,1,0:T(8,128)(2,1)} %param.10) | copy-start | bytes 110596
  1.6 5.8 %copy-start.4 = (bf16[9,32,64]{2,1,0:T(8,128)(2,1)S(1)}, bf16[9,32,64]{2,1,0:T(8,128)(2,1)}, u32[]{:S(2)}) copy-start(bf16[9,32,64]{2,1,0:T(8,128)(2,1)} %param.9) | copy-start | bytes 110596
  1.6 5.8 %copy-start.5 = (bf16[4,64,32]{1,2,0:T(8,128)(2,1)S(1)}, bf16[4,64,32]{1,2,0:T(8,128)(2,1)}, u32[]{:S(2)}) copy-start(bf16[4,64,32]{1,2,0:T(8,128)(2,1)} %param.11) | copy-start | bytes 49156
  3.0 2.2 %collective-permute-start = (bf16[256,128]{1,0:T(8,128)(2,1)S(1)}, bf16[256,128]{1,0:T(8,128)(2,1)S(1)}, u32[]{:S(2)}, u32[]{:S(2)}) collective-permute-start(bf16[256,128]{1,0:T(8,128)(2,1)S(1)} %get-tuple-element.20), channel_id=1, source_target_pairs={{0,1},{1,0},{2,3},{3,2},{4,5},{5,4},{6,7},{7,6},{8,9},{9,8},{10,11... | collective-permute-start | bytes 196616 | tf_op jit(solution)/shard_map/ppermute | solution.py:645
  5.2 11.2 %collective-permute-start.1 = (bf16[512,128]{1,0:T(8,128)(2,1)S(1)}, bf16[512,128]{1,0:T(8,128)(2,1)S(1)}, u32[]{:S(2)}, u32[]{:S(2)}) collective-permute-start(bf16[512,128]{1,0:T(8,128)(2,1)S(1)} %pad_maximum_fusion.1), channel_id=1, source_target_pairs={{1,2},{3,4},{5,6},{7,8},{9,10},{11,12},{13,14},{15,16},{17,18},{19... | collective-permute-start | bytes 393224 | tf_op jit(solution)/shard_map/ppermute | solution.py:654
  7.4 1.5 %collective-permute-start.2 = (bf16[23,32,64]{2,1,0:T(8,128)(2,1)S(1)}, bf16[23,32,64]{2,1,0:T(8,128)(2,1)S(1)}, u32[]{:S(2)}, u32[]{:S(2)}) collective-permute-start(bf16[23,32,64]{2,1,0:T(8,128)(2,1)S(1)} %pad_maximum_fusion.own_ref), channel_id=1, source_target_pairs={{0,1},{1,0},{2,3},{3,2},{4,5},{5,4},{6,7},{7,6},{8,9},{9,8},{10,11... | collective-permute-start | bytes 282632 | tf_op jit(solution)/shard_map/ppermute | solution.py:649
  16.4 3.5 %copy-start.2 = (s32[128]{0:T(128)S(1)}, s32[128]{0:T(128)}, u32[]{:S(2)}) copy-start(s32[128]{0:T(128)} %param.8) | copy-start | bytes 1540
  18.3 1.6 %collective-permute-start.4 = (bf16[4,256,128]{2,1,0:T(8,128)(2,1)S(1)}, bf16[4,256,128]{2,1,0:T(8,128)(2,1)S(1)}, u32[]{:S(2)}, u32[]{:S(2)}) collective-permute-start(bf16[4,256,128]{2,1,0:T(8,128)(2,1)S(1)} %get-tuple-element.33), channel_id=1, source_target_pairs={{0,1},{1,0},{2,3},{3,2},{4,5},{5,4},{6,7},{7,6},{8,9},{9,8},{10,11... | collective-permute-start | bytes 786440 | tf_op jit(solution)/shard_map/ppermute | solution.py:712
  22.3 33.9 %all-to-all-start = ((bf16[16,264,128]{2,1,0:T(8,128)(2,1)}), bf16[16,264,128]{2,1,0:T(8,128)(2,1)S(1)}, u32[]{:S(2)}, u32[]{:S(2)}) async-start(bf16[16,264,128]{2,1,0:T(8,128)(2,1)} %pack.1.after_hbm), calls=%async_computation | async-start | bytes 2162688 | tf_op jit(solution)/shard_map/all_to_all | solution.py:733
  32.6 2.7 %collective-permute-start.5 = (bf16[32,64,256]{2,1,0:T(8,128)(2,1)S(1)}, bf16[32,64,256]{2,1,0:T(8,128)(2,1)S(1)}, u32[]{:S(2)}, u32[]{:S(2)}) collective-permute-start(bf16[32,64,256]{2,1,0:T(8,128)(2,1)S(1)} %get-tuple-element.34), channel_id=1, source_target_pairs={{0,1},{1,0},{2,3},{3,2},{4,5},{5,4},{6,7},{7,6},{8,9},{9,8},{10,11... | collective-permute-start | bytes 3145736 | tf_op jit(solution)/shard_map/ppermute | solution.py:757

commit v7 on v6

--- a/solution.py
+++ b/solution.py
@@ -292,7 +292,6 @@
 
 def border_kernel(
     rows,
-    devices,
     outer_ref,
     masks_ref,
     w1,
@@ -326,9 +325,6 @@
         mm(turn4, jnp.concatenate(pieces[n * cols // lanes : (n + 1) * cols // lanes], axis=1))
         for n in range(2)
     ]
-    place = lax.axis_index("tiles")
-    inside = place != jnp.where(top, 0, devices - 1)
-    own, oth = jnp.where(inside, own, 0.0), jnp.where(inside, oth, 0.0)
     halo = [
         jnp.concatenate([p[r * chans : (r + 1) * chans] for p in (own, oth)], axis=0)
         for r in range(HALO)
@@ -421,14 +417,14 @@
     group = div(iota(now[0].shape, 1), width)
     bit = 1
     while bit < n:
-        odd = group & bit != 0
+        odd = jnp.where(group & bit != 0, 1.0, 0.0).astype(BF) > jnp.bfloat16(0.5)
         now = [jnp.where(odd, now[(j + bit) % n], now[j]) for j in range(n)]
         bit *= 2
     return now
 
 
 def pack_kernel(
-    side, slots, owner_ref, mown_ref, mrecv_ref, out_ref, arr, lhs, mid, code_ref
+    side, slots, owner_ref, mown_ref, mrecv_ref, out_hbm, out_ref, arr, lhs, mid, code_ref, sems
 ):
     core, tile = lax.axis_index("chan"), lax.axis_index("tiles")
     count = owner_ref.shape[1]
@@ -436,6 +432,15 @@
     blocks, all_rows, _ = out_ref.shape
     per = side * slots
     wide = lanes // side
+    copies = []
+
+    def send_out(at, n):
+        part = pl.ds(at, n)
+        copies.append(
+            pltpu.make_async_copy(out_ref.at[part], out_hbm.at[part], sems.at[len(copies)])
+        )
+        copies[-1].start()
+
     for k in range(mine):
         arr[core * mine + k] = mown_ref[k]
         arr[(1 - core) * mine + k] = mrecv_ref[k]
@@ -473,21 +478,17 @@
             got = mm(lhs[v], take).astype(BF)
             for h in range(halves):
                 mid[h * side + i] = got[:, h * lanes : (h + 1) * lanes]
-        for h in range(halves):
-
-            def by_owner(step, carry, h=h):
-                at = pl.ds(pl.multiple_of(step * BLK, BLK), BLK)
-                done = deal([mid[h * side + i, at, :] for i in range(side)], wide)
-                for j in range(side):
-                    out_ref[h * side + -j % side, at, :] = done[j]
-                return carry
-
-            lax.fori_loop(0, rows // BLK, by_owner, 0, unroll=4)
         tally = mm(jnp.ones((all_rows - rows, count), BF), marks)
         for d in range(blocks):
             out_ref[d, rows:all_rows, :] = jnp.broadcast_to(
                 tally[:, d : d + 1], (all_rows - rows, lanes)
             ).astype(BF)
+        for h in range(halves):
+            for r in range(0, rows, BLK):
+                done = deal([mid[h * side + i, r : r + BLK, :] for i in range(side)], wide)
+                for j in range(side):
+                    out_ref[h * side + -j % side, r : r + BLK, :] = done[j]
+            send_out(h * side, side)
     else:
         code = owner * per + within
         lane = iota((wide, lanes), 1)
@@ -509,6 +510,9 @@
                 goal = div(iota((count, lanes), 1) + at * lanes, per)
                 tally = mm(jnp.ones((all_rows - rows, count), BF), ones_where(owner == goal))
                 out_ref[at, rows:all_rows, :] = tally.astype(BF)
+        send_out(0, blocks)
+    for copy in copies:
+        copy.wait()
 
 
 def targets(tallies, lanes, group, slots):
@@ -534,10 +538,11 @@
     return jnp.where(same, jnp.ones_like(goal), jnp.zeros_like(goal))
 
 
-def unpack_kernel(side, slots, got_ref, out_ref, picked, data):
+def unpack_kernel(side, slots, got_ref, out_hbm, out_ref, picked, data, column, sems):
     tile = lax.axis_index("tiles")
     blocks, all_rows, lanes = got_ref.shape
     chans, _, cap = out_ref.shape
+    copies = []
     rows = side * chans
     per = side * slots
     room = picked.shape[2]
@@ -551,7 +556,10 @@
                 other = got_ref[h * side + s, rows:all_rows, :].astype(F32)
                 tally = jnp.where(group == s, other, tally)
             tallies.append(tally.astype(BF))
-        spots = targets(tallies, lanes, slots, slots)
+        for h, spot in enumerate(targets(tallies, lanes, slots, slots)):
+            turned = jnp.transpose(jnp.broadcast_to(spot, (lanes, lanes))).astype(BF)
+            column[h, 0:lanes, :] = turned
+            column[h, lanes : 2 * lanes, :] = turned
         for h in range(halves):
 
             def turn_rows(step, carry, h=h):
@@ -566,11 +574,15 @@
             v = lax.rem(2 * side - j - lax.rem(tile, side), side)
             left = jnp.concatenate([data[h, j] for h in range(halves)], axis=1)
             right = []
-            for spot in spots:
-                line = jnp.broadcast_to(spot, (side, lanes))
-                line = pltpu.roll(line, (side - j) * slots, 1) if j else line
-                right.append(hits(line[0:1], room))
-            picked[v] = mm_nt(left, jnp.concatenate(right, axis=1)).astype(BF)
+            for h in range(halves):
+                spot = column[h, j * slots : j * slots + lanes, :]
+                parts = []
+                for at in range(0, room, lanes):
+                    goal = (iota((1, lanes), 1) + at).astype(F32).astype(BF)
+                    same = spot == jnp.broadcast_to(goal, (lanes, lanes))
+                    parts.append(jnp.where(same, jnp.ones_like(spot), jnp.zeros_like(spot)))
+                right.append(jnp.concatenate(parts, axis=1))
+            picked[v] = mm(left, jnp.concatenate(right, axis=0)).astype(BF)
     else:
         tallies = [got_ref[b, rows:all_rows, :] for b in range(blocks)]
         spots = [hits(t, room) for t in targets(tallies, lanes, per, slots)]
@@ -590,8 +602,8 @@
         & (mod(div(row, side), two) == mod(div(col, BLK), two))
         & (mod(row, side) == div(col, BLK * two))
     )
-    for u in range(0, side, two):
-        for ch in range(0, chans, BLK):
+    for ch in range(0, chans, BLK):
+        for u in range(0, side, two):
             block = jnp.concatenate(
                 [
                     picked[v, (u + w) * chans + ch : (u + w) * chans + ch + BLK, :]
@@ -602,6 +614,13 @@
             )
             done = mm(turn, block).astype(BF).reshape(BLK, BLK, room)
             out_ref[ch : ch + BLK, u * side : (u + two) * side, :] = done[:, :, :cap]
+        part = pl.ds(ch, BLK)
+        copies.append(
+            pltpu.make_async_copy(out_ref.at[part], out_hbm.at[part], sems.at[ch // BLK])
+        )
+        copies[-1].start()
+    for copy in copies:
+        copy.wait()
 
 
 def on_device(features, tile_valid, parent_owner, w_first, w_second, w_merge):
@@ -647,9 +666,8 @@
         [w_first, w_second, jnp.swapaxes(w_merge, 1, 2), send[None, :chans, :allc]], axis=0
     )
     extra_oth = lax.ppermute(extra, "chan", swap)
-    ends = 2 * devices - 1
-    cross = [(2 * t + 1, 2 * t + 2) for t in range(devices - 1)] + [(ends, 0)]
-    cross += [(2 * t, 2 * t - 1) for t in range(1, devices)] + [(0, ends)]
+    cross = [(2 * t + 1, 2 * t + 2) for t in range(devices - 1)]
+    cross += [(2 * t, 2 * t - 1) for t in range(1, devices)]
     payload = jnp.concatenate([keep, sent], axis=0)
     outer = lax.ppermute(payload, ("tiles", "chan"), cross)
     w1, w2, wm = pl.pallas_call(
@@ -691,7 +709,7 @@
         name="conv",
     )(features, feat_oth, masks, w1, w2, wm)
     es, m_own, m_oth = pl.pallas_call(
-        functools.partial(border_kernel, rows, devices),
+        functools.partial(border_kernel, rows),
         out_shape=(
             jax.ShapeDtypeStruct(es.shape, BF),
             jax.ShapeDtypeStruct((parent_rows, side * chans, col_count // 2), BF),
@@ -715,12 +733,14 @@
         functools.partial(pack_kernel, side, slots),
         out_shape=jax.ShapeDtypeStruct((blocks, all_rows, lanes), BF),
         in_specs=[vmem, vmem, vmem],
-        out_specs=vmem,
+        out_specs=hbm,
         scratch_shapes=[
+            pltpu.VMEM((blocks, all_rows, lanes), BF),
             pltpu.VMEM((2 * parent_rows, side * chans, lanes), BF),
             pltpu.VMEM((side, side * chans, lanes), BF),
             pltpu.VMEM((blocks, side * chans, lanes), BF),
             pltpu.VMEM((parents_dev * side, lanes), BF if fold == 1 else jnp.int32),
+            pltpu.SemaphoreType.DMA((max(1, blocks // side),)),
         ],
         compiler_params=limit(16),
         name="pack",
@@ -770,10 +790,13 @@
         functools.partial(unpack_kernel, side, slots),
         out_shape=jax.ShapeDtypeStruct((chans, side * side, own_cap), BF),
         in_specs=[vmem],
-        out_specs=vmem,
+        out_specs=hbm,
         scratch_shapes=[
+            pltpu.VMEM((chans, side * side, own_cap), BF),
             pltpu.VMEM((side, side * chans, room), BF),
             pltpu.VMEM((2, side, side * chans, lanes), BF),
+            pltpu.VMEM((2, 2 * lanes, lanes), BF),
+            pltpu.SemaphoreType.DMA((chans // BLK,)),
         ],
         compiler_params=limit(24),
         name="unpack",

time: 58.9 us -> 58.5 us (level)
  Pallas kernels: 19.8 us -> 19.2 us
    ppermute x1, starting transfers between devices: 2.14 us -> 3.98 us  [on_device(): outer = lax.ppermute(payload, ('tiles', 'chan'), cross)]
    all_to_all x1, starting transfers between devices: 7.11 us -> 5.5 us  [to_peers(): x = lax.all_to_all(x, 'tiles', split_axis=0, concat_axis=0, tiled=True)]
  transfers between devices with their start and end apart: 7 -> 7, of which waited for: 5 -> 5; matrix products, arithmetic and copies ran while one was open for 0% -> 0% of each run, Pallas kernels for 22% -> 23%
where the time goes in v7:
time: 58.5 us; the launch traced here: 58.2 us
  waiting for transfers between devices  27 us (46%)
  Pallas kernels  19.2 us (33%)
  starting transfers between devices  10.4 us (18%)
  local copies, waits for them, and re-layouts  0.85 us (1%)
  between operations  0.81 us (1%)
    all_to_all x1, waiting for transfers between devices, to_peers(): x = lax.all_to_all(x, 'tiles', split_axis=0, concat_axis=0, tiled=True)  19.8 us
    pallas_call x1, Pallas kernels, on_device(): pl.pallas_call(functools.partial(conv_kernel, side), out_shape=(jax.Shape...  7.18 us
    all_to_all x1, starting transfers between devices, to_peers(): x = lax.all_to_all(x, 'tiles', split_axis=0, concat_axis=0, tiled=True)  5.5 us
    ppermute x1, starting transfers between devices, on_device(): outer = lax.ppermute(payload, ('tiles', 'chan'), cross)  3.98 us
    pallas_call x1, Pallas kernels, on_device(): pl.pallas_call(restore_kernel, out_shape=(jax.ShapeDtypeStruct((chans, ro...  3.2 us
    ppermute x1, waiting for transfers between devices, on_device(): e_recv = lax.ppermute(e_oth, 'chan', swap)  2.65 us
    pallas_call x1, Pallas kernels, on_device(): pl.pallas_call(functools.partial(unpack_kernel, side, slots), out_shape=j...  2.12 us
    pallas_call x1, Pallas kernels, on_device(): pl.pallas_call(functools.partial(pack_kernel, side, slots), out_shape=jax...  2.1 us
  transfers between devices with their start and end apart: 7, of which 5 were waited for; matrix products, arithmetic and copies ran while one was open for 0% of the time, Pallas kernels for 23%

profile of v7, /device:TPU:8, one launch (start us, length us, event | category | flops | bytes accessed | tf_op | source)
XLA Modules:
  0.0 58.2 jit_solution(16255414050419453167)
XLA Ops:
  0.6 0.1 collective-permute-start.3
  0.7 0.8 %copy-done.1 = s32[16,32]{1,0:T(8,128)S(1)} copy-done((s32[16,32]{1,0:T(8,128)S(1)}, s32[16,32]{1,0:T(8,128)}, u32[]{:S(2)}) %copy-start.1) | copy-done | bytes 2072
  1.6 1.4 %edges.1 = (bf16[256,128]{1,0:T(8,128)(2,1)S(1)}, bf16[256,128]{1,0:T(8,128)(2,1)S(1)}, f32[16,256]{1,0:T(8,128)S(1)}) custom-call(bf16[32,128,256]{2,1,0:T(8,128)(2,1)} %own_ref.1, s32[16,32]{1,0:T(8,128)S(1)} %copy-done.1), custom_call_target="tpu_custom_call" | custom-call | tf_op jit(solution)/shard_map/edges/pallas_call | solution.py:648
  3.0 0.4 collective-permute-start
  3.4 1.7 %collective-permute-done = bf16[256,128]{1,0:T(8,128)(2,1)S(1)} collective-permute-done((bf16[256,128]{1,0:T(8,128)(2,1)S(1)}, bf16[256,128]{1,0:T(8,128)(2,1)S(1)}, u32[]{:S(2)}, u32[]{:S(2)}) %collective-permute-start) | collective-permute-done | bytes 65568 | tf_op jit(solution)/shard_map/ppermute | solution.py:664
  5.2 4.0 %collective-permute-start.1 = (bf16[512,128]{1,0:T(8,128)(2,1)S(1)}, bf16[512,128]{1,0:T(8,128)(2,1)S(1)}, u32[]{:S(2)}, u32[]{:S(2)}) collective-permute-start(bf16[512,128]{1,0:T(8,128)(2,1)S(1)} %pad_maximum_fusion.1), channel_id=1, source_target_pairs={{1,2},{3,4},{5,6},{7,8},{9,10},{11,12},{13,14},{15,16},{17,18},{19... | collective-permute-start | bytes 393224 | tf_op jit(solution)/shard_map/ppermute | solution.py:672
  9.2 0.1 pad_maximum_fusion.own_ref
  9.3 0.1 collective-permute-start.2
  9.3 1.4 %collective-permute-done.2.oth_ref = bf16[23,32,64]{2,1,0:T(8,128)(2,1)S(1)} collective-permute-done((bf16[23,32,64]{2,1,0:T(8,128)(2,1)S(1)}, bf16[23,32,64]{2,1,0:T(8,128)(2,1)S(1)}, u32[]{:S(2)}, u32[]{:S(2)}) %collective-permute-start.2) | collective-permute-done | bytes 94240 | tf_op jit(solution)/shard_map/ppermute | solution.py:668
  10.8 0.3 weights.1
  11.1 7.2 %conv.1 = (bf16[1408,64,256]{2,1,0:T(8,128)(2,1)}, bf16[4,256,128]{2,1,0:T(8,128)(2,1)S(1)}, bf16[4,256,128]{2,1,0:T(8,128)(2,1)S(1)}, bf16[3,192,256]{2,1,0:T(8...) custom-call(bf16[32,128,256]{2,1,0:T(8,128)(2,1)S(1)} %copy-done, ...), custom_call_target="tpu_custom_call" | custom-call | tf_op jit(solution)/shard_map/conv/pallas_call | solution.py:688
  18.3 0.0 collective-permute-done.1.outer_ref
  18.3 0.0 copy-start.2
  18.3 1.8 %border.1 = (bf16[1408,64,256]{2,1,0:T(8,128)(2,1)}, bf16[4,256,128]{2,1,0:T(8,128)(2,1)S(1)}, bf16[4,256,128]{2,1,0:T(8,128)(2,1)S(1)}) custom-call(bf16[512,128]{1,0:T(8,128)(2,1)S(1)} %collective-permute-done.1.outer_ref, f32[16,256]{1,0:T(8,128)S(1)} %get-tuple-element.21.masks_ref, ...), custom_call_target="tpu_custom_call", output_to_operand_aliasing={{0}: (10, {})} | custom-call | tf_op jit(solution)/shard_map/border/pallas_call | solution.py:711
  20.1 0.2 collective-permute-start.4
  20.4 1.4 %collective-permute-done.4.mrecv_ref = bf16[4,256,128]{2,1,0:T(8,128)(2,1)S(1)} collective-permute-done((bf16[4,256,128]{2,1,0:T(8,128)(2,1)S(1)}, bf16[4,256,128]{2,1,0:T(8,128)(2,1)S(1)}, u32[]{:S(2)}, u32[]{:S(2)}) %collective-permute-start.4) | collective-permute-done | bytes 262176 | tf_op jit(solution)/shard_map/ppermute | solution.py:730
  21.8 2.1 %pack.1.after_hbm = bf16[16,264,128]{2,1,0:T(8,128)(2,1)} custom-call(s32[1,128]{1,0:T(1,128)S(1)} %bitcast.5, bf16[4,256,128]{2,1,0:T(8,128)(2,1)S(1)} %get-tuple-element.32.mown_ref, bf16[4,256,128]{2,1,0:T(8,128)(2,1)S(1)} %collective-permute-done.4.mrecv_ref), custom_call_target="tpu_custom_call" | custom-call | tf_op jit(solution)/shard_map/pack/pallas_call | solution.py:732
  23.9 5.5 %all-to-all-start = ((bf16[16,264,128]{2,1,0:T(8,128)(2,1)}), bf16[16,264,128]{2,1,0:T(8,128)(2,1)S(1)}, u32[]{:S(2)}, u32[]{:S(2)}) async-start(bf16[16,264,128]{2,1,0:T(8,128)(2,1)} %pack.1.after_hbm), calls=%async_computation | async-start | bytes 2162688 | tf_op jit(solution)/shard_map/all_to_all | solution.py:753
  29.4 3.2 %restore.1 = (bf16[32,128,256]{2,1,0:T(8,128)(2,1)}, bf16[32,64,256]{2,1,0:T(8,128)(2,1)S(1)}) custom-call(bf16[1408,64,256]{2,1,0:T(8,128)(2,1)} %get-tuple-element.31.es_hbm, bf16[16,264,128]{2,1,0:T(8,128)(2,1)} %pack.1.after_hbm), custom_call_target="tpu_custom_call" | custom-call | tf_op jit(solution)/shard_map/restore/pallas_call | solution.py:760
  32.6 0.1 collective-permute-start.5
  32.7 2.6 %collective-permute-done.5.recv_ref = bf16[32,64,256]{2,1,0:T(8,128)(2,1)S(1)} collective-permute-done((bf16[32,64,256]{2,1,0:T(8,128)(2,1)S(1)}, bf16[32,64,256]{2,1,0:T(8,128)(2,1)S(1)}, u32[]{:S(2)}, u32[]{:S(2)}) %collective-permute-start.5) | collective-permute-done | bytes 1048608 | tf_op jit(solution)/shard_map/ppermute | solution.py:777
  35.3 1.0 %fill.1 = bf16[32,128,256]{2,1,0:T(8,128)(2,1)} custom-call(bf16[32,64,256]{2,1,0:T(8,128)(2,1)S(1)} %collective-permute-done.5.recv_ref, bf16[32,128,256]{2,1,0:T(8,128)(2,1)} %get-tuple-element.35.held_hbm), custom_call_target="tpu_custom_call", output_to_operand_aliasing={{}: (1, {})} | custom-call | tf_op jit(solution)/shard_map/fill/pallas_call | solution.py:778
  36.3 19.8 %all-to-all-done.got_ref = bf16[16,264,128]{2,1,0:T(8,128)(2,1)S(1)} async-done(((bf16[16,264,128]{2,1,0:T(8,128)(2,1)}), bf16[16,264,128]{2,1,0:T(8,128)(2,1)S(1)}, u32[]{:S(2)}, u32[]{:S(2)}) %all-to-all-start) | async-done | bytes 1081376 | tf_op jit(solution)/shard_map/all_to_all | solution.py:753
  56.1 2.1 %unpack.1 = bf16[32,64,192]{2,1,0:T(8,128)(2,1)} custom-call(bf16[16,264,128]{2,1,0:T(8,128)(2,1)S(1)} %all-to-all-done.got_ref), custom_call_target="tpu_custom_call" | custom-call | tf_op jit(solution)/shard_map/unpack/pallas_call | solution.py:789
  (13 shorter events, 0.0 us)
Async XLA Ops:
  0.6 10.5 %copy-start = (bf16[32,128,256]{2,1,0:T(8,128)(2,1)S(1)}, bf16[32,128,256]{2,1,0:T(8,128)(2,1)}, u32[]{:S(2)}) copy-start(bf16[32,128,256]{2,1,0:T(8,128)(2,1)} %own_ref.1) | copy-start | bytes 6291460
  0.6 10.4 %collective-permute-start.3 = (bf16[32,128,256]{2,1,0:T(8,128)(2,1)}, bf16[32,128,256]{2,1,0:T(8,128)(2,1)S(1)}, u32[]{:S(2)}, u32[]{:S(2)}) collective-permute-start(bf16[32,128,256]{2,1,0:T(8,128)(2,1)} %own_ref.1), channel_id=1, source_target_pairs={{0,1},{1,0},{2,3},{3,2},{4,5},{5,4},{6,7},{7,6},{8,9},{9,8},{10,11... | collective-permute-start | bytes 6291464 | tf_op jit(solution)/shard_map/ppermute | solution.py:646
  0.7 0.8 %copy-start.1 = (s32[16,32]{1,0:T(8,128)S(1)}, s32[16,32]{1,0:T(8,128)}, u32[]{:S(2)}) copy-start(s32[16,32]{1,0:T(8,128)} %valid_ref.1) | copy-start | bytes 6148
  1.6 7.6 %copy-start.3 = (bf16[9,32,64]{2,1,0:T(8,128)(2,1)S(1)}, bf16[9,32,64]{2,1,0:T(8,128)(2,1)}, u32[]{:S(2)}) copy-start(bf16[9,32,64]{2,1,0:T(8,128)(2,1)} %param.10) | copy-start | bytes 110596
  1.6 7.6 %copy-start.4 = (bf16[9,32,64]{2,1,0:T(8,128)(2,1)S(1)}, bf16[9,32,64]{2,1,0:T(8,128)(2,1)}, u32[]{:S(2)}) copy-start(bf16[9,32,64]{2,1,0:T(8,128)(2,1)} %param.9) | copy-start | bytes 110596
  1.6 7.6 %copy-start.5 = (bf16[4,64,32]{1,2,0:T(8,128)(2,1)S(1)}, bf16[4,64,32]{1,2,0:T(8,128)(2,1)}, u32[]{:S(2)}) copy-start(bf16[4,64,32]{1,2,0:T(8,128)(2,1)} %param.11) | copy-start | bytes 49156
  3.0 2.2 %collective-permute-start = (bf16[256,128]{1,0:T(8,128)(2,1)S(1)}, bf16[256,128]{1,0:T(8,128)(2,1)S(1)}, u32[]{:S(2)}, u32[]{:S(2)}) collective-permute-start(bf16[256,128]{1,0:T(8,128)(2,1)S(1)} %get-tuple-element.20), channel_id=1, source_target_pairs={{0,1},{1,0},{2,3},{3,2},{4,5},{5,4},{6,7},{7,6},{8,9},{9,8},{10,11... | collective-permute-start | bytes 196616 | tf_op jit(solution)/shard_map/ppermute | solution.py:664
  5.2 13.1 %collective-permute-start.1 = (bf16[512,128]{1,0:T(8,128)(2,1)S(1)}, bf16[512,128]{1,0:T(8,128)(2,1)S(1)}, u32[]{:S(2)}, u32[]{:S(2)}) collective-permute-start(bf16[512,128]{1,0:T(8,128)(2,1)S(1)} %pad_maximum_fusion.1), channel_id=1, source_target_pairs={{1,2},{3,4},{5,6},{7,8},{9,10},{11,12},{13,14},{15,16},{17,18},{19... | collective-permute-start | bytes 393224 | tf_op jit(solution)/shard_map/ppermute | solution.py:672
  9.3 1.5 %collective-permute-start.2 = (bf16[23,32,64]{2,1,0:T(8,128)(2,1)S(1)}, bf16[23,32,64]{2,1,0:T(8,128)(2,1)S(1)}, u32[]{:S(2)}, u32[]{:S(2)}) collective-permute-start(bf16[23,32,64]{2,1,0:T(8,128)(2,1)S(1)} %pad_maximum_fusion.own_ref), channel_id=1, source_target_pairs={{0,1},{1,0},{2,3},{3,2},{4,5},{5,4},{6,7},{7,6},{8,9},{9,8},{10,11... | collective-permute-start | bytes 282632 | tf_op jit(solution)/shard_map/ppermute | solution.py:668
  18.3 3.5 %copy-start.2 = (s32[128]{0:T(128)S(1)}, s32[128]{0:T(128)}, u32[]{:S(2)}) copy-start(s32[128]{0:T(128)} %param.8) | copy-start | bytes 1540
  20.1 1.6 %collective-permute-start.4 = (bf16[4,256,128]{2,1,0:T(8,128)(2,1)S(1)}, bf16[4,256,128]{2,1,0:T(8,128)(2,1)S(1)}, u32[]{:S(2)}, u32[]{:S(2)}) collective-permute-start(bf16[4,256,128]{2,1,0:T(8,128)(2,1)S(1)} %get-tuple-element.33), channel_id=1, source_target_pairs={{0,1},{1,0},{2,3},{3,2},{4,5},{5,4},{6,7},{7,6},{8,9},{9,8},{10,11... | collective-permute-start | bytes 786440 | tf_op jit(solution)/shard_map/ppermute | solution.py:730
  23.9 32.2 %all-to-all-start = ((bf16[16,264,128]{2,1,0:T(8,128)(2,1)}), bf16[16,264,128]{2,1,0:T(8,128)(2,1)S(1)}, u32[]{:S(2)}, u32[]{:S(2)}) async-start(bf16[16,264,128]{2,1,0:T(8,128)(2,1)} %pack.1.after_hbm), calls=%async_computation | async-start | bytes 2162688 | tf_op jit(solution)/shard_map/all_to_all | solution.py:753
  32.6 2.7 %collective-permute-start.5 = (bf16[32,64,256]{2,1,0:T(8,128)(2,1)S(1)}, bf16[32,64,256]{2,1,0:T(8,128)(2,1)S(1)}, u32[]{:S(2)}, u32[]{:S(2)}) collective-permute-start(bf16[32,64,256]{2,1,0:T(8,128)(2,1)S(1)} %get-tuple-element.34), channel_id=1, source_target_pairs={{0,1},{1,0},{2,3},{3,2},{4,5},{5,4},{6,7},{7,6},{8,9},{9,8},{10,11... | collective-permute-start | bytes 3145736 | tf_op jit(solution)/shard_map/ppermute | solution.py:777
